TPU v7x, 128 devices: a whole 4x4x4 slice. The times are simulated.
128 devices in a mesh: seq: 16 (over y, x_hi, core), grp: 8 (over z, x_lo).
Axes of the slice: x: 4 (x_hi: 2, x_lo: 2; x = x_hi * 2 + x_lo), y: 4, z: 4, core: 2. Of those that a mesh axis runs over, the one named last changes fastest.
Arguments:
- byte_ids: int32 [3072, 8], P('seq'), may hold values from 0 to 255
- patch_order: int32 [3072], P('seq'), may hold values from 0 to 3071, as said below
- query_rows: bfloat16 [3072, 8192], P('seq', 'grp'), may hold values from -25 to 25
- key_rows: bfloat16 [3072, 8192], P('seq', 'grp'), may hold values from -25 to 25
- value_rows: bfloat16 [3072, 8192], P('seq', 'grp'), may hold values from -6 to 6
- byte_embed: bfloat16 [256, 1024], replicated, may hold values from -6.5 to 6.5
- norm_gain: float32 [1024], replicated, may hold values from 0.25 to 1.75
- w_up: bfloat16 [1024, 4096], replicated, may hold values from -0.1875 to 0.1875
- w_down: bfloat16 [4096, 1024], replicated, may hold values from -0.09375 to 0.09375
- vocab_head: bfloat16 [1024, 256], replicated, may hold values from -12 to 12
Outputs:
- byte_loss: float32 [3072, 8], P(('seq', 'grp'))
- query_grad: bfloat16 [3072, 8192], P('seq', 'grp')
- key_grad: bfloat16 [3072, 8192], P('seq', 'grp')
- value_grad: bfloat16 [3072, 8192], P('seq', 'grp')
Inputs may be any that keep to these rules, and one draw needn't show every extreme that they name: `patch_order`: each aligned block of 192 entries is a permutation of that block's own indices.
All inputs are finite; a program needn't handle non-finite values.
Results may differ from a plain program's by a relative error of at most 0.028.
Values may be sent and summed in bfloat16 or wider, within the bound.
No kernel may reach another device: no remote copies, remote signals or barrier semaphores. Data moves between devices by JAX's collectives and lax.ppermute only.
A program may use at most 192 MiB of HBM per device.

v0:
```python
import functools

import jax
import jax.numpy as jnp
from jax import lax
from jax.experimental import pallas as pl
from jax.experimental.pallas import tpu as pltpu
from jax.sharding import Mesh
from jax.sharding import PartitionSpec as P

HEAD = 128
PATCH = 8
SEQ = ("seq_0", "seq_1", "seq_2")
SEQ_GRP = ("seq_0", "seq_1", "seq_2", "grp")
CHIPS = ("seq_0", "seq_1")

EPSILON = 1e-05
FLOOR = -1e30
SCALE = HEAD ** (-0.5)
LOG2E = 1.4426950408889634
MIB = 2**20

BF16 = jnp.bfloat16
F32 = jnp.float32

NT = (((1,), (1,)), ((), ()))
NN = (((1,), (0,)), ((), ()))


def dot(a, b, dims=NN):
    return lax.dot_general(a, b, dims, preferred_element_type=F32)


WIDE = 256


def chunk_plan(rows, block):
    plan = []
    base = 0
    for first in range(0, rows, WIDE):
        lowest, highest = first // block, (first + WIDE - 1) // block
        own_keys = first + WIDE
        other_keys = min(rows, 2 * block * ((highest + 2) // 2))
        pieces = []
        for at in range(0, own_keys, WIDE):
            pieces.append((0, at, WIDE, "causal" if at == first else "all"))
        at = 0
        while at < other_keys:
            part = at // block
            if part < lowest:
                pieces.append((1, at, block, "all"))
            elif part <= highest:
                pieces.append((1, at, block, "block"))
            else:
                pieces.append((1, at, block, "none"))
            at += block
        plan.append((first, base, own_keys, other_keys, pieces))
        base += own_keys + other_keys
    return plan, base


def forward_kernel(
    plan, block, core_ref, own_ref, other_ref, out_ref, inverse_ref, kept_ref, key_s, turned_s, score_s
):
    parts = own_ref.shape[0]
    for j in range(parts):
        rows = pl.ds(j * block, block)
        key_s[0, rows] = own_ref[j, 1]
        key_s[1, rows] = other_ref[j, 0]
    for j in range(0, parts, 2):
        columns = pl.ds(j * block, 2 * block)
        for side in range(2):
            ref = own_ref if side == 0 else other_ref
            at = 2 if side == 0 else 1
            two = jnp.concatenate([ref[j, at], ref[j + 1, at]], 0)
            turned_s[side, :, columns] = two.T
    core = core_ref[0]
    factor = SCALE * LOG2E
    for first, base, own_keys, other_keys, pieces in plan:
        q_parts = []
        at = first
        while at < first + WIDE:
            stop = min(first + WIDE, (at // block + 1) * block)
            q_parts.append(own_ref[at // block, 0, pl.ds(at % block, stop - at)])
            at = stop
        queries = jnp.concatenate(q_parts, 0)
        top = None
        for side, at, size, kind in pieces:
            if kind == "none":
                continue
            score = dot(key_s[side, pl.ds(at, size)], queries, NT)
            if kind == "causal":
                key_at = lax.broadcasted_iota(jnp.int32, score.shape, 0)
                query_at = lax.broadcasted_iota(jnp.int32, score.shape, 1)
                score = jnp.where(key_at <= query_at, score, FLOOR)
            elif kind == "block":
                row = first + lax.broadcasted_iota(jnp.int32, (1, WIDE), 1)
                part = at // block
                shown = row >= block * (part + 1 - core)
                score = jnp.where(shown, score, FLOOR)
            score_s[pl.ds(side * own_keys + at, size)] = score
            piece_top = jnp.max(score, axis=0, keepdims=True)
            top = piece_top if top is None else jnp.maximum(top, piece_top)
        shift = top * factor
        total = jnp.zeros((1, WIDE), F32)
        for side, at, size, kind in pieces:
            spot = side * own_keys + at
            if kind == "none":
                kept_ref[pl.ds(base + spot, size)] = jnp.zeros((size, WIDE), BF16)
                continue
            chance = jnp.exp2(score_s[pl.ds(spot, size)] * factor - shift)
            total = total + jnp.sum(chance, axis=0, keepdims=True)
            kept_ref[pl.ds(base + spot, size)] = chance.astype(BF16)
        mixed = dot(turned_s[0, :, :own_keys], kept_ref[pl.ds(base, own_keys)])
        mixed += dot(turned_s[1, :, :other_keys], kept_ref[pl.ds(base + own_keys, other_keys)])
        inverse = jnp.broadcast_to(1.0 / total, (HEAD, WIDE))
        out_ref[pl.ds(first, WIDE)] = (mixed * inverse).T.astype(BF16)
        inverse_ref[pl.ds(first, WIDE)] = inverse.T


def backward_kernel(
    plan,
    block,
    own_ref,
    other_ref,
    mixed_ref,
    inverse_ref,
    kept_ref,
    grad_ref,
    query_ref,
    own_out_ref,
    other_out_ref,
    value_s,
    turned_s,
    key_sum,
    value_sum,
    slope_s,
):
    parts = own_ref.shape[0]
    for j in range(parts):
        rows = pl.ds(j * block, block)
        value_s[0, rows] = own_ref[j, 2]
        value_s[1, rows] = other_ref[j, 1]
    for j in range(0, parts, 2):
        columns = pl.ds(j * block, 2 * block)
        for side in range(2):
            ref = own_ref if side == 0 else other_ref
            at = 1 if side == 0 else 0
            two = jnp.concatenate([ref[j, at], ref[j + 1, at]], 0)
            turned_s[side, :, columns] = two.T
    reached = [0, 0]
    for first, base, own_keys, other_keys, pieces in plan:
        q_parts = []
        at = first
        while at < first + WIDE:
            stop = min(first + WIDE, (at // block + 1) * block)
            q_parts.append(own_ref[at // block, 0, pl.ds(at % block, stop - at)])
            at = stop
        queries = jnp.concatenate(q_parts, 0)
        rows = pl.ds(first, WIDE)
        grads = (grad_ref[rows].astype(F32) * inverse_ref[rows]).astype(BF16)
        product = grads.astype(F32) * mixed_ref[rows].astype(F32)
        row_dot = jnp.sum(product.T, axis=0, keepdims=True)
        for side, at, size, kind in pieces:
            spot = side * own_keys + at
            if kind == "none":
                slope_s[pl.ds(spot, size)] = jnp.zeros((size, WIDE), BF16)
                continue
            kept = kept_ref[pl.ds(base + spot, size)]
            chance_grad = dot(value_s[side, pl.ds(at, size)], grads, NT)
            slope = (kept.astype(F32) * (chance_grad - row_dot)).astype(BF16)
            slope_s[pl.ds(spot, size)] = slope
            value_part = dot(kept, grads)
            key_part = dot(slope, queries)
            keys = pl.ds(at, size)
            if at >= reached[side]:
                reached[side] = at + size
                value_sum[side, keys] = value_part
                key_sum[side, keys] = key_part
            else:
                value_sum[side, keys] += value_part
                key_sum[side, keys] += key_part
        turned = dot(turned_s[0, :, :own_keys], slope_s[pl.ds(0, own_keys)])
        turned += dot(turned_s[1, :, :other_keys], slope_s[pl.ds(own_keys, other_keys)])
        query_ref[rows] = (turned * SCALE).T.astype(BF16)
    for j in range(parts):
        rows = pl.ds(j * block, block)
        own_out_ref[j, 0] = key_sum[0, rows] * SCALE
        own_out_ref[j, 1] = value_sum[0, rows]
        other_out_ref[j, 0] = (key_sum[1, rows] * SCALE).astype(BF16)
        other_out_ref[j, 1] = value_sum[1, rows].astype(BF16)


GELU_A = 0.7978845608028654
GELU_B = 0.044715


def byte_kernel(
    pieces,
    place_ref,
    rows_ref,
    ids_ref,
    order_ref,
    embed_ref,
    gain_ref,
    up_hbm,
    down_hbm,
    vocab_ref,
    grad_ref,
    loss_ref,
    up_s,
    down_s,
    bend_s,
    up_sem,
    down_sem,
):
    heads, count, _ = rows_ref.shape
    width = embed_ref.shape[1]
    hidden = up_s.shape[1]
    size = hidden // pieces
    up_copies = []
    down_copies = []
    for i in range(pieces):
        part = pl.ds(i * size, size)
        up_copies.append(pltpu.make_async_copy(up_hbm.at[:, part], up_s.at[:, part], up_sem.at[i]))
        down_copies.append(pltpu.make_async_copy(down_hbm.at[part], down_s.at[part], down_sem.at[i]))
        up_copies[-1].start()
        down_copies[-1].start()
    place = place_ref[0]
    ids = ids_ref[...]
    lane = lax.broadcasted_iota(jnp.int32, ids.shape, 1)
    target = jnp.sum(jnp.where(lane == place, ids, 0), axis=1, keepdims=True)
    previous = jnp.sum(jnp.where(lane == place - 1, ids, 0), axis=1, keepdims=True)
    letters = lax.broadcasted_iota(jnp.int32, (count, vocab_ref.shape[1]), 1)
    live = jnp.where(place > 0, 1.0, 0.0)
    one_hot = jnp.where(previous == letters, live, 0.0).astype(BF16)
    hidden_in = jnp.concatenate([rows_ref[h].astype(F32) for h in range(heads)], 1)
    hidden_in = hidden_in + dot(one_hot, embed_ref[...])
    inverse_rms = lax.rsqrt(jnp.mean(hidden_in * hidden_in, axis=1, keepdims=True) + EPSILON)
    gain = gain_ref[...]
    normed = (hidden_in * inverse_rms * gain).astype(BF16)
    after = hidden_in
    for i in range(pieces):
        part = pl.ds(i * size, size)
        up_copies[i].wait()
        raised = dot(normed, up_s[:, part])
        square = raised * raised
        bent = jnp.tanh(GELU_A * raised * (1.0 + GELU_B * square))
        half = 0.5 * (1.0 + bent)
        active = (raised * half).astype(BF16)
        bend_s[:, part] = half + 0.5 * raised * (1.0 - bent * bent) * (
            GELU_A + (3.0 * GELU_A * GELU_B) * square
        )
        down_copies[i].wait()
        after = after + dot(active, down_s[part])
    final_scale = lax.rsqrt(jnp.mean(after * after, axis=1, keepdims=True) + EPSILON)
    final_rows = (after * final_scale).astype(BF16)
    logits = dot(final_rows, vocab_ref[...])
    row_top = jnp.max(logits, axis=1, keepdims=True)
    raised_mass = jnp.exp(logits - row_top)
    mass = jnp.sum(raised_mass, axis=1, keepdims=True)
    is_target = target == letters
    chosen = jnp.sum(jnp.where(is_target, logits, 0.0), axis=1, keepdims=True)
    loss = jnp.log(mass) + row_top - chosen
    row_at = lax.broadcasted_iota(jnp.int32, (count, count), 0)
    loss_ref[...] = jnp.sum(jnp.where(row_at == order_ref[...], loss, 0.0), axis=0, keepdims=True)
    logit_grad = raised_mass / mass - jnp.where(is_target, 1.0, 0.0)
    final_grad = dot(logit_grad.astype(BF16), vocab_ref[...], NT).astype(BF16).astype(F32)
    mean_dot = jnp.mean(final_grad * after, axis=1, keepdims=True)
    after_grad = final_scale * final_grad - after * (final_scale * final_scale * final_scale * mean_dot)
    narrow = after_grad.astype(BF16)
    normed_grad = None
    for i in range(pieces):
        part = pl.ds(i * size, size)
        active_grad = dot(narrow, down_s[part], NT).astype(BF16).astype(F32)
        raised_grad = (active_grad * bend_s[:, part]).astype(BF16)
        term = dot(raised_grad, up_s[:, part], NT)
        normed_grad = term if normed_grad is None else normed_grad + term
    scaled = normed_grad.astype(BF16).astype(F32) * gain
    mean_dot = jnp.mean(scaled * hidden_in, axis=1, keepdims=True)
    total = (
        after_grad
        + inverse_rms * scaled
        - hidden_in * (inverse_rms * inverse_rms * inverse_rms * mean_dot)
    ).astype(BF16)
    for h in range(heads):
        grad_ref[h] = total[:, h * HEAD : (h + 1) * HEAD]


def vmem():
    return pl.BlockSpec(memory_space=pltpu.VMEM)


def smem():
    return pl.BlockSpec(memory_space=pltpu.SMEM)


def shape(dims, kind=BF16):
    return jax.ShapeDtypeStruct(dims, kind)


def exchange(value):
    return lax.all_to_all(value, CHIPS, split_axis=0, concat_axis=0, tiled=True)


def swap_cores(value):
    return lax.ppermute(value, "seq_2", [(0, 1), (1, 0)])


def shards(
    byte_ids,
    patch_order,
    query_rows,
    key_rows,
    value_rows,
    byte_embed,
    norm_gain,
    w_up,
    w_down,
    vocab_head,
):
    count, columns = query_rows.shape
    heads = columns // HEAD
    rows = heads * count
    seq_here = lax.axis_index(SEQ)
    place = lax.axis_index("grp").astype(jnp.int32)
    core = lax.axis_index("seq_2").astype(jnp.int32)
    plan, kept_rows = chunk_plan(rows, count)

    stacked = jnp.stack([query_rows, key_rows, value_rows])
    stacked = stacked.reshape(3, count, heads, HEAD).transpose(2, 0, 1, 3)
    own = exchange(stacked)
    other = swap_cores(own[:, 1:])

    attended, inverse, kept = pl.pallas_call(
        functools.partial(forward_kernel, plan, count),
        out_shape=(shape((rows, HEAD)), shape((rows, HEAD), F32), shape((kept_rows, WIDE))),
        in_specs=[smem(), vmem(), vmem()],
        out_specs=(vmem(), vmem(), vmem()),
        scratch_shapes=[
            pltpu.VMEM((2, rows, HEAD), BF16),
            pltpu.VMEM((2, HEAD, rows), BF16),
            pltpu.VMEM((2 * rows, WIDE), F32),
        ],
        compiler_params=pltpu.CompilerParams(vmem_limit_bytes=30 * MIB),
        cost_estimate=pl.CostEstimate(
            flops=4 * kept_rows * WIDE * HEAD, bytes_accessed=8 * MIB, transcendentals=kept_rows * WIDE
        ),
        name="attention_forward",
    )(core[None], own, other)

    owned_rows = exchange(attended.reshape(heads, count, HEAD))
    local_order = (patch_order - seq_here * count)[None]
    hidden = w_up.shape[1]
    pieces = 8
    context_grad, loss = pl.pallas_call(
        functools.partial(byte_kernel, pieces),
        out_shape=(shape((heads, count, HEAD)), shape((1, count), F32)),
        in_specs=[
            smem(),
            vmem(),
            vmem(),
            vmem(),
            vmem(),
            vmem(),
            pl.BlockSpec(memory_space=pl.ANY),
            pl.BlockSpec(memory_space=pl.ANY),
            vmem(),
        ],
        out_specs=(vmem(), vmem()),
        scratch_shapes=[
            pltpu.VMEM(w_up.shape, BF16),
            pltpu.VMEM(w_down.shape, BF16),
            pltpu.VMEM((count, hidden), F32),
            pltpu.SemaphoreType.DMA((pieces,)),
            pltpu.SemaphoreType.DMA((pieces,)),
        ],
        compiler_params=pltpu.CompilerParams(vmem_limit_bytes=44 * MIB),
        cost_estimate=pl.CostEstimate(
            flops=8 * count * columns * hidden,
            bytes_accessed=4 * columns * hidden,
            transcendentals=count * hidden,
        ),
        name="byte_layer",
    )(
        place[None],
        owned_rows,
        byte_ids,
        local_order,
        byte_embed,
        norm_gain[None],
        w_up,
        w_down,
        vocab_head,
    )

    grad_rows = exchange(context_grad).reshape(rows, HEAD)
    query_grad, own_grad, other_grad = pl.pallas_call(
        functools.partial(backward_kernel, plan, count),
        out_shape=(
            shape((rows, HEAD)),
            shape((heads, 2, count, HEAD), F32),
            shape((heads, 2, count, HEAD)),
        ),
        in_specs=[vmem()] * 6,
        out_specs=(vmem(), vmem(), vmem()),
        scratch_shapes=[
            pltpu.VMEM((2, rows, HEAD), BF16),
            pltpu.VMEM((2, HEAD, rows), BF16),
            pltpu.VMEM((2, rows, HEAD), F32),
            pltpu.VMEM((2, rows, HEAD), F32),
            pltpu.VMEM((2 * rows, WIDE), BF16),
        ],
        compiler_params=pltpu.CompilerParams(vmem_limit_bytes=30 * MIB),
        cost_estimate=pl.CostEstimate(
            flops=8 * kept_rows * WIDE * HEAD, bytes_accessed=12 * MIB, transcendentals=0
        ),
        name="attention_backward",
    )(own, other, attended, inverse, kept, grad_rows)

    pair_grad = (own_grad + swap_cores(other_grad).astype(F32)).astype(BF16)
    all_grads = jnp.concatenate([query_grad.reshape(heads, 1, count, HEAD), pair_grad], 1)
    back = exchange(all_grads).transpose(1, 2, 0, 3).reshape(3, count, columns)

    losses = lax.all_gather(loss[0], "grp")
    own_slots = count // PATCH
    byte_loss = lax.dynamic_slice_in_dim(losses, place * own_slots, own_slots, 1).T
    return byte_loss, back[0], back[1], back[2]


def solution(mesh):
    torus = Mesh(
        mesh.devices.reshape(4, 2, 2, mesh.shape["grp"]), ("seq_0", "seq_1", "seq_2", "grp")
    )
    placed = (
        P(SEQ, None),
        P(SEQ),
        P(SEQ, "grp"),
        P(SEQ, "grp"),
        P(SEQ, "grp"),
        P(),
        P(),
        P(),
        P(),
        P(),
    )
    return jax.shard_map(
        shards,
        mesh=torus,
        in_specs=placed,
        out_specs=(P(SEQ_GRP, None), P(SEQ, "grp"), P(SEQ, "grp"), P(SEQ, "grp")),
        check_vma=False,
    )
```

profile of v0, /device:TPU:0, one launch (start us, length us, event | category | flops | bytes accessed | tf_op | source)
XLA Modules:
  0.0 134.3 jit_solution(12364245742768487682)
XLA Ops:
  0.6 1.1 copy.29
  1.8 0.1 copy.30
  1.9 0.1 copy.23
  2.0 0.8 copy-done.9
  2.8 0.1 copy.31
  2.9 0.1 maximum_bitcast_fusion
  3.0 25.5 %all_to_all.20.own_ref = bf16[8,3,192,128]{3,2,1,0:T(8,128)(2,1)S(1)} all-to-all(bf16[8,3,192,128]{3,2,1,0:T(8,128)(2,1)S(1)} %maximum_bitcast_fusion), channel_id=1, replica_groups=mesh['seq_0'=4,'seq_1'=2,'seq_2'=2,'grp'=8] {'seq_0','seq_1'}, dimensions={0} | all-to-all | bytes 2359296 | tf_op jit(solution)/shard_map/all_to_all | solution.py:303
  28.6 0.1 collective-permute-start
  28.7 2.3 %collective-permute-done.other_ref = bf16[8,2,192,128]{3,2,1,0:T(8,128)(2,1)S(1)} collective-permute-done((bf16[8,2,192,128]{3,2,1,0:T(8,128)(2,1)S(1)}, bf16[8,2,192,128]{3,2,1,0:T(8,128)(2,1)S(1)}, u32[]{:S(2)}, u32[]{:S(2)}) %collective-permute-start) | collective-permute-done | bytes 786464 | tf_op jit(solution)/shard_map/ppermute | solution.py:307
  31.0 6.8 %attention_forward.1 = (bf16[1536,128]{1,0:T(8,128)(2,1)}, f32[1536,128]{1,0:T(8,128)S(1)}, bf16[11520,256]{1,0:T(8,128)(2,1)S(1)}) custom-call(s32[1]{0:T(128)} %bitcast.1.core_ref, bf16[8,3,192,128]{3,2,1,0:T(8,128)(2,1)S(1)} %all_to_all.20.own_ref, bf16[8,2,192,128]{3,2,1,0:T(8,128)(2,1)S(1)} %collective-permute-done.other_ref), custom_call_target="tpu_custom_call" | custom-call | flops 1509949440 | bytes 8388608 | tf_op jit(solution)/shard_map/attention_forward/pallas_call | solution.py:335
  37.8 2.5 %copy-done.4 = bf16[11520,256]{1,0:T(8,128)(2,1)} copy-done((bf16[11520,256]{1,0:T(8,128)(2,1)}, bf16[11520,256]{1,0:T(8,128)(2,1)S(1)}, u32[]{:S(2)}) %copy-start.4) | copy-done | bytes 5898264
  40.4 0.9 copy-done.6
  41.2 3.6 %all-to-all-start.1 = ((bf16[8,192,128]{2,1,0:T(8,128)(2,1)}), bf16[8,192,128]{2,1,0:T(8,128)(2,1)S(1)}, u32[]{:S(2)}, u32[]{:S(2)}) async-start(bf16[8,192,128]{2,1,0:T(8,128)(2,1)} %bitcast.3), calls=%async_computation.1 | async-start | bytes 786432 | tf_op jit(solution)/shard_map/all_to_all | solution.py:303
  44.9 0.1 copy.25.ids_ref
  45.0 10.4 %all-to-all-done.1.rows_ref = bf16[8,192,128]{2,1,0:T(8,128)(2,1)S(1)} async-done(((bf16[8,192,128]{2,1,0:T(8,128)(2,1)}), bf16[8,192,128]{2,1,0:T(8,128)(2,1)S(1)}, u32[]{:S(2)}, u32[]{:S(2)}) %all-to-all-start.1) | async-done | bytes 393248 | tf_op jit(solution)/shard_map/all_to_all | solution.py:303
  55.4 3.4 %copy-done = bf16[1024,4096]{1,0:T(8,128)(2,1)S(1)} copy-done((bf16[1024,4096]{1,0:T(8,128)(2,1)S(1)}, bf16[1024,4096]{1,0:T(8,128)(2,1)}, u32[]{:S(2)}) %copy-start) | copy-done | bytes 8388632
  58.8 15.4 %byte_layer.1 = (bf16[8,192,128]{2,1,0:T(8,128)(2,1)S(1)}, f32[1,192]{1,0:T(1,128)S(1)}) custom-call(s32[1]{0:T(128)} %bitcast.place_ref, bf16[8,192,128]{2,1,0:T(8,128)(2,1)S(1)} %all-to-all-done.1.rows_ref, s32[192,8]{1,0:T(8,128)S(1)} %copy.25.ids_ref, s32[1,192]{1,0:T(1,128)S(1)} %bitcast.39, bf16[256,1024]{1,0:T(8,128)(2,1)S(1)} %copy-done.1, ...), custom_call_target="tpu_custom_call" | custom-call | flops 6442450944 | bytes 16777216 | tf_op jit(solution)/shard_map/byte_layer/pallas_call | solution.py:356
  74.2 12.8 %all_to_all.21 = bf16[8,192,128]{2,1,0:T(8,128)(2,1)S(1)} all-to-all(bf16[8,192,128]{2,1,0:T(8,128)(2,1)S(1)} %get-tuple-element.16), channel_id=1, replica_groups=mesh['seq_0'=4,'seq_1'=2,'seq_2'=2,'grp'=8] {'seq_0','seq_1'}, dimensions={0} | all-to-all | bytes 786432 | tf_op jit(solution)/shard_map/all_to_all | solution.py:303
  87.0 8.4 %attention_backward.1 = (bf16[1536,128]{1,0:T(8,128)(2,1)S(1)}, f32[8,2,192,128]{3,2,1,0:T(8,128)S(1)}, bf16[8,2,192,128]{3,2,1,0:T(8,128)(2,1)S(1)}) custom-call(bf16[8,3,192,128]{3,2,1,0:T(8,128)(2,1)S(1)} %all_to_all.20.own_ref, bf16[8,2,192,128]{3,2,1,0:T(8,128)(2,1)S(1)} %collective-permute-done.other_ref, ...), custom_call_target="tpu_custom_call" | custom-call | flops 3019898880 | bytes 12582912 | tf_op jit(solution)/shard_map/attention_backward/pallas_call | solution.py:398
  95.4 0.1 collective-permute-start.1
  95.5 2.3 %collective-permute-done.1 = bf16[8,2,192,128]{3,2,1,0:T(8,128)(2,1)S(1)} collective-permute-done((bf16[8,2,192,128]{3,2,1,0:T(8,128)(2,1)S(1)}, bf16[8,2,192,128]{3,2,1,0:T(8,128)(2,1)S(1)}, u32[]{:S(2)}, u32[]{:S(2)}) %collective-permute-start.1) | collective-permute-done | bytes 786464 | tf_op jit(solution)/shard_map/ppermute | solution.py:307
  97.8 0.2 add_convert_fusion
  98.0 1.1 pad_maximum_fusion
  99.1 3.6 %all-to-all-start.3 = ((bf16[8,3,192,128]{3,2,1,0:T(8,128)(2,1)}), bf16[8,3,192,128]{3,2,1,0:T(8,128)(2,1)S(1)}, u32[]{:S(2)}, u32[]{:S(2)}) async-start(bf16[8,3,192,128]{3,2,1,0:T(8,128)(2,1)} %pad_maximum_fusion), calls=%async_computation.3 | async-start | bytes 2359296 | tf_op jit(solution)/shard_map/all_to_all | solution.py:303
  102.7 28.2 %all-gather = f32[8,1,192]{2,1,0:T(1,128)S(1)} all-gather(f32[1,1,192]{2,1,0:T(1,128)S(1)} %bitcast.38), channel_id=1, replica_groups=mesh['seq_0'=4,'seq_1'=2,'seq_2'=2,'grp'=8] {'grp'}, dimensions={0}, use_global_device_ids=true | all-gather | bytes 6912 | tf_op jit(solution)/shard_map/all_gather | solution.py:425
  130.9 0.7 constant_dynamic-slice_fusion
  131.6 0.1 fusion
  131.6 0.3 copy.27
  131.9 0.3 copy.28
  132.2 0.3 copy.26
  132.4 0.8 copy.38
  133.3 1.0 copy_bitcast_fusion
  (25 shorter events, 0.2 us)
Async XLA Ops:
  0.6 1.2 copy-start.8
  1.8 1.0 copy-start.9
  28.6 2.4 %collective-permute-start = (bf16[8,2,192,128]{3,2,1,0:T(8,128)(2,1)S(1)}, bf16[8,2,192,128]{3,2,1,0:T(8,128)(2,1)S(1)}, u32[]{:S(2)}, u32[]{:S(2)}) collective-permute-start(bf16[8,2,192,128]{3,2,1,0:T(8,128)(2,1)S(1)} %slice.19), channel_id=1, source_target_pairs={{0,8},{8,0},{1,9},{9,1},{2,10},{10,2},{3,11},{11,3},{4,12},{12,4},... | collective-permute-start | bytes 2359304 | tf_op jit(solution)/shard_map/ppermute | solution.py:307
  31.0 13.9 %copy-start.10 = (s32[192,8]{0,1:T(8,128)S(1)}, s32[192,8]{0,1:T(8,128)}, u32[]{:S(2)}) copy-start(s32[192,8]{0,1:T(8,128)} %param.10) | copy-start | bytes 18436
  31.0 14.0 %copy-start.11 = (s32[192]{0:T(256)S(1)}, s32[192]{0:T(256)}, u32[]{:S(2)}) copy-start(s32[192]{0:T(256)} %param.11) | copy-start | bytes 2308
  31.0 24.4 %copy-start.1 = (bf16[256,1024]{1,0:T(8,128)(2,1)S(1)}, bf16[256,1024]{1,0:T(8,128)(2,1)}, u32[]{:S(2)}) copy-start(bf16[256,1024]{1,0:T(8,128)(2,1)} %embed_ref.1) | copy-start | bytes 1572868
  31.0 24.4 %copy-start.2 = (bf16[1024,256]{1,0:T(8,128)(2,1)S(1)}, bf16[1024,256]{1,0:T(8,128)(2,1)}, u32[]{:S(2)}) copy-start(bf16[1024,256]{1,0:T(8,128)(2,1)} %vocab_ref.1) | copy-start | bytes 1572868
  31.0 24.4 %copy-start.3 = (f32[1024]{0:T(1024)S(1)}, f32[1024]{0:T(1024)}, u32[]{:S(2)}) copy-start(f32[1024]{0:T(1024)} %param.16) | copy-start | bytes 12292
  37.8 2.5 %copy-start.4 = (bf16[11520,256]{1,0:T(8,128)(2,1)}, bf16[11520,256]{1,0:T(8,128)(2,1)S(1)}, u32[]{:S(2)}) copy-start(bf16[11520,256]{1,0:T(8,128)(2,1)S(1)} %get-tuple-element.15.kept_ref) | copy-start | bytes 17694724
  40.4 0.9 copy-start.6
  41.2 14.2 %all-to-all-start.1 = ((bf16[8,192,128]{2,1,0:T(8,128)(2,1)}), bf16[8,192,128]{2,1,0:T(8,128)(2,1)S(1)}, u32[]{:S(2)}, u32[]{:S(2)}) async-start(bf16[8,192,128]{2,1,0:T(8,128)(2,1)} %bitcast.3), calls=%async_computation.1 | async-start | bytes 786432 | tf_op jit(solution)/shard_map/all_to_all | solution.py:303
  55.4 3.4 %copy-start = (bf16[1024,4096]{1,0:T(8,128)(2,1)S(1)}, bf16[1024,4096]{1,0:T(8,128)(2,1)}, u32[]{:S(2)}) copy-start(bf16[1024,4096]{1,0:T(8,128)(2,1)} %up_hbm.1) | copy-start | bytes 25165828
  58.8 28.2 %copy-start.5 = (bf16[11520,256]{1,0:T(8,128)(2,1)S(1)}, bf16[11520,256]{1,0:T(8,128)(2,1)}, u32[]{:S(2)}) copy-start(bf16[11520,256]{1,0:T(8,128)(2,1)} %copy-done.4) | copy-start | bytes 17694724
  58.8 28.2 %copy-start.7 = (f32[1536,128]{1,0:T(8,128)S(1)}, f32[1536,128]{1,0:T(8,128)}, u32[]{:S(2)}) copy-start(f32[1536,128]{1,0:T(8,128)} %copy-done.6) | copy-start | bytes 2359300
  95.4 2.4 %collective-permute-start.1 = (bf16[8,2,192,128]{3,2,1,0:T(8,128)(2,1)S(1)}, bf16[8,2,192,128]{3,2,1,0:T(8,128)(2,1)S(1)}, u32[]{:S(2)}, u32[]{:S(2)}) collective-permute-start(bf16[8,2,192,128]{3,2,1,0:T(8,128)(2,1)S(1)} %get-tuple-element.19), channel_id=1, source_target_pairs={{0,8},{8,0},{1,9},{9,1},{2,10},{10,2},{3,11},{11,3},{4,12},{12,4},... | collective-permute-start | bytes 2359304 | tf_op jit(solution)/shard_map/ppermute | solution.py:307
  99.1 32.5 %all-to-all-start.3 = ((bf16[8,3,192,128]{3,2,1,0:T(8,128)(2,1)}), bf16[8,3,192,128]{3,2,1,0:T(8,128)(2,1)S(1)}, u32[]{:S(2)}, u32[]{:S(2)}) async-start(bf16[8,3,192,128]{3,2,1,0:T(8,128)(2,1)} %pad_maximum_fusion), calls=%async_computation.3 | async-start | bytes 2359296 | tf_op jit(solution)/shard_map/all_to_all | solution.py:303
where the time goes:
time: 135 us; the launch traced here: 134 us
  blocking collectives  66.5 us (49%)
  Pallas kernels  30.6 us (23%)
  waiting for transfers between devices  14.9 us (11%)
  local copies, waits for them, and re-layouts  12.5 us (9%)
  starting transfers between devices  7.37 us (5%)
  other arithmetic  1.46 us (1%)
    all_to_all x2, blocking collectives, exchange(): return lax.all_to_all(value, CHIPS, split_axis=0, concat_axis=0, tiled=True)  38.3 us
    all_gather x1, blocking collectives, shards(): losses = lax.all_gather(loss[0], 'grp')  28.2 us
    pallas_call x1, Pallas kernels, shards(): pl.pallas_call(functools.partial(byte_kernel, pieces), out_shape=(shape((...  15.4 us
    all_to_all x2, waiting for transfers between devices, exchange(): return lax.all_to_all(value, CHIPS, split_axis=0, concat_axis=0, tiled=True)  10.4 us
    unnamed x29, local copies, waits for them, and re-layouts  9.76 us
    pallas_call x1, Pallas kernels, shards(): pl.pallas_call(functools.partial(backward_kernel, plan, count), out_shape...  8.39 us
    all_to_all x2, starting transfers between devices, exchange(): return lax.all_to_all(value, CHIPS, split_axis=0, concat_axis=0, tiled=True)  7.2 us
    pallas_call x1, Pallas kernels, shards(): pl.pallas_call(functools.partial(forward_kernel, plan, count), out_shape=...  6.83 us
  transfers between devices with their start and end apart: 4, of which 3 were waited for; matrix products, arithmetic and copies ran while one was open for 1% of the time, Pallas kernels for 0%

commit v1 on v0

v1 whole, which is shorter than its diff:
```python
import functools

import jax
import jax.numpy as jnp
from jax import lax
from jax.experimental import pallas as pl
from jax.experimental.pallas import tpu as pltpu
from jax.sharding import Mesh
from jax.sharding import PartitionSpec as P

HEAD = 128
PATCH = 8
SEQ = ("seq_0", "seq_1", "seq_2")
SEQ_GRP = ("seq_0", "seq_1", "seq_2", "grp")
CHIPS = ("seq_0", "seq_1")

EPSILON = 1e-05
FLOOR = -1e30
SCALE = HEAD ** (-0.5)
LOG2E = 1.4426950408889634
MIB = 2**20

BF16 = jnp.bfloat16
F32 = jnp.float32

NT = (((1,), (1,)), ((), ()))
NN = (((1,), (0,)), ((), ()))


def dot(a, b, dims=NN):
    return lax.dot_general(a, b, dims, preferred_element_type=F32)


WIDE = 256


def own_plan(rows):
    plan = []
    base = 0
    for first in range(0, rows, WIDE):
        pieces = [(at, WIDE, "causal" if at == first else "all") for at in range(0, first + WIDE, WIDE)]
        plan.append((first, base, first + WIDE, pieces))
        base += first + WIDE
    return plan, base


def other_plan(rows, block):
    plan = []
    base = 0
    for first in range(0, rows, WIDE):
        lowest, highest = first // block, (first + WIDE - 1) // block
        keys = min(rows, 2 * block * ((highest + 2) // 2))
        pieces = []
        for at in range(0, keys, block):
            part = at // block
            kind = "all" if part < lowest else "block" if part <= highest else "none"
            pieces.append((at, block, kind))
        plan.append((first, base, keys, pieces))
        base += keys
    return plan, base


def flat_rows(ref, at, target):
    block = ref.shape[2]
    for j in range(ref.shape[0]):
        target[pl.ds(j * block, block)] = ref[j, at]


def turned_rows(ref, at, target):
    block = ref.shape[2]
    for j in range(0, ref.shape[0], 2):
        two = jnp.concatenate([ref[j, at], ref[j + 1, at]], 0)
        target[:, pl.ds(j * block, 2 * block)] = two.T


def query_chunk(ref, first):
    block = ref.shape[2]
    found = []
    at = first
    while at < first + WIDE:
        stop = min(first + WIDE, (at // block + 1) * block)
        found.append(ref[at // block, 0, pl.ds(at % block, stop - at)])
        at = stop
    return jnp.concatenate(found, 0)


def piece_scores(queries, first, pieces, key_s, score_s, core):
    top = None
    for at, size, kind in pieces:
        if kind == "none":
            continue
        score = dot(key_s[pl.ds(at, size)], queries, NT)
        if kind == "causal":
            key_at = lax.broadcasted_iota(jnp.int32, score.shape, 0)
            query_at = lax.broadcasted_iota(jnp.int32, score.shape, 1)
            score = jnp.where(key_at <= query_at, score, FLOOR)
        elif kind == "block":
            row = first + lax.broadcasted_iota(jnp.int32, (1, WIDE), 1)
            shown = row >= size * (at // size + 1 - core)
            score = jnp.where(shown, score, FLOOR)
        score_s[pl.ds(at, size)] = score
        piece_top = jnp.max(score, axis=0, keepdims=True)
        top = piece_top if top is None else jnp.maximum(top, piece_top)
    return top


def piece_chances(shift, base, pieces, score_s, kept_ref):
    total = jnp.zeros((1, WIDE), F32)
    for at, size, kind in pieces:
        kept = pl.ds(base + at, size)
        if kind == "none":
            kept_ref[kept] = jnp.zeros((size, WIDE), BF16)
            continue
        chance = jnp.exp2(score_s[pl.ds(at, size)] * (SCALE * LOG2E) - shift)
        total = total + jnp.sum(chance, axis=0, keepdims=True)
        kept_ref[kept] = chance.astype(BF16)
    return total


def forward_own(plan, own_ref, load_ref, kept_ref, mixed_ref, stats_ref, loaded_ref, key_s, turned_s, score_s, sem):
    load = pltpu.make_async_copy(load_ref, loaded_ref, sem)
    load.start()
    flat_rows(own_ref, 1, key_s)
    turned_rows(own_ref, 2, turned_s)
    for i, (first, base, keys, pieces) in enumerate(plan):
        top = piece_scores(query_chunk(own_ref, first), first, pieces, key_s, score_s, None)
        shift = top * (SCALE * LOG2E)
        total = piece_chances(shift, base, pieces, score_s, kept_ref)
        mixed_ref[i] = dot(turned_s[:, :keys], kept_ref[pl.ds(base, keys)])
        stats_ref[i, 0:1] = shift
        stats_ref[i, 1:2] = total
    load.wait()


def forward_other(
    plan,
    facts_ref,
    own_ref,
    other_ref,
    mixed_ref,
    stats_ref,
    load_ref,
    kept_ref,
    out_ref,
    own_inverse_ref,
    inverse_ref,
    loaded_ref,
    key_s,
    turned_s,
    score_s,
    sem,
):
    load = pltpu.make_async_copy(load_ref, loaded_ref, sem)
    load.start()
    flat_rows(other_ref, 0, key_s)
    turned_rows(other_ref, 1, turned_s)
    core = facts_ref[2]
    for i, (first, base, keys, pieces) in enumerate(plan):
        top = piece_scores(query_chunk(own_ref, first), first, pieces, key_s, score_s, core)
        own_shift = stats_ref[i, 0:1]
        shift = jnp.maximum(top * (SCALE * LOG2E), own_shift)
        total = piece_chances(shift, base, pieces, score_s, kept_ref)
        own_part = jnp.exp2(own_shift - shift)
        total = total + own_part * stats_ref[i, 1:2]
        mixed = mixed_ref[i] * own_part + dot(turned_s[:, :keys], kept_ref[pl.ds(base, keys)])
        inverse = 1.0 / total
        rows = pl.ds(first, WIDE)
        out_ref[rows] = (mixed * inverse).T.astype(BF16)
        inverse_ref[rows] = jnp.broadcast_to(inverse, (HEAD, WIDE)).T
        own_inverse_ref[rows] = jnp.broadcast_to(own_part * inverse, (HEAD, WIDE)).T
    load.wait()


def backward_side(
    plan, key_at, own_ref, side_ref, mixed_ref, inverse_ref, kept_ref, grad_ref, key_sum, value_sum, value_s, turned_s,
    slope_s,
):
    flat_rows(side_ref, key_at + 1, value_s)
    turned_rows(side_ref, key_at, turned_s)
    reached = 0
    for i, (first, base, keys, pieces) in enumerate(plan):
        queries = query_chunk(own_ref, first)
        rows = pl.ds(first, WIDE)
        grads = (grad_ref[rows].astype(F32) * inverse_ref[rows]).astype(BF16)
        product = grads.astype(F32) * mixed_ref[rows].astype(F32)
        row_dot = jnp.sum(product.T, axis=0, keepdims=True)
        for at, size, kind in pieces:
            spot = pl.ds(at, size)
            if kind == "none":
                slope_s[spot] = jnp.zeros((size, WIDE), BF16)
                continue
            kept = kept_ref[pl.ds(base + at, size)]
            chance_grad = dot(value_s[spot], grads, NT)
            slope = (kept.astype(F32) * (chance_grad - row_dot)).astype(BF16)
            slope_s[spot] = slope
            value_part = dot(kept, grads)
            key_part = dot(slope, queries)
            if at >= reached:
                reached = at + size
                value_sum[spot] = value_part
                key_sum[spot] = key_part
            else:
                value_sum[spot] += value_part
                key_sum[spot] += key_part
        yield i, dot(turned_s[:, :keys], slope_s[pl.ds(0, keys)])


def backward_other(
    plan, own_ref, other_ref, mixed_ref, inverse_ref, kept_ref, grad_ref, pair_ref, query_ref, key_sum, value_sum,
    value_s, turned_s, slope_s,
):
    for i, turned in backward_side(
        plan, 0, own_ref, other_ref, mixed_ref, inverse_ref, kept_ref, grad_ref, key_sum, value_sum, value_s, turned_s,
        slope_s,
    ):
        query_ref[i] = turned
    parts, _, block, _ = other_ref.shape
    for j in range(parts):
        rows = pl.ds(j * block, block)
        pair_ref[j, 0] = (key_sum[rows] * SCALE).astype(BF16)
        pair_ref[j, 1] = value_sum[rows].astype(BF16)


def backward_own(
    plan, own_ref, mixed_ref, inverse_ref, kept_ref, grad_ref, turned_ref, query_ref, key_ref, value_ref, value_s,
    turned_s, slope_s,
):
    for i, turned in backward_side(
        plan, 1, own_ref, own_ref, mixed_ref, inverse_ref, kept_ref, grad_ref, key_ref, value_ref, value_s, turned_s,
        slope_s,
    ):
        first = plan[i][0]
        query_ref[pl.ds(first, WIDE)] = ((turned + turned_ref[i]) * SCALE).T.astype(BF16)


def join_kernel(query_ref, key_ref, value_ref, pair_ref, out_ref):
    parts, _, block, _ = out_ref.shape
    for j in range(parts):
        rows = pl.ds(j * block, block)
        out_ref[j, 0] = query_ref[rows]
        out_ref[j, 1] = (key_ref[rows] * SCALE + pair_ref[j, 0].astype(F32)).astype(BF16)
        out_ref[j, 2] = (value_ref[rows] + pair_ref[j, 1].astype(F32)).astype(BF16)


def pack_kernel(*refs):
    arrays, out_ref, sems = refs[:-2], refs[-2], refs[-1]
    copies = []
    for t, ref in enumerate(arrays):
        for h in range(out_ref.shape[0]):
            source = ref.at[:, pl.ds(h * HEAD, HEAD)]
            copies.append(pltpu.make_async_copy(source, out_ref.at[h, t], sems.at[len(copies)]))
            copies[-1].start()
    for copy in copies:
        copy.wait()


def unpack_kernel(stack_ref, *refs):
    arrays, sems = refs[:-1], refs[-1]
    copies = []
    for t, ref in enumerate(arrays):
        for h in range(stack_ref.shape[0]):
            target = ref.at[:, pl.ds(h * HEAD, HEAD)]
            copies.append(pltpu.make_async_copy(stack_ref.at[h, t], target, sems.at[len(copies)]))
            copies[-1].start()
    for copy in copies:
        copy.wait()


def turn_kernel(up_ref, down_ref, up_out, down_out):
    up_out[...] = up_ref[...].T
    down_out[...] = down_ref[...].T


GELU_A = 0.7978845608028654
GELU_B = 0.044715


def byte_kernel(
    pieces,
    facts_ref,
    rows_ref,
    ids_ref,
    order_ref,
    embed_ref,
    gain_ref,
    up_ref,
    down_ref,
    up_turned_ref,
    down_turned_ref,
    vocab_ref,
    grad_ref,
    loss_ref,
    bend_s,
):
    heads, count, _ = rows_ref.shape
    size = up_ref.shape[1] // pieces
    place = facts_ref[0]
    ids = ids_ref[...].T
    lane = lax.broadcasted_iota(jnp.int32, ids.shape, 1)
    target = jnp.sum(jnp.where(lane == place, ids, 0), axis=1, keepdims=True)
    previous = jnp.sum(jnp.where(lane == place - 1, ids, 0), axis=1, keepdims=True)
    letters = lax.broadcasted_iota(jnp.int32, (count, vocab_ref.shape[1]), 1)
    live = jnp.where(place > 0, 1.0, 0.0)
    one_hot = jnp.where(previous == letters, live, 0.0).astype(BF16)
    hidden_in = jnp.concatenate([rows_ref[h].astype(F32) for h in range(heads)], 1)
    hidden_in = hidden_in + dot(one_hot, embed_ref[...])
    inverse_rms = lax.rsqrt(jnp.mean(hidden_in * hidden_in, axis=1, keepdims=True) + EPSILON)
    gain = gain_ref[...]
    normed = (hidden_in * inverse_rms * gain).astype(BF16)
    after = hidden_in
    for i in range(pieces):
        part = pl.ds(i * size, size)
        raised = dot(normed, up_ref[:, part])
        square = raised * raised
        half = 0.5 + 0.5 * jnp.tanh(raised * (GELU_A + (GELU_A * GELU_B) * square))
        active = (raised * half).astype(BF16)
        bend_s[:, part] = half + half * (1.0 - half) * raised * (
            2.0 * GELU_A + (6.0 * GELU_A * GELU_B) * square
        )
        after = after + dot(active, down_ref[part])
    final_scale = lax.rsqrt(jnp.mean(after * after, axis=1, keepdims=True) + EPSILON)
    final_rows = (after * final_scale).astype(BF16)
    logits = dot(final_rows, vocab_ref[...])
    row_top = jnp.max(logits, axis=1, keepdims=True)
    raised_mass = jnp.exp(logits - row_top)
    mass = jnp.sum(raised_mass, axis=1, keepdims=True)
    is_target = target == letters
    chosen = jnp.sum(jnp.where(is_target, logits, 0.0), axis=1, keepdims=True)
    loss = jnp.log(mass) + row_top - chosen
    row_at = lax.broadcasted_iota(jnp.int32, (count, count), 0)
    ordered = jnp.sum(jnp.where(row_at == order_ref[...] - facts_ref[1], loss, 0.0), axis=0, keepdims=True)
    slot = lax.broadcasted_iota(jnp.int32, loss_ref.shape, 0)
    loss_ref[...] = jnp.where(slot == place, ordered, 0.0)
    logit_grad = raised_mass / mass - jnp.where(is_target, 1.0, 0.0)
    final_grad = dot(logit_grad.astype(BF16), vocab_ref[...], NT).astype(BF16).astype(F32)
    mean_dot = jnp.mean(final_grad * after, axis=1, keepdims=True)
    after_grad = final_scale * final_grad - after * (final_scale * final_scale * final_scale * mean_dot)
    narrow = after_grad.astype(BF16)
    normed_grad = None
    for i in range(pieces):
        part = pl.ds(i * size, size)
        active_grad = dot(narrow, down_turned_ref[:, part]).astype(BF16).astype(F32)
        raised_grad = (active_grad * bend_s[:, part]).astype(BF16)
        term = dot(raised_grad, up_turned_ref[part])
        normed_grad = term if normed_grad is None else normed_grad + term
    scaled = normed_grad.astype(BF16).astype(F32) * gain
    mean_dot = jnp.mean(scaled * hidden_in, axis=1, keepdims=True)
    total = (
        after_grad
        + inverse_rms * scaled
        - hidden_in * (inverse_rms * inverse_rms * inverse_rms * mean_dot)
    ).astype(BF16)
    for h in range(heads):
        grad_ref[h] = total[:, h * HEAD : (h + 1) * HEAD]


def vmem():
    return pl.BlockSpec(memory_space=pltpu.VMEM)


def far():
    return pl.BlockSpec(memory_space=pltpu.HBM)


def smem():
    return pl.BlockSpec(memory_space=pltpu.SMEM)


def held(dims, kind=BF16):
    return pltpu.VMEM(dims, kind)


def shape(dims, kind=BF16):
    return jax.ShapeDtypeStruct(dims, kind)


def exchange(value):
    return lax.all_to_all(value, CHIPS, split_axis=0, concat_axis=0, tiled=True)


def gather_losses(value, bit):
    return value + lax.ppermute(value, "grp", [(i, i ^ (1 << bit)) for i in range(PATCH)])


def swap_cores(value):
    return lax.ppermute(value, "seq_2", [(0, 1), (1, 0)])


def anywhere():
    return pl.BlockSpec(memory_space=pl.ANY)


def kernel_call(body, name, outs, ins, out_specs, scratch, grant, flops, transcendentals=0, moved=4 * MIB):
    return pl.pallas_call(
        body,
        out_shape=outs,
        in_specs=ins,
        out_specs=out_specs,
        scratch_shapes=scratch,
        compiler_params=pltpu.CompilerParams(vmem_limit_bytes=grant * MIB),
        cost_estimate=pl.CostEstimate(
            flops=flops, bytes_accessed=moved, transcendentals=transcendentals
        ),
        name=name,
    )


def shards(
    byte_ids,
    patch_order,
    query_rows,
    key_rows,
    value_rows,
    byte_embed,
    norm_gain,
    w_up,
    w_down,
    vocab_head,
):
    count, columns = query_rows.shape
    hidden = w_up.shape[1]
    heads = columns // HEAD
    rows = heads * count
    chunks = rows // WIDE
    seq_here = lax.axis_index(SEQ)
    place = lax.axis_index("grp").astype(jnp.int32)
    core = lax.axis_index("seq_2").astype(jnp.int32)
    facts = jnp.stack([place, seq_here * count, core])
    query_rows, facts = lax.optimization_barrier((query_rows, facts))
    near_plan, near_rows = own_plan(rows)
    far_plan, far_rows = other_plan(rows, count)

    query_rows, key_rows, value_rows = (
        pltpu.with_memory_space_constraint(a, pltpu.HBM) for a in (query_rows, key_rows, value_rows)
    )
    stacked = kernel_call(
        pack_kernel,
        "pack",
        shape((heads, 3, count, HEAD)),
        [far()] * 3,
        anywhere(),
        [pltpu.SemaphoreType.DMA((3 * heads,))],
        1,
        0,
    )(query_rows, key_rows, value_rows)
    own = exchange(stacked)

    size = 512
    w_up = pltpu.with_memory_space_constraint(w_up, pltpu.HBM)
    w_down = pltpu.with_memory_space_constraint(w_down, pltpu.HBM)
    wide_block = pl.BlockSpec((columns, size), lambda i: (0, i))
    tall_block = pl.BlockSpec((size, columns), lambda i: (i, 0))
    turned = pl.pallas_call(
        turn_kernel,
        out_shape=(pltpu.HBM((hidden, columns), BF16), pltpu.HBM((columns, hidden), BF16)),
        grid=(hidden // size,),
        in_specs=[wide_block, tall_block],
        out_specs=(tall_block, wide_block),
        compiler_params=pltpu.CompilerParams(vmem_limit_bytes=12 * MIB),
        cost_estimate=pl.CostEstimate(flops=0, bytes_accessed=32 * MIB, transcendentals=0),
        name="turn_weights",
    )(w_up, w_down)
    own, turned = lax.optimization_barrier((own, turned))
    other = swap_cores(own[:, 1:])

    kv_scratch = [pltpu.VMEM((rows, HEAD), BF16), pltpu.VMEM((HEAD, rows), BF16)]
    near_kept, near_mixed, stats, up_held = kernel_call(
        functools.partial(forward_own, near_plan),
        "forward_own",
        (
            held((near_rows, WIDE)),
            held((chunks, HEAD, WIDE), F32),
            held((chunks, 8, WIDE), F32),
            held(w_up.shape),
        ),
        [vmem(), far()],
        (vmem(),) * 4,
        kv_scratch + [pltpu.VMEM((rows, WIDE), F32), pltpu.SemaphoreType.DMA],
        8,
        4 * near_rows * WIDE * HEAD,
        near_rows * WIDE,
    )(own, w_up)
    far_kept, attended, near_inverse, far_inverse, down_held = kernel_call(
        functools.partial(forward_other, far_plan),
        "forward_other",
        (
            held((far_rows, WIDE)),
            held((rows, HEAD)),
            held((rows, HEAD), F32),
            held((rows, HEAD), F32),
            held(w_down.shape),
        ),
        [smem()] + [vmem()] * 4 + [far()],
        (vmem(),) * 5,
        kv_scratch + [pltpu.VMEM((rows, WIDE), F32), pltpu.SemaphoreType.DMA],
        8,
        4 * far_rows * WIDE * HEAD,
        far_rows * WIDE,
    )(facts, own, other, near_mixed, stats, w_down)

    byte_pieces = 4
    owned_rows = exchange(attended.reshape(heads, count, HEAD))
    context_grad, losses = kernel_call(
        functools.partial(byte_kernel, byte_pieces),
        "byte_layer",
        (shape((heads, count, HEAD)), shape((PATCH, count), F32)),
        [smem()] + [vmem()] * 10,
        (vmem(), vmem()),
        [pltpu.VMEM((count, hidden), F32)],
        14,
        8 * count * columns * hidden,
        count * hidden,
    )(
        facts,
        owned_rows,
        byte_ids.T,
        patch_order[None],
        byte_embed,
        norm_gain[None],
        up_held,
        down_held,
        *turned,
        vocab_head,
    )

    grad_rows, losses = lax.optimization_barrier((exchange(context_grad), losses))
    grad_rows = grad_rows.reshape(rows, HEAD)
    side_scratch = kv_scratch + [pltpu.VMEM((rows, WIDE), BF16)]
    sums = [pltpu.VMEM((rows, HEAD), F32)] * 2
    pair_grad, turned_grad = kernel_call(
        functools.partial(backward_other, far_plan),
        "backward_other",
        (shape((heads, 2, count, HEAD)), shape((chunks, HEAD, WIDE), F32)),
        [vmem()] * 6,
        (vmem(), vmem()),
        sums + side_scratch,
        8,
        8 * far_rows * WIDE * HEAD,
    )(own, other, attended, far_inverse, far_kept, grad_rows)
    pair_grad, turned_grad, losses = lax.optimization_barrier((pair_grad, turned_grad, gather_losses(losses, 0)))
    pair_sent = swap_cores(pair_grad)
    query_grad, key_grad, value_grad = kernel_call(
        functools.partial(backward_own, near_plan),
        "backward_own",
        (shape((rows, HEAD)), shape((rows, HEAD), F32), shape((rows, HEAD), F32)),
        [vmem()] * 6,
        (vmem(), vmem(), vmem()),
        side_scratch,
        8,
        8 * near_rows * WIDE * HEAD,
    )(own, attended, near_inverse, near_kept, grad_rows, turned_grad)
    query_grad, losses = lax.optimization_barrier((query_grad, gather_losses(losses, 1)))
    losses = gather_losses(losses, 2)
    joined = kernel_call(
        join_kernel,
        "join",
        shape((heads, 3, count, HEAD)),
        [vmem()] * 4,
        vmem(),
        [],
        4,
        0,
    )(query_grad, key_grad, value_grad, pair_sent)
    joined, losses = lax.optimization_barrier((joined, losses))
    back = exchange(joined)
    query_out, key_out, value_out = kernel_call(
        unpack_kernel,
        "unpack",
        (shape((count, columns)),) * 3,
        [anywhere()],
        (anywhere(),) * 3,
        [pltpu.SemaphoreType.DMA((3 * heads,))],
        1,
        0,
    )(back)

    own_slots = count // PATCH
    byte_loss = lax.dynamic_slice_in_dim(losses, place * own_slots, own_slots, 1).T
    return byte_loss, query_out, key_out, value_out


def solution(mesh):
    torus = Mesh(
        mesh.devices.reshape(4, 2, 2, mesh.shape["grp"]), ("seq_0", "seq_1", "seq_2", "grp")
    )
    placed = (
        P(SEQ, None),
        P(SEQ),
        P(SEQ, "grp"),
        P(SEQ, "grp"),
        P(SEQ, "grp"),
        P(),
        P(),
        P(),
        P(),
        P(),
    )
    return jax.shard_map(
        shards,
        mesh=torus,
        in_specs=placed,
        out_specs=(P(SEQ_GRP, None), P(SEQ, "grp"), P(SEQ, "grp"), P(SEQ, "grp")),
        check_vma=False,
    )
```

time: 135 us -> 149 us (1.10)
  Pallas kernels: 30.6 us -> 79.7 us
  blocking collectives: 66.5 us -> 26.5 us
  local copies, waits for them, and re-layouts: 12.5 us -> 0.77 us
  starting transfers between devices: 7.37 us -> 17 us
  waiting for transfers between devices: 14.9 us -> 23.6 us
    pallas_call x3 -> x9, Pallas kernels: 30.6 us -> 79.7 us  [the longest x1 37 us: shards(): kernel_call(pack_kernel, 'pack', shape((heads, 3, count, HEAD)), [far()]...]
    all_gather x1 -> x0, blocking collectives: 28.2 us -> none  [shards(): losses = lax.all_gather(loss[0], 'grp')]
    all_to_all x2, blocking collectives: 38.3 us -> 26.5 us  [exchange(): return lax.all_to_all(value, CHIPS, split_axis=0, concat_axis=0, tiled=True)]
    all_to_all x2, waiting for transfers between devices: 10.4 us -> 21.9 us  [exchange(): return lax.all_to_all(value, CHIPS, split_axis=0, concat_axis=0, tiled=True)]
    unnamed x29 -> x16, local copies, waits for them, and re-layouts: 9.76 us -> 0.05 us
    ppermute x0 -> x3, starting transfers between devices: none -> 6.26 us  [gather_losses(): lax.ppermute(value, 'grp', [(i, i ^ 1 << bit) for i in range(PATCH)])]
    ppermute x2, waiting for transfers between devices: 4.54 us -> 0.01 us  [swap_cores(): return lax.ppermute(value, 'seq_2', [(0, 1), (1, 0)])]
    all_to_all x2, starting transfers between devices: 7.2 us -> 10.6 us  [exchange(): return lax.all_to_all(value, CHIPS, split_axis=0, concat_axis=0, tiled=True)]
  transfers between devices with their start and end apart: 4 -> 7, of which waited for: 3 -> 3; matrix products, arithmetic and copies ran while one was open for 1% -> 0% of each run, Pallas kernels for 0% -> 17%
where the time goes in v1:
time: 149 us
  Pallas kernels  79.7 us (53%)
  blocking collectives  26.5 us (18%)
  waiting for transfers between devices  23.6 us (16%)
  starting transfers between devices  17 us (11%)
    pallas_call x1, Pallas kernels, shards(): kernel_call(pack_kernel, 'pack', shape((heads, 3, count, HEAD)), [far()]...  37 us
    all_to_all x2, blocking collectives, exchange(): return lax.all_to_all(value, CHIPS, split_axis=0, concat_axis=0, tiled=True)  26.5 us
    all_to_all x2, waiting for transfers between devices, exchange(): return lax.all_to_all(value, CHIPS, split_axis=0, concat_axis=0, tiled=True)  21.9 us
    pallas_call x1, Pallas kernels, shards(): pl.pallas_call(turn_kernel, out_shape=(pltpu.HBM((hidden, columns), BF16)...  14.3 us
    all_to_all x2, starting transfers between devices, exchange(): return lax.all_to_all(value, CHIPS, split_axis=0, concat_axis=0, tiled=True)  10.6 us
    pallas_call x1, Pallas kernels, shards(): kernel_call(functools.partial(byte_kernel, byte_pieces), 'byte_layer', (s...  9.82 us
    ppermute x3, starting transfers between devices, gather_losses(): lax.ppermute(value, 'grp', [(i, i ^ 1 << bit) for i in range(PATCH)])  6.26 us
    pallas_call x1, Pallas kernels, shards(): kernel_call(functools.partial(forward_other, far_plan), 'forward_other',...  4.73 us
  transfers between devices with their start and end apart: 7, of which 3 were waited for; matrix products, arithmetic and copies ran while one was open for 0% of the time, Pallas kernels for 17%

profile of v1, /device:TPU:0, one launch (start us, length us, event | category | flops | bytes accessed | tf_op | source)
XLA Modules:
  0.0 148.7 jit_solution(10108839887247648807)
XLA Ops:
  0.6 0.1 pad_add_fusion.facts_ref
  0.7 37.0 %pack.1 = bf16[8,3,192,128]{3,2,1,0:T(8,128)(2,1)} custom-call(bf16[192,1024]{1,0:T(8,128)(2,1)} %refs_0_, bf16[192,1024]{1,0:T(8,128)(2,1)} %refs_1_.1, bf16[192,1024]{1,0:T(8,128)(2,1)} %refs_2_.1), custom_call_target="tpu_custom_call" | custom-call | bytes 4194304 | tf_op jit(solution)/shard_map/pack/pallas_call | solution.py:436
  37.8 7.0 %all-to-all-start = ((bf16[8,3,192,128]{3,2,1,0:T(8,128)(2,1)}), bf16[8,3,192,128]{3,2,1,0:T(8,128)(2,1)S(1)}, u32[]{:S(2)}, u32[]{:S(2)}) async-start(bf16[8,3,192,128]{3,2,1,0:T(8,128)(2,1)} %pack.1), calls=%async_computation | async-start | bytes 2359296 | tf_op jit(solution)/shard_map/all_to_all | solution.py:378
  44.8 14.3 %turn_weights.1 = (bf16[4096,1024]{1,0:T(8,128)(2,1)}, bf16[1024,4096]{1,0:T(8,128)(2,1)}) custom-call(bf16[1024,4096]{1,0:T(8,128)(2,1)} %load_ref.2, bf16[4096,1024]{1,0:T(8,128)(2,1)} %load_ref.3), custom_call_target="tpu_custom_call" | custom-call | bytes 33554432 | tf_op jit(solution)/shard_map/turn_weights/pallas_call | solution.py:453
  59.1 4.3 %all-to-all-done.own_ref = bf16[8,3,192,128]{3,2,1,0:T(8,128)(2,1)S(1)} async-done(((bf16[8,3,192,128]{3,2,1,0:T(8,128)(2,1)}), bf16[8,3,192,128]{3,2,1,0:T(8,128)(2,1)S(1)}, u32[]{:S(2)}, u32[]{:S(2)}) %all-to-all-start) | async-done | bytes 1179680 | tf_op jit(solution)/shard_map/all_to_all | solution.py:378
  63.4 0.1 slice.3
  63.5 0.1 collective-permute-start
  63.6 0.0 slice-start
  63.6 3.5 %forward_own.1 = (bf16[5376,256]{1,0:T(8,128)(2,1)S(1)}, f32[6,128,256]{2,1,0:T(8,128)S(1)}, f32[6,8,256]{2,1,0:T(8,128)S(1)}, bf16[1024,4096]{1,0:T(8,128)(2,1)S(1)}) custom-call(bf16[8,3,192,128]{3,2,1,0:T(8,128)(2,1)S(1)} %all-to-all-done.own_ref, bf16[1024,4096]{1,0:T(8,128)(2,1)} %load_ref.2), custom_call_target="tpu_custom_call" | custom-call | flops 704643072 | bytes 4194304 | tf_op jit(solution)/shard_map/forward_own/pallas_call | solution.py:467
  67.2 0.0 copy-start.1
  67.2 0.0 copy-start.2
  67.2 0.0 copy-start.3
  67.2 0.0 copy-start.4
  67.2 0.0 copy-start.5
  67.3 4.7 %forward_other.1 = (bf16[6144,256]{1,0:T(8,128)(2,1)S(1)}, bf16[1536,128]{1,0:T(8,128)(2,1)S(1)}, f32[1536,128]{1,0:T(8,128)S(1)}, f32[1536,128]{1,0:T(8,128)S(1)}, bf16[4096,1024]{1,0:T(8,128)(2,1)S(1)}) custom-call(s32[3]{0:T(128)S(1)} %pad_add_fusion.facts_ref, bf16[8,3,192,128]{3,2,1,0:T(8,128)(2,1)S(1)} %all-to-all-done.own_ref, ...), custom_call_target="tpu_custom_call" | custom-call | flops 805306368 | bytes 4194304 | tf_op jit(solution)/shard_map/forward_other/pallas_call | solution.py:483
  72.0 14.0 %all_to_all.20.rows_ref = bf16[8,192,128]{2,1,0:T(8,128)(2,1)S(1)} all-to-all(bf16[8,192,128]{2,1,0:T(8,128)(2,1)S(1)} %bitcast.12), channel_id=1, replica_groups=mesh['seq_0'=4,'seq_1'=2,'seq_2'=2,'grp'=8] {'seq_0','seq_1'}, dimensions={0} | all-to-all | bytes 786432 | tf_op jit(solution)/shard_map/all_to_all | solution.py:378
  86.1 9.8 %byte_layer.1 = (bf16[8,192,128]{2,1,0:T(8,128)(2,1)S(1)}, f32[8,192]{1,0:T(8,128)S(1)}) custom-call(s32[3]{0:T(128)S(1)} %pad_add_fusion.facts_ref, bf16[8,192,128]{2,1,0:T(8,128)(2,1)S(1)} %all_to_all.20.rows_ref, s32[8,192]{1,0:T(8,128)S(1)} %bitcast.15, s32[1,192]{1,0:T(1,128)S(1)} %bitcast.17, bf16[256,1024]{1,0:T(8,128)(2,1)S(1)} %copy-done.1, ...), custom_call_target="tpu_custom_call" | custom-call | flops 6442450944 | bytes 4194304 | tf_op jit(solution)/shard_map/byte_layer/pallas_call | solution.py:503
  95.9 12.5 %all_to_all.21 = bf16[8,192,128]{2,1,0:T(8,128)(2,1)S(1)} all-to-all(bf16[8,192,128]{2,1,0:T(8,128)(2,1)S(1)} %get-tuple-element.53), channel_id=1, replica_groups=mesh['seq_0'=4,'seq_1'=2,'seq_2'=2,'grp'=8] {'seq_0','seq_1'}, dimensions={0} | all-to-all | bytes 786432 | tf_op jit(solution)/shard_map/all_to_all | solution.py:378
  108.4 0.6 collective-permute-start.1
  109.0 4.3 %backward_other.1 = (bf16[8,2,192,128]{3,2,1,0:T(8,128)(2,1)S(1)}, f32[6,128,256]{2,1,0:T(8,128)S(1)}) custom-call(bf16[8,3,192,128]{3,2,1,0:T(8,128)(2,1)S(1)} %all-to-all-done.own_ref, bf16[8,2,192,128]{3,2,1,0:T(8,128)(2,1)S(1)} %collective-permute-done.other_ref, bf16[1536,128]{1,0:T(8,128)(2,1)S(1)} %get-tuple-element.46.mixed_ref, ...), custom_call_target="tpu_custom_call" | custom-call | flops 1610612736 | bytes 4194304 | tf_op jit(solution)/shard_map/backward_other/pallas_call | solution.py:530
  113.3 0.0 collective-permute-done.1
  113.3 0.1 collective-permute-start.3
  113.4 2.0 %collective-permute-start.2 = (f32[8,192]{1,0:T(8,128)S(1)}, f32[8,192]{1,0:T(8,128)S(1)}, u32[]{:S(2)}, u32[]{:S(2)}) collective-permute-start(f32[8,192]{1,0:T(8,128)S(1)} %add.20), channel_id=1, source_target_pairs={{0,2},{1,3},{2,0},{3,1},{4,6},{5,7},{6,4},{7,5},{8,10},{9,11},{10,... | collective-permute-start | bytes 18440 | tf_op jit(solution)/shard_map/ppermute | solution.py:382
  115.4 3.5 %backward_own.1 = (bf16[1536,128]{1,0:T(8,128)(2,1)S(1)}, f32[1536,128]{1,0:T(8,128)S(1)}, f32[1536,128]{1,0:T(8,128)S(1)}) custom-call(bf16[8,3,192,128]{3,2,1,0:T(8,128)(2,1)S(1)} %all-to-all-done.own_ref, bf16[1536,128]{1,0:T(8,128)(2,1)S(1)} %get-tuple-element.46.mixed_ref, f32[1536,128]{1,0:T(8,128)S(1)} %get-tuple-element.47.inverse_ref, ...), custom_call_target="tpu_custom_call" | custom-call | flops 1409286144 | bytes 4194304 | tf_op jit(solution)/shard_map/backward_own/pallas_call | solution.py:542
  118.9 0.0 collective-permute-done.2
  118.9 3.7 %collective-permute-start.4 = (f32[8,192]{1,0:T(8,128)S(1)}, f32[8,192]{1,0:T(8,128)S(1)}, u32[]{:S(2)}, u32[]{:S(2)}) collective-permute-start(f32[8,192]{1,0:T(8,128)S(1)} %add.21), channel_id=1, source_target_pairs={{0,4},{1,5},{2,6},{3,7},{4,0},{5,1},{6,2},{7,3},{8,12},{9,13},{10,... | collective-permute-start | bytes 18440 | tf_op jit(solution)/shard_map/ppermute | solution.py:382
  122.6 1.6 %collective-permute-done.4 = f32[8,192]{1,0:T(8,128)S(1)} collective-permute-done((f32[8,192]{1,0:T(8,128)S(1)}, f32[8,192]{1,0:T(8,128)S(1)}, u32[]{:S(2)}, u32[]{:S(2)}) %collective-permute-start.4) | collective-permute-done | bytes 6176 | tf_op jit(solution)/shard_map/ppermute | solution.py:382
  124.2 1.2 join.1
  125.4 3.6 %all-to-all-start.3 = ((bf16[8,3,192,128]{3,2,1,0:T(8,128)(2,1)}), bf16[8,3,192,128]{3,2,1,0:T(8,128)(2,1)S(1)}, u32[]{:S(2)}, u32[]{:S(2)}) async-start(bf16[8,3,192,128]{3,2,1,0:T(8,128)(2,1)} %join.1), calls=%async_computation.3 | async-start | bytes 2359296 | tf_op jit(solution)/shard_map/all_to_all | solution.py:378
  129.0 0.7 dynamic-slice_bitcast_fusion
  129.7 17.6 %all-to-all-done.3.stack_ref = bf16[8,3,192,128]{3,2,1,0:T(8,128)(2,1)S(1)} async-done(((bf16[8,3,192,128]{3,2,1,0:T(8,128)(2,1)}), bf16[8,3,192,128]{3,2,1,0:T(8,128)(2,1)S(1)}, u32[]{:S(2)}, u32[]{:S(2)}) %all-to-all-start.3) | async-done | bytes 1179680 | tf_op jit(solution)/shard_map/all_to_all | solution.py:378
  147.3 1.2 unpack.1
  (16 shorter events, 0.0 us)
Async XLA Ops:
  37.8 25.7 %all-to-all-start = ((bf16[8,3,192,128]{3,2,1,0:T(8,128)(2,1)}), bf16[8,3,192,128]{3,2,1,0:T(8,128)(2,1)S(1)}, u32[]{:S(2)}, u32[]{:S(2)}) async-start(bf16[8,3,192,128]{3,2,1,0:T(8,128)(2,1)} %pack.1), calls=%async_computation | async-start | bytes 2359296 | tf_op jit(solution)/shard_map/all_to_all | solution.py:378
  63.5 3.7 %collective-permute-start = (bf16[8,2,192,128]{3,2,1,0:T(8,128)(2,1)S(1)}, bf16[8,2,192,128]{3,2,1,0:T(8,128)(2,1)S(1)}, u32[]{:S(2)}, u32[]{:S(2)}) collective-permute-start(bf16[8,2,192,128]{3,2,1,0:T(8,128)(2,1)S(1)} %slice.3), channel_id=1, source_target_pairs={{0,8},{8,0},{1,9},{9,1},{2,10},{10,2},{3,11},{11,3},{4,12},{12,4},... | collective-permute-start | bytes 2359304 | tf_op jit(solution)/shard_map/ppermute | solution.py:386
  63.6 22.4 %slice-start = ((s8[8388608]{0:T(1024)(128)(4,1)}), s8[4194304]{0:T(1024)(128)(4,1)S(1)}, s32[]{:S(2)}) async-start(s8[8388608]{0:T(1024)(128)(4,1)} %bitcast.10), calls=%async_computation.4 | async-start | bytes 8388608
  63.6 22.4 %copy-start = (bf16[1024,4096]{1,0:T(8,128)(2,1)S(1)}, bf16[1024,4096]{1,0:T(8,128)(2,1)}, u32[]{:S(2)}) copy-start(bf16[1024,4096]{1,0:T(8,128)(2,1)} %get-tuple-element.52.down_turned_ref) | copy-start | bytes 25165828
  67.2 18.8 %copy-start.1 = (bf16[256,1024]{1,0:T(8,128)(2,1)S(1)}, bf16[256,1024]{1,0:T(8,128)(2,1)}, u32[]{:S(2)}) copy-start(bf16[256,1024]{1,0:T(8,128)(2,1)} %embed_ref.1) | copy-start | bytes 1572868
  67.2 18.8 %copy-start.2 = (bf16[1024,256]{1,0:T(8,128)(2,1)S(1)}, bf16[1024,256]{1,0:T(8,128)(2,1)}, u32[]{:S(2)}) copy-start(bf16[1024,256]{1,0:T(8,128)(2,1)} %vocab_ref.1) | copy-start | bytes 1572868
  67.2 18.8 %copy-start.3 = (s32[192,8]{0,1:T(8,128)S(1)}, s32[192,8]{0,1:T(8,128)}, u32[]{:S(2)}) copy-start(s32[192,8]{0,1:T(8,128)} %param.10) | copy-start | bytes 18436
  67.2 18.8 %copy-start.4 = (f32[1024]{0:T(1024)S(1)}, f32[1024]{0:T(1024)}, u32[]{:S(2)}) copy-start(f32[1024]{0:T(1024)} %param.16) | copy-start | bytes 12292
  67.2 18.8 %copy-start.5 = (s32[192]{0:T(256)S(1)}, s32[192]{0:T(256)}, u32[]{:S(2)}) copy-start(s32[192]{0:T(256)} %param.11) | copy-start | bytes 2308
  67.2 18.8 %slice-start.1 = ((s8[8388608]{0:T(1024)(128)(4,1)}), s8[4194304]{0:T(1024)(128)(4,1)S(1)}, s32[]{:S(2)}) async-start(s8[8388608]{0:T(1024)(128)(4,1)} %bitcast.10), calls=%async_computation.5 | async-start | bytes 8388608
  108.4 4.9 %collective-permute-start.1 = (f32[8,192]{1,0:T(8,128)S(1)}, f32[8,192]{1,0:T(8,128)S(1)}, u32[]{:S(2)}, u32[]{:S(2)}) collective-permute-start(f32[8,192]{1,0:T(8,128)S(1)} %get-tuple-element.60), channel_id=1, source_target_pairs={{0,1},{1,0},{2,3},{3,2},{4,5},{5,4},{6,7},{7,6},{8,9},{9,8},{10,11... | collective-permute-start | bytes 18440 | tf_op jit(solution)/shard_map/ppermute | solution.py:382
  113.3 10.9 %collective-permute-start.3 = (bf16[8,2,192,128]{3,2,1,0:T(8,128)(2,1)S(1)}, bf16[8,2,192,128]{3,2,1,0:T(8,128)(2,1)S(1)}, u32[]{:S(2)}, u32[]{:S(2)}) collective-permute-start(bf16[8,2,192,128]{3,2,1,0:T(8,128)(2,1)S(1)} %get-tuple-element.67), channel_id=1, source_target_pairs={{0,8},{8,0},{1,9},{9,1},{2,10},{10,2},{3,11},{11,3},{4,12},{12,4},... | collective-permute-start | bytes 2359304 | tf_op jit(solution)/shard_map/ppermute | solution.py:386
  113.4 5.5 %collective-permute-start.2 = (f32[8,192]{1,0:T(8,128)S(1)}, f32[8,192]{1,0:T(8,128)S(1)}, u32[]{:S(2)}, u32[]{:S(2)}) collective-permute-start(f32[8,192]{1,0:T(8,128)S(1)} %add.20), channel_id=1, source_target_pairs={{0,2},{1,3},{2,0},{3,1},{4,6},{5,7},{6,4},{7,5},{8,10},{9,11},{10,... | collective-permute-start | bytes 18440 | tf_op jit(solution)/shard_map/ppermute | solution.py:382
  118.9 5.3 %collective-permute-start.4 = (f32[8,192]{1,0:T(8,128)S(1)}, f32[8,192]{1,0:T(8,128)S(1)}, u32[]{:S(2)}, u32[]{:S(2)}) collective-permute-start(f32[8,192]{1,0:T(8,128)S(1)} %add.21), channel_id=1, source_target_pairs={{0,4},{1,5},{2,6},{3,7},{4,0},{5,1},{6,2},{7,3},{8,12},{9,13},{10,... | collective-permute-start | bytes 18440 | tf_op jit(solution)/shard_map/ppermute | solution.py:382
  125.4 21.8 %all-to-all-start.3 = ((bf16[8,3,192,128]{3,2,1,0:T(8,128)(2,1)}), bf16[8,3,192,128]{3,2,1,0:T(8,128)(2,1)S(1)}, u32[]{:S(2)}, u32[]{:S(2)}) async-start(bf16[8,3,192,128]{3,2,1,0:T(8,128)(2,1)} %join.1), calls=%async_computation.3 | async-start | bytes 2359296 | tf_op jit(solution)/shard_map/all_to_all | solution.py:378

commit v2 on v1

--- a/solution.py
+++ b/solution.py
@@ -243,25 +243,33 @@
 
 
 def pack_kernel(*refs):
-    arrays, out_ref, sems = refs[:-2], refs[-2], refs[-1]
-    copies = []
-    for t, ref in enumerate(arrays):
-        for h in range(out_ref.shape[0]):
-            source = ref.at[:, pl.ds(h * HEAD, HEAD)]
-            copies.append(pltpu.make_async_copy(source, out_ref.at[h, t], sems.at[len(copies)]))
-            copies[-1].start()
-    for copy in copies:
-        copy.wait()
-
-
-def unpack_kernel(stack_ref, *refs):
-    arrays, sems = refs[:-1], refs[-1]
+    arrays, out_ref, held_ref, in_sems, out_sems = refs[:-4], refs[-4], refs[-3], refs[-2], refs[-1]
+    heads = out_ref.shape[0]
+    loads = [pltpu.make_async_copy(ref, held_ref.at[t], in_sems.at[t]) for t, ref in enumerate(arrays)]
+    for load in loads:
+        load.start()
+    stores = []
+    for t, load in enumerate(loads):
+        load.wait()
+        for h in range(heads):
+            source = held_ref.at[t, :, pl.ds(h * HEAD, HEAD)]
+            stores.append(pltpu.make_async_copy(source, out_ref.at[h, t], out_sems.at[len(stores)]))
+            stores[-1].start()
+    for store in stores:
+        store.wait()
+
+
+def unpack_kernel(facts_ref, stack_ref, losses_ref, *refs):
+    arrays, loss_ref, turned_s, sems = refs[:-3], refs[-3], refs[-2], refs[-1]
     copies = []
     for t, ref in enumerate(arrays):
         for h in range(stack_ref.shape[0]):
             target = ref.at[:, pl.ds(h * HEAD, HEAD)]
             copies.append(pltpu.make_async_copy(stack_ref.at[h, t], target, sems.at[len(copies)]))
             copies[-1].start()
+    slots = loss_ref.shape[1]
+    turned_s[...] = losses_ref[...].T
+    loss_ref[...] = turned_s[pl.ds(pl.multiple_of(facts_ref[0] * slots, 8), slots)].T
     for copy in copies:
         copy.wait()
 
@@ -439,8 +447,12 @@
         shape((heads, 3, count, HEAD)),
         [far()] * 3,
         anywhere(),
-        [pltpu.SemaphoreType.DMA((3 * heads,))],
-        1,
+        [
+            pltpu.VMEM((3, count, columns), BF16),
+            pltpu.SemaphoreType.DMA((3,)),
+            pltpu.SemaphoreType.DMA((3 * heads,)),
+        ],
+        4,
         0,
     )(query_rows, key_rows, value_rows)
     own = exchange(stacked)
@@ -550,7 +562,6 @@
         8 * near_rows * WIDE * HEAD,
     )(own, attended, near_inverse, near_kept, grad_rows, turned_grad)
     query_grad, losses = lax.optimization_barrier((query_grad, gather_losses(losses, 1)))
-    losses = gather_losses(losses, 2)
     joined = kernel_call(
         join_kernel,
         "join",
@@ -561,22 +572,19 @@
         4,
         0,
     )(query_grad, key_grad, value_grad, pair_sent)
-    joined, losses = lax.optimization_barrier((joined, losses))
     back = exchange(joined)
-    query_out, key_out, value_out = kernel_call(
+    losses = gather_losses(losses, 2)
+    query_out, key_out, value_out, byte_loss = kernel_call(
         unpack_kernel,
         "unpack",
-        (shape((count, columns)),) * 3,
-        [anywhere()],
-        (anywhere(),) * 3,
-        [pltpu.SemaphoreType.DMA((3 * heads,))],
-        1,
+        (shape((count, columns)),) * 3 + (shape((PATCH, count // PATCH), F32),),
+        [smem(), anywhere(), vmem()],
+        (anywhere(),) * 3 + (vmem(),),
+        [pltpu.VMEM((count, PATCH), F32), pltpu.SemaphoreType.DMA((3 * heads,))],
+        2,
         0,
-    )(back)
-
-    own_slots = count // PATCH
-    byte_loss = lax.dynamic_slice_in_dim(losses, place * own_slots, own_slots, 1).T
-    return byte_loss, query_out, key_out, value_out
+    )(facts, back, losses)
+    return byte_loss.T, query_out, key_out, value_out
 
 
 def solution(mesh):

time: 149 us -> 111 us (0.74)
  Pallas kernels: 79.7 us -> 46 us
  waiting for transfers between devices: 23.6 us -> 19.9 us
    pallas_call x1, Pallas kernels: 37 us -> 2.29 us  [shards(): kernel_call(pack_kernel, 'pack', shape((heads, 3, count, HEAD)), [far()]...]
    all_to_all x2, waiting for transfers between devices: 21.9 us -> 18.2 us  [exchange(): return lax.all_to_all(value, CHIPS, split_axis=0, concat_axis=0, tiled=True)]
  transfers between devices with their start and end apart: 7 -> 7, of which waited for: 3 -> 3; matrix products, arithmetic and copies ran while one was open for 0% -> 0% of each run, Pallas kernels for 17% -> 23%
where the time goes in v2:
time: 111 us
  Pallas kernels  46 us (41%)
  blocking collectives  26.5 us (24%)
  waiting for transfers between devices  19.9 us (18%)
  starting transfers between devices  17 us (15%)
    all_to_all x2, blocking collectives, exchange(): return lax.all_to_all(value, CHIPS, split_axis=0, concat_axis=0, tiled=True)  26.5 us
    all_to_all x2, waiting for transfers between devices, exchange(): return lax.all_to_all(value, CHIPS, split_axis=0, concat_axis=0, tiled=True)  18.2 us
    pallas_call x1, Pallas kernels, shards(): pl.pallas_call(turn_kernel, out_shape=(pltpu.HBM((hidden, columns), BF16)...  14.3 us
    all_to_all x2, starting transfers between devices, exchange(): return lax.all_to_all(value, CHIPS, split_axis=0, concat_axis=0, tiled=True)  10.6 us
    pallas_call x1, Pallas kernels, shards(): kernel_call(functools.partial(byte_kernel, byte_pieces), 'byte_layer', (s...  9.82 us
    ppermute x3, starting transfers between devices, gather_losses(): lax.ppermute(value, 'grp', [(i, i ^ 1 << bit) for i in range(PATCH)])  6.26 us
    pallas_call x1, Pallas kernels, shards(): kernel_call(functools.partial(forward_other, far_plan), 'forward_other',...  4.73 us
    pallas_call x1, Pallas kernels, shards(): kernel_call(functools.partial(backward_other, far_plan), 'backward_other'...  4.25 us
  transfers between devices with their start and end apart: 7, of which 3 were waited for; matrix products, arithmetic and copies ran while one was open for 0% of the time, Pallas kernels for 23%

profile of v2, /device:TPU:0, one launch (start us, length us, event | category | flops | bytes accessed | tf_op | source)
XLA Modules:
  0.0 110.7 jit_solution(10115386199196342398)
XLA Ops:
  0.6 0.1 pad_add_fusion.facts_ref
  0.7 2.3 %pack.1 = bf16[8,3,192,128]{3,2,1,0:T(8,128)(2,1)} custom-call(bf16[192,1024]{1,0:T(8,128)(2,1)} %refs_0_, bf16[192,1024]{1,0:T(8,128)(2,1)} %refs_1_.1, bf16[192,1024]{1,0:T(8,128)(2,1)} %refs_2_.1), custom_call_target="tpu_custom_call" | custom-call | bytes 4194304 | tf_op jit(solution)/shard_map/pack/pallas_call | solution.py:444
  3.0 7.0 %all-to-all-start = ((bf16[8,3,192,128]{3,2,1,0:T(8,128)(2,1)}), bf16[8,3,192,128]{3,2,1,0:T(8,128)(2,1)S(1)}, u32[]{:S(2)}, u32[]{:S(2)}) async-start(bf16[8,3,192,128]{3,2,1,0:T(8,128)(2,1)} %pack.1), calls=%async_computation | async-start | bytes 2359296 | tf_op jit(solution)/shard_map/all_to_all | solution.py:386
  10.0 14.3 %turn_weights.1 = (bf16[4096,1024]{1,0:T(8,128)(2,1)}, bf16[1024,4096]{1,0:T(8,128)(2,1)}) custom-call(bf16[1024,4096]{1,0:T(8,128)(2,1)} %load_ref.2, bf16[4096,1024]{1,0:T(8,128)(2,1)} %load_ref.3), custom_call_target="tpu_custom_call" | custom-call | bytes 33554432 | tf_op jit(solution)/shard_map/turn_weights/pallas_call | solution.py:465
  24.4 4.3 %all-to-all-done.own_ref = bf16[8,3,192,128]{3,2,1,0:T(8,128)(2,1)S(1)} async-done(((bf16[8,3,192,128]{3,2,1,0:T(8,128)(2,1)}), bf16[8,3,192,128]{3,2,1,0:T(8,128)(2,1)S(1)}, u32[]{:S(2)}, u32[]{:S(2)}) %all-to-all-start) | async-done | bytes 1179680 | tf_op jit(solution)/shard_map/all_to_all | solution.py:386
  28.7 0.1 slice.3
  28.7 0.1 collective-permute-start
  28.8 0.0 slice-start
  28.9 3.5 %forward_own.1 = (bf16[5376,256]{1,0:T(8,128)(2,1)S(1)}, f32[6,128,256]{2,1,0:T(8,128)S(1)}, f32[6,8,256]{2,1,0:T(8,128)S(1)}, bf16[1024,4096]{1,0:T(8,128)(2,1)S(1)}) custom-call(bf16[8,3,192,128]{3,2,1,0:T(8,128)(2,1)S(1)} %all-to-all-done.own_ref, bf16[1024,4096]{1,0:T(8,128)(2,1)} %load_ref.2), custom_call_target="tpu_custom_call" | custom-call | flops 704643072 | bytes 4194304 | tf_op jit(solution)/shard_map/forward_own/pallas_call | solution.py:479
  32.4 0.0 copy-start.1
  32.4 0.0 copy-start.2
  32.4 0.0 copy-start.3
  32.4 0.0 copy-start.4
  32.5 0.0 copy-start.5
  32.5 0.0 collective-permute-done.other_ref
  32.5 0.0 slice-start.1
  32.5 4.7 %forward_other.1 = (bf16[6144,256]{1,0:T(8,128)(2,1)S(1)}, bf16[1536,128]{1,0:T(8,128)(2,1)S(1)}, f32[1536,128]{1,0:T(8,128)S(1)}, f32[1536,128]{1,0:T(8,128)S(1)}, bf16[4096,1024]{1,0:T(8,128)(2,1)S(1)}) custom-call(s32[3]{0:T(128)S(1)} %pad_add_fusion.facts_ref, bf16[8,3,192,128]{3,2,1,0:T(8,128)(2,1)S(1)} %all-to-all-done.own_ref, ...), custom_call_target="tpu_custom_call" | custom-call | flops 805306368 | bytes 4194304 | tf_op jit(solution)/shard_map/forward_other/pallas_call | solution.py:495
  37.2 14.0 %all_to_all.20.rows_ref = bf16[8,192,128]{2,1,0:T(8,128)(2,1)S(1)} all-to-all(bf16[8,192,128]{2,1,0:T(8,128)(2,1)S(1)} %bitcast.11), channel_id=1, replica_groups=mesh['seq_0'=4,'seq_1'=2,'seq_2'=2,'grp'=8] {'seq_0','seq_1'}, dimensions={0} | all-to-all | bytes 786432 | tf_op jit(solution)/shard_map/all_to_all | solution.py:386
  51.3 9.8 %byte_layer.1 = (bf16[8,192,128]{2,1,0:T(8,128)(2,1)S(1)}, f32[8,192]{1,0:T(8,128)S(1)}) custom-call(s32[3]{0:T(128)S(1)} %pad_add_fusion.facts_ref, bf16[8,192,128]{2,1,0:T(8,128)(2,1)S(1)} %all_to_all.20.rows_ref, s32[8,192]{1,0:T(8,128)S(1)} %bitcast.14, s32[1,192]{1,0:T(1,128)S(1)} %bitcast.16, bf16[256,1024]{1,0:T(8,128)(2,1)S(1)} %copy-done.1, ...), custom_call_target="tpu_custom_call" | custom-call | flops 6442450944 | bytes 4194304 | tf_op jit(solution)/shard_map/byte_layer/pallas_call | solution.py:515
  61.1 12.5 %all_to_all.21 = bf16[8,192,128]{2,1,0:T(8,128)(2,1)S(1)} all-to-all(bf16[8,192,128]{2,1,0:T(8,128)(2,1)S(1)} %get-tuple-element.52), channel_id=1, replica_groups=mesh['seq_0'=4,'seq_1'=2,'seq_2'=2,'grp'=8] {'seq_0','seq_1'}, dimensions={0} | all-to-all | bytes 786432 | tf_op jit(solution)/shard_map/all_to_all | solution.py:386
  73.6 0.6 collective-permute-start.1
  74.2 4.3 %backward_other.1 = (bf16[8,2,192,128]{3,2,1,0:T(8,128)(2,1)S(1)}, f32[6,128,256]{2,1,0:T(8,128)S(1)}) custom-call(bf16[8,3,192,128]{3,2,1,0:T(8,128)(2,1)S(1)} %all-to-all-done.own_ref, bf16[8,2,192,128]{3,2,1,0:T(8,128)(2,1)S(1)} %collective-permute-done.other_ref, bf16[1536,128]{1,0:T(8,128)(2,1)S(1)} %get-tuple-element.45.mixed_ref, ...), custom_call_target="tpu_custom_call" | custom-call | flops 1610612736 | bytes 4194304 | tf_op jit(solution)/shard_map/backward_other/pallas_call | solution.py:542
  78.5 0.1 collective-permute-start.3
  78.6 2.0 %collective-permute-start.2 = (f32[8,192]{1,0:T(8,128)S(1)}, f32[8,192]{1,0:T(8,128)S(1)}, u32[]{:S(2)}, u32[]{:S(2)}) collective-permute-start(f32[8,192]{1,0:T(8,128)S(1)} %add.17), channel_id=1, source_target_pairs={{0,2},{1,3},{2,0},{3,1},{4,6},{5,7},{6,4},{7,5},{8,10},{9,11},{10,... | collective-permute-start | bytes 18440 | tf_op jit(solution)/shard_map/ppermute | solution.py:390
  80.6 3.5 %backward_own.1 = (bf16[1536,128]{1,0:T(8,128)(2,1)S(1)}, f32[1536,128]{1,0:T(8,128)S(1)}, f32[1536,128]{1,0:T(8,128)S(1)}) custom-call(bf16[8,3,192,128]{3,2,1,0:T(8,128)(2,1)S(1)} %all-to-all-done.own_ref, bf16[1536,128]{1,0:T(8,128)(2,1)S(1)} %get-tuple-element.45.mixed_ref, f32[1536,128]{1,0:T(8,128)S(1)} %get-tuple-element.46.inverse_ref, ...), custom_call_target="tpu_custom_call" | custom-call | flops 1409286144 | bytes 4194304 | tf_op jit(solution)/shard_map/backward_own/pallas_call | solution.py:554
  84.1 0.0 collective-permute-done.2
  84.2 1.2 %join.1 = bf16[8,3,192,128]{3,2,1,0:T(8,128)(2,1)} custom-call(bf16[1536,128]{1,0:T(8,128)(2,1)S(1)} %get-tuple-element.63.query_ref, f32[1536,128]{1,0:T(8,128)S(1)} %get-tuple-element.64.key_ref, f32[1536,128]{1,0:T(8,128)S(1)} %get-tuple-element.65.value_ref, bf16[8,2,192,128]{3,2,1,0:T(8,128)(2,1)S(1)} %collective-permute-done.3.pair_ref), custom_call_target="tpu_custom_call" | custom-call | bytes 4194304 | tf_op jit(solution)/shard_map/join/pallas_call | solution.py:565
  85.4 3.6 %all-to-all-start.3 = ((bf16[8,3,192,128]{3,2,1,0:T(8,128)(2,1)}), bf16[8,3,192,128]{3,2,1,0:T(8,128)(2,1)S(1)}, u32[]{:S(2)}, u32[]{:S(2)}) async-start(bf16[8,3,192,128]{3,2,1,0:T(8,128)(2,1)} %join.1), calls=%async_computation.3 | async-start | bytes 2359296 | tf_op jit(solution)/shard_map/all_to_all | solution.py:386
  89.0 3.7 %collective-permute-start.4 = (f32[8,192]{1,0:T(8,128)S(1)}, f32[8,192]{1,0:T(8,128)S(1)}, u32[]{:S(2)}, u32[]{:S(2)}) collective-permute-start(f32[8,192]{1,0:T(8,128)S(1)} %add.18), channel_id=1, source_target_pairs={{0,4},{1,5},{2,6},{3,7},{4,0},{5,1},{6,2},{7,3},{8,12},{9,13},{10,... | collective-permute-start | bytes 18440 | tf_op jit(solution)/shard_map/ppermute | solution.py:390
  92.6 1.6 %collective-permute-done.4 = f32[8,192]{1,0:T(8,128)S(1)} collective-permute-done((f32[8,192]{1,0:T(8,128)S(1)}, f32[8,192]{1,0:T(8,128)S(1)}, u32[]{:S(2)}, u32[]{:S(2)}) %collective-permute-start.4) | collective-permute-done | bytes 6176 | tf_op jit(solution)/shard_map/ppermute | solution.py:390
  94.3 13.9 %all-to-all-done.3.stack_ref = bf16[8,3,192,128]{3,2,1,0:T(8,128)(2,1)S(1)} async-done(((bf16[8,3,192,128]{3,2,1,0:T(8,128)(2,1)}), bf16[8,3,192,128]{3,2,1,0:T(8,128)(2,1)S(1)}, u32[]{:S(2)}, u32[]{:S(2)}) %all-to-all-start.3) | async-done | bytes 1179680 | tf_op jit(solution)/shard_map/all_to_all | solution.py:386
  108.2 2.3 %unpack.1 = (bf16[192,1024]{1,0:T(8,128)(2,1)}, bf16[192,1024]{1,0:T(8,128)(2,1)}, bf16[192,1024]{1,0:T(8,128)(2,1)}, f32[8,24]{1,0:T(8,128)}) custom-call(s32[3]{0:T(128)S(1)} %pad_add_fusion.facts_ref, bf16[8,3,192,128]{3,2,1,0:T(8,128)(2,1)S(1)} %all-to-all-done.3.stack_ref, f32[8,192]{1,0:T(8,128)S(1)} %add.19.losses_ref), custom_call_target="tpu_custom_call" | custom-call | bytes 4194304 | tf_op jit(solution)/shard_map/unpack/pallas_call | solution.py:577
  (15 shorter events, 0.0 us)
Async XLA Ops:
  3.0 25.7 %all-to-all-start = ((bf16[8,3,192,128]{3,2,1,0:T(8,128)(2,1)}), bf16[8,3,192,128]{3,2,1,0:T(8,128)(2,1)S(1)}, u32[]{:S(2)}, u32[]{:S(2)}) async-start(bf16[8,3,192,128]{3,2,1,0:T(8,128)(2,1)} %pack.1), calls=%async_computation | async-start | bytes 2359296 | tf_op jit(solution)/shard_map/all_to_all | solution.py:386
  28.7 3.7 %collective-permute-start = (bf16[8,2,192,128]{3,2,1,0:T(8,128)(2,1)S(1)}, bf16[8,2,192,128]{3,2,1,0:T(8,128)(2,1)S(1)}, u32[]{:S(2)}, u32[]{:S(2)}) collective-permute-start(bf16[8,2,192,128]{3,2,1,0:T(8,128)(2,1)S(1)} %slice.3), channel_id=1, source_target_pairs={{0,8},{8,0},{1,9},{9,1},{2,10},{10,2},{3,11},{11,3},{4,12},{12,4},... | collective-permute-start | bytes 2359304 | tf_op jit(solution)/shard_map/ppermute | solution.py:394
  28.8 22.4 %slice-start = ((s8[8388608]{0:T(1024)(128)(4,1)}), s8[4194304]{0:T(1024)(128)(4,1)S(1)}, s32[]{:S(2)}) async-start(s8[8388608]{0:T(1024)(128)(4,1)} %bitcast.9), calls=%async_computation.4 | async-start | bytes 8388608
  28.8 22.4 %copy-start = (bf16[1024,4096]{1,0:T(8,128)(2,1)S(1)}, bf16[1024,4096]{1,0:T(8,128)(2,1)}, u32[]{:S(2)}) copy-start(bf16[1024,4096]{1,0:T(8,128)(2,1)} %get-tuple-element.51.down_turned_ref) | copy-start | bytes 25165828
  32.4 18.8 %copy-start.1 = (bf16[256,1024]{1,0:T(8,128)(2,1)S(1)}, bf16[256,1024]{1,0:T(8,128)(2,1)}, u32[]{:S(2)}) copy-start(bf16[256,1024]{1,0:T(8,128)(2,1)} %embed_ref.1) | copy-start | bytes 1572868
  32.4 18.8 %copy-start.2 = (bf16[1024,256]{1,0:T(8,128)(2,1)S(1)}, bf16[1024,256]{1,0:T(8,128)(2,1)}, u32[]{:S(2)}) copy-start(bf16[1024,256]{1,0:T(8,128)(2,1)} %vocab_ref.1) | copy-start | bytes 1572868
  32.4 18.8 %copy-start.3 = (s32[192,8]{0,1:T(8,128)S(1)}, s32[192,8]{0,1:T(8,128)}, u32[]{:S(2)}) copy-start(s32[192,8]{0,1:T(8,128)} %param.10) | copy-start | bytes 18436
  32.4 18.8 %copy-start.4 = (f32[1024]{0:T(1024)S(1)}, f32[1024]{0:T(1024)}, u32[]{:S(2)}) copy-start(f32[1024]{0:T(1024)} %param.16) | copy-start | bytes 12292
  32.5 18.8 %copy-start.5 = (s32[192]{0:T(256)S(1)}, s32[192]{0:T(256)}, u32[]{:S(2)}) copy-start(s32[192]{0:T(256)} %param.11) | copy-start | bytes 2308
  32.5 18.8 %slice-start.1 = ((s8[8388608]{0:T(1024)(128)(4,1)}), s8[4194304]{0:T(1024)(128)(4,1)S(1)}, s32[]{:S(2)}) async-start(s8[8388608]{0:T(1024)(128)(4,1)} %bitcast.9), calls=%async_computation.5 | async-start | bytes 8388608
  73.6 4.9 %collective-permute-start.1 = (f32[8,192]{1,0:T(8,128)S(1)}, f32[8,192]{1,0:T(8,128)S(1)}, u32[]{:S(2)}, u32[]{:S(2)}) collective-permute-start(f32[8,192]{1,0:T(8,128)S(1)} %get-tuple-element.59), channel_id=1, source_target_pairs={{0,1},{1,0},{2,3},{3,2},{4,5},{5,4},{6,7},{7,6},{8,9},{9,8},{10,11... | collective-permute-start | bytes 18440 | tf_op jit(solution)/shard_map/ppermute | solution.py:390
  78.5 5.6 %collective-permute-start.3 = (bf16[8,2,192,128]{3,2,1,0:T(8,128)(2,1)S(1)}, bf16[8,2,192,128]{3,2,1,0:T(8,128)(2,1)S(1)}, u32[]{:S(2)}, u32[]{:S(2)}) collective-permute-start(bf16[8,2,192,128]{3,2,1,0:T(8,128)(2,1)S(1)} %get-tuple-element.66), channel_id=1, source_target_pairs={{0,8},{8,0},{1,9},{9,1},{2,10},{10,2},{3,11},{11,3},{4,12},{12,4},... | collective-permute-start | bytes 2359304 | tf_op jit(solution)/shard_map/ppermute | solution.py:394
  78.6 5.5 %collective-permute-start.2 = (f32[8,192]{1,0:T(8,128)S(1)}, f32[8,192]{1,0:T(8,128)S(1)}, u32[]{:S(2)}, u32[]{:S(2)}) collective-permute-start(f32[8,192]{1,0:T(8,128)S(1)} %add.17), channel_id=1, source_target_pairs={{0,2},{1,3},{2,0},{3,1},{4,6},{5,7},{6,4},{7,5},{8,10},{9,11},{10,... | collective-permute-start | bytes 18440 | tf_op jit(solution)/shard_map/ppermute | solution.py:390
  85.4 22.8 %all-to-all-start.3 = ((bf16[8,3,192,128]{3,2,1,0:T(8,128)(2,1)}), bf16[8,3,192,128]{3,2,1,0:T(8,128)(2,1)S(1)}, u32[]{:S(2)}, u32[]{:S(2)}) async-start(bf16[8,3,192,128]{3,2,1,0:T(8,128)(2,1)} %join.1), calls=%async_computation.3 | async-start | bytes 2359296 | tf_op jit(solution)/shard_map/all_to_all | solution.py:386
  89.0 5.3 %collective-permute-start.4 = (f32[8,192]{1,0:T(8,128)S(1)}, f32[8,192]{1,0:T(8,128)S(1)}, u32[]{:S(2)}, u32[]{:S(2)}) collective-permute-start(f32[8,192]{1,0:T(8,128)S(1)} %add.18), channel_id=1, source_target_pairs={{0,4},{1,5},{2,6},{3,7},{4,0},{5,1},{6,2},{7,3},{8,12},{9,13},{10,... | collective-permute-start | bytes 18440 | tf_op jit(solution)/shard_map/ppermute | solution.py:390

commit v3 on v2

--- a/solution.py
+++ b/solution.py
@@ -139,19 +139,14 @@
     other_ref,
     mixed_ref,
     stats_ref,
-    load_ref,
     kept_ref,
     out_ref,
     own_inverse_ref,
     inverse_ref,
-    loaded_ref,
     key_s,
     turned_s,
     score_s,
-    sem,
 ):
-    load = pltpu.make_async_copy(load_ref, loaded_ref, sem)
-    load.start()
     flat_rows(other_ref, 0, key_s)
     turned_rows(other_ref, 1, turned_s)
     core = facts_ref[2]
@@ -168,7 +163,6 @@
         out_ref[rows] = (mixed * inverse).T.astype(BF16)
         inverse_ref[rows] = jnp.broadcast_to(inverse, (HEAD, WIDE)).T
         own_inverse_ref[rows] = jnp.broadcast_to(own_part * inverse, (HEAD, WIDE)).T
-    load.wait()
 
 
 def backward_side(
@@ -260,7 +254,7 @@
 
 
 def unpack_kernel(facts_ref, stack_ref, losses_ref, *refs):
-    arrays, loss_ref, turned_s, sems = refs[:-3], refs[-3], refs[-2], refs[-1]
+    arrays, loss_ref, turned_s, loss_s, sems = refs[:-4], refs[-4], refs[-3], refs[-2], refs[-1]
     copies = []
     for t, ref in enumerate(arrays):
         for h in range(stack_ref.shape[0]):
@@ -269,21 +263,18 @@
             copies[-1].start()
     slots = loss_ref.shape[1]
     turned_s[...] = losses_ref[...].T
-    loss_ref[...] = turned_s[pl.ds(pl.multiple_of(facts_ref[0] * slots, 8), slots)].T
+    loss_s[...] = turned_s[pl.ds(pl.multiple_of(facts_ref[0] * slots, 8), slots)].T
+    copies.append(pltpu.make_async_copy(loss_s, loss_ref, sems.at[len(copies)]))
+    copies[-1].start()
     for copy in copies:
         copy.wait()
 
 
-def turn_kernel(up_ref, down_ref, up_out, down_out):
-    up_out[...] = up_ref[...].T
-    down_out[...] = down_ref[...].T
-
-
 GELU_A = 0.7978845608028654
 GELU_B = 0.044715
 
 
-def byte_kernel(
+def byte_forward(
     pieces,
     facts_ref,
     rows_ref,
@@ -293,12 +284,12 @@
     gain_ref,
     up_ref,
     down_ref,
-    up_turned_ref,
-    down_turned_ref,
     vocab_ref,
+    loss_ref,
+    bend_ref,
+    hidden_ref,
+    scale_ref,
     grad_ref,
-    loss_ref,
-    bend_s,
 ):
     heads, count, _ = rows_ref.shape
     size = up_ref.shape[1] // pieces
@@ -313,8 +304,9 @@
     hidden_in = jnp.concatenate([rows_ref[h].astype(F32) for h in range(heads)], 1)
     hidden_in = hidden_in + dot(one_hot, embed_ref[...])
     inverse_rms = lax.rsqrt(jnp.mean(hidden_in * hidden_in, axis=1, keepdims=True) + EPSILON)
-    gain = gain_ref[...]
-    normed = (hidden_in * inverse_rms * gain).astype(BF16)
+    normed = (hidden_in * inverse_rms * gain_ref[...]).astype(BF16)
+    hidden_ref[...] = hidden_in
+    scale_ref[...] = jnp.broadcast_to(inverse_rms, scale_ref.shape)
     after = hidden_in
     for i in range(pieces):
         part = pl.ds(i * size, size)
@@ -322,7 +314,7 @@
         square = raised * raised
         half = 0.5 + 0.5 * jnp.tanh(raised * (GELU_A + (GELU_A * GELU_B) * square))
         active = (raised * half).astype(BF16)
-        bend_s[:, part] = half + half * (1.0 - half) * raised * (
+        bend_ref[:, part] = half + half * (1.0 - half) * raised * (
             2.0 * GELU_A + (6.0 * GELU_A * GELU_B) * square
         )
         after = after + dot(active, down_ref[part])
@@ -336,22 +328,34 @@
     chosen = jnp.sum(jnp.where(is_target, logits, 0.0), axis=1, keepdims=True)
     loss = jnp.log(mass) + row_top - chosen
     row_at = lax.broadcasted_iota(jnp.int32, (count, count), 0)
-    ordered = jnp.sum(jnp.where(row_at == order_ref[...] - facts_ref[1], loss, 0.0), axis=0, keepdims=True)
+    ordered = jnp.sum(
+        jnp.where(row_at == order_ref[...] - facts_ref[1], loss, 0.0), axis=0, keepdims=True
+    )
     slot = lax.broadcasted_iota(jnp.int32, loss_ref.shape, 0)
     loss_ref[...] = jnp.where(slot == place, ordered, 0.0)
     logit_grad = raised_mass / mass - jnp.where(is_target, 1.0, 0.0)
     final_grad = dot(logit_grad.astype(BF16), vocab_ref[...], NT).astype(BF16).astype(F32)
     mean_dot = jnp.mean(final_grad * after, axis=1, keepdims=True)
-    after_grad = final_scale * final_grad - after * (final_scale * final_scale * final_scale * mean_dot)
+    grad_ref[...] = final_scale * final_grad - after * (
+        final_scale * final_scale * final_scale * mean_dot
+    )
+
+
+def byte_backward(pieces, gain_ref, up_ref, down_ref, bend_ref, hidden_ref, scale_ref, after_ref, grad_ref):
+    heads, count, _ = grad_ref.shape
+    size = up_ref.shape[1] // pieces
+    after_grad = after_ref[...]
     narrow = after_grad.astype(BF16)
     normed_grad = None
     for i in range(pieces):
         part = pl.ds(i * size, size)
-        active_grad = dot(narrow, down_turned_ref[:, part]).astype(BF16).astype(F32)
-        raised_grad = (active_grad * bend_s[:, part]).astype(BF16)
-        term = dot(raised_grad, up_turned_ref[part])
+        active_grad = dot(narrow, down_ref[part], NT).astype(BF16).astype(F32)
+        raised_grad = (active_grad * bend_ref[:, part]).astype(BF16)
+        term = dot(raised_grad, up_ref[:, part], NT)
         normed_grad = term if normed_grad is None else normed_grad + term
-    scaled = normed_grad.astype(BF16).astype(F32) * gain
+    hidden_in = hidden_ref[...]
+    inverse_rms = scale_ref[:, 0:1]
+    scaled = normed_grad.astype(BF16).astype(F32) * gain_ref[...]
     mean_dot = jnp.mean(scaled * hidden_in, axis=1, keepdims=True)
     total = (
         after_grad
@@ -457,33 +461,17 @@
     )(query_rows, key_rows, value_rows)
     own = exchange(stacked)
 
-    size = 512
-    w_up = pltpu.with_memory_space_constraint(w_up, pltpu.HBM)
-    w_down = pltpu.with_memory_space_constraint(w_down, pltpu.HBM)
-    wide_block = pl.BlockSpec((columns, size), lambda i: (0, i))
-    tall_block = pl.BlockSpec((size, columns), lambda i: (i, 0))
-    turned = pl.pallas_call(
-        turn_kernel,
-        out_shape=(pltpu.HBM((hidden, columns), BF16), pltpu.HBM((columns, hidden), BF16)),
-        grid=(hidden // size,),
-        in_specs=[wide_block, tall_block],
-        out_specs=(tall_block, wide_block),
-        compiler_params=pltpu.CompilerParams(vmem_limit_bytes=12 * MIB),
-        cost_estimate=pl.CostEstimate(flops=0, bytes_accessed=32 * MIB, transcendentals=0),
-        name="turn_weights",
-    )(w_up, w_down)
-    own, turned = lax.optimization_barrier((own, turned))
     other = swap_cores(own[:, 1:])
 
     kv_scratch = [pltpu.VMEM((rows, HEAD), BF16), pltpu.VMEM((HEAD, rows), BF16)]
-    near_kept, near_mixed, stats, up_held = kernel_call(
+    near_kept, near_mixed, stats, down_held = kernel_call(
         functools.partial(forward_own, near_plan),
         "forward_own",
         (
             held((near_rows, WIDE)),
             held((chunks, HEAD, WIDE), F32),
             held((chunks, 8, WIDE), F32),
-            held(w_up.shape),
+            held(w_down.shape),
         ),
         [vmem(), far()],
         (vmem(),) * 4,
@@ -491,8 +479,8 @@
         8,
         4 * near_rows * WIDE * HEAD,
         near_rows * WIDE,
-    )(own, w_up)
-    far_kept, attended, near_inverse, far_inverse, down_held = kernel_call(
+    )(own, pltpu.with_memory_space_constraint(w_down, pltpu.HBM))
+    far_kept, attended, near_inverse, far_inverse = kernel_call(
         functools.partial(forward_other, far_plan),
         "forward_other",
         (
@@ -500,27 +488,33 @@
             held((rows, HEAD)),
             held((rows, HEAD), F32),
             held((rows, HEAD), F32),
-            held(w_down.shape),
         ),
-        [smem()] + [vmem()] * 4 + [far()],
-        (vmem(),) * 5,
-        kv_scratch + [pltpu.VMEM((rows, WIDE), F32), pltpu.SemaphoreType.DMA],
+        [smem()] + [vmem()] * 4,
+        (vmem(),) * 4,
+        kv_scratch + [pltpu.VMEM((rows, WIDE), F32)],
         8,
         4 * far_rows * WIDE * HEAD,
         far_rows * WIDE,
-    )(facts, own, other, near_mixed, stats, w_down)
+    )(facts, own, other, near_mixed, stats)
 
     byte_pieces = 4
     owned_rows = exchange(attended.reshape(heads, count, HEAD))
-    context_grad, losses = kernel_call(
-        functools.partial(byte_kernel, byte_pieces),
-        "byte_layer",
-        (shape((heads, count, HEAD)), shape((PATCH, count), F32)),
-        [smem()] + [vmem()] * 10,
-        (vmem(), vmem()),
-        [pltpu.VMEM((count, hidden), F32)],
-        14,
-        8 * count * columns * hidden,
+    gain = norm_gain[None]
+    losses, bend, hidden_in, scale, after_grad = kernel_call(
+        functools.partial(byte_forward, byte_pieces),
+        "byte_forward",
+        (
+            shape((PATCH, count), F32),
+            held((count, hidden), F32),
+            held((count, columns), F32),
+            held((count, HEAD), F32),
+            held((count, columns), F32),
+        ),
+        [smem()] + [vmem()] * 8,
+        (vmem(),) * 5,
+        [],
+        12,
+        4 * count * columns * hidden,
         count * hidden,
     )(
         facts,
@@ -528,13 +522,23 @@
         byte_ids.T,
         patch_order[None],
         byte_embed,
-        norm_gain[None],
-        up_held,
+        gain,
+        w_up,
         down_held,
-        *turned,
         vocab_head,
     )
-
+    sent_losses = gather_losses(losses, 0)
+    context_grad = kernel_call(
+        functools.partial(byte_backward, byte_pieces),
+        "byte_backward",
+        held((heads, count, HEAD)),
+        [vmem()] * 7,
+        vmem(),
+        [],
+        12,
+        4 * count * columns * hidden,
+    )(gain, w_up, down_held, bend, hidden_in, scale, after_grad)
+    context_grad, losses = lax.optimization_barrier((context_grad, sent_losses))
     grad_rows, losses = lax.optimization_barrier((exchange(context_grad), losses))
     grad_rows = grad_rows.reshape(rows, HEAD)
     side_scratch = kv_scratch + [pltpu.VMEM((rows, WIDE), BF16)]
@@ -549,7 +553,7 @@
         8,
         8 * far_rows * WIDE * HEAD,
     )(own, other, attended, far_inverse, far_kept, grad_rows)
-    pair_grad, turned_grad, losses = lax.optimization_barrier((pair_grad, turned_grad, gather_losses(losses, 0)))
+    pair_grad, turned_grad, losses = lax.optimization_barrier((pair_grad, turned_grad, gather_losses(losses, 1)))
     pair_sent = swap_cores(pair_grad)
     query_grad, key_grad, value_grad = kernel_call(
         functools.partial(backward_own, near_plan),
@@ -561,7 +565,7 @@
         8,
         8 * near_rows * WIDE * HEAD,
     )(own, attended, near_inverse, near_kept, grad_rows, turned_grad)
-    query_grad, losses = lax.optimization_barrier((query_grad, gather_losses(losses, 1)))
+    query_grad, losses = lax.optimization_barrier((query_grad, gather_losses(losses, 2)))
     joined = kernel_call(
         join_kernel,
         "join",
@@ -573,14 +577,17 @@
         0,
     )(query_grad, key_grad, value_grad, pair_sent)
     back = exchange(joined)
-    losses = gather_losses(losses, 2)
     query_out, key_out, value_out, byte_loss = kernel_call(
         unpack_kernel,
         "unpack",
         (shape((count, columns)),) * 3 + (shape((PATCH, count // PATCH), F32),),
         [smem(), anywhere(), vmem()],
-        (anywhere(),) * 3 + (vmem(),),
-        [pltpu.VMEM((count, PATCH), F32), pltpu.SemaphoreType.DMA((3 * heads,))],
+        (anywhere(),) * 4,
+        [
+            pltpu.VMEM((count, PATCH), F32),
+            pltpu.VMEM((PATCH, count // PATCH), F32),
+            pltpu.SemaphoreType.DMA((3 * heads + 1,)),
+        ],
         2,
         0,
     )(facts, back, losses)

time: 111 us -> 114 us (1.027)
  blocking collectives: 26.5 us -> 73.6 us
  waiting for transfers between devices: 19.9 us -> 0.01 us
  Pallas kernels: 46 us -> 31.7 us
  starting transfers between devices: 17 us -> 6.84 us
    all_to_all x2 -> x4, blocking collectives: 26.5 us -> 73.6 us  [exchange(): return lax.all_to_all(value, CHIPS, split_axis=0, concat_axis=0, tiled=True)]
    all_to_all x2 -> x0, waiting for transfers between devices: 18.2 us -> none  [exchange(): return lax.all_to_all(value, CHIPS, split_axis=0, concat_axis=0, tiled=True)]
    pallas_call x2, Pallas kernels: 24.1 us -> 12.7 us  [the longest x1 6.75 us: shards(): kernel_call(functools.partial(byte_forward, byte_pieces), 'byte_forward',...]
    all_to_all x2 -> x0, starting transfers between devices: 10.6 us -> none  [exchange(): return lax.all_to_all(value, CHIPS, split_axis=0, concat_axis=0, tiled=True)]
    ppermute x3, waiting for transfers between devices: 1.64 us -> 0.01 us  [gather_losses(): lax.ppermute(value, 'grp', [(i, i ^ 1 << bit) for i in range(PATCH)])]
  transfers between devices with their start and end apart: 7 -> 5, of which waited for: 3 -> 0; matrix products, arithmetic and copies ran while one was open for 0% -> 0% of each run, Pallas kernels for 23% -> 15%
where the time goes in v3:
time: 114 us; the launch traced here: 113 us
  blocking collectives  73.6 us (65%)
  Pallas kernels  31.7 us (28%)
  starting transfers between devices  6.84 us (6%)
    all_to_all x4, blocking collectives, exchange(): return lax.all_to_all(value, CHIPS, split_axis=0, concat_axis=0, tiled=True)  73.6 us
    pallas_call x1, Pallas kernels, shards(): kernel_call(functools.partial(byte_forward, byte_pieces), 'byte_forward',...  6.75 us
    ppermute x3, starting transfers between devices, gather_losses(): lax.ppermute(value, 'grp', [(i, i ^ 1 << bit) for i in range(PATCH)])  6.67 us
    pallas_call x1, Pallas kernels, shards(): kernel_call(functools.partial(byte_backward, byte_pieces), 'byte_backward...  5.95 us
    pallas_call x1, Pallas kernels, shards(): kernel_call(functools.partial(backward_other, far_plan), 'backward_other'...  4.26 us
    pallas_call x1, Pallas kernels, shards(): kernel_call(functools.partial(forward_other, far_plan), 'forward_other',...  4.16 us
    pallas_call x1, Pallas kernels, shards(): kernel_call(functools.partial(forward_own, near_plan), 'forward_own', (he...  3.54 us
    pallas_call x1, Pallas kernels, shards(): kernel_call(functools.partial(backward_own, near_plan), 'backward_own', (...  3.51 us
  transfers between devices with their start and end apart: 5, of which 0 were waited for; matrix products, arithmetic and copies ran while one was open for 0% of the time, Pallas kernels for 15%

profile of v3, /device:TPU:0, one launch (start us, length us, event | category | flops | bytes accessed | tf_op | source)
XLA Modules:
  0.0 113.4 jit_solution(17062382249022207474)
XLA Ops:
  0.6 0.1 pad_add_fusion.facts_ref
  0.7 1.6 %pack.1 = bf16[8,3,192,128]{3,2,1,0:T(8,128)(2,1)S(1)} custom-call(bf16[192,1024]{1,0:T(8,128)(2,1)} %refs_0_, bf16[192,1024]{1,0:T(8,128)(2,1)} %refs_1_.1, bf16[192,1024]{1,0:T(8,128)(2,1)} %refs_2_.1), custom_call_target="tpu_custom_call" | custom-call | bytes 4194304 | tf_op jit(solution)/shard_map/pack/pallas_call | solution.py:448
  2.3 0.0 slice-start
  2.4 25.8 %all_to_all.20.own_ref = bf16[8,3,192,128]{3,2,1,0:T(8,128)(2,1)S(1)} all-to-all(bf16[8,3,192,128]{3,2,1,0:T(8,128)(2,1)S(1)} %pack.1), channel_id=1, replica_groups=mesh['seq_0'=4,'seq_1'=2,'seq_2'=2,'grp'=8] {'seq_0','seq_1'}, dimensions={0} | all-to-all | bytes 2359296 | tf_op jit(solution)/shard_map/all_to_all | solution.py:390
  28.2 0.1 slice.4
  28.2 0.0 slice-start.1
  28.2 0.1 collective-permute-start
  28.3 3.5 %forward_own.1 = (bf16[5376,256]{1,0:T(8,128)(2,1)S(1)}, f32[6,128,256]{2,1,0:T(8,128)S(1)}, f32[6,8,256]{2,1,0:T(8,128)S(1)}, bf16[4096,1024]{1,0:T(8,128)(2,1)S(1)}) custom-call(bf16[8,3,192,128]{3,2,1,0:T(8,128)(2,1)S(1)} %all_to_all.20.own_ref, bf16[4096,1024]{1,0:T(8,128)(2,1)} %load_ref.1), custom_call_target="tpu_custom_call" | custom-call | flops 704643072 | bytes 4194304 | tf_op jit(solution)/shard_map/forward_own/pallas_call | solution.py:467
  31.9 0.0 copy-start
  31.9 0.0 copy-start.1
  31.9 0.0 copy-start.2
  31.9 0.0 copy-start.3
  31.9 0.0 copy-start.4
  31.9 0.0 collective-permute-done.other_ref
  31.9 4.2 %forward_other.1 = (bf16[6144,256]{1,0:T(8,128)(2,1)S(1)}, bf16[1536,128]{1,0:T(8,128)(2,1)S(1)}, f32[1536,128]{1,0:T(8,128)S(1)}, f32[1536,128]{1,0:T(8,128)S(1)}) custom-call(s32[3]{0:T(128)S(1)} %pad_add_fusion.facts_ref, bf16[8,3,192,128]{3,2,1,0:T(8,128)(2,1)S(1)} %all_to_all.20.own_ref, bf16[8,2,192,128]{3,2,1,0:T(8,128)(2,1)S(1)} %collective-permute-done.other_ref, ...), custom_call_target="tpu_custom_call" | custom-call | flops 805306368 | bytes 4194304 | tf_op jit(solution)/shard_map/forward_other/pallas_call | solution.py:483
  36.1 13.5 %all_to_all.21.rows_ref = bf16[8,192,128]{2,1,0:T(8,128)(2,1)S(1)} all-to-all(bf16[8,192,128]{2,1,0:T(8,128)(2,1)S(1)} %bitcast.11), channel_id=1, replica_groups=mesh['seq_0'=4,'seq_1'=2,'seq_2'=2,'grp'=8] {'seq_0','seq_1'}, dimensions={0} | all-to-all | bytes 786432 | tf_op jit(solution)/shard_map/all_to_all | solution.py:390
  49.6 6.8 %byte_forward.1 = (f32[8,192]{1,0:T(8,128)S(1)}, f32[192,4096]{1,0:T(8,128)S(1)}, f32[192,1024]{1,0:T(8,128)S(1)}, f32[192,128]{1,0:T(8,128)S(1)}, f32[192,1024]{1,0:T(8,128)S(1)}) custom-call(s32[3]{0:T(128)S(1)} %pad_add_fusion.facts_ref, bf16[8,192,128]{2,1,0:T(8,128)(2,1)S(1)} %all_to_all.21.rows_ref, s32[8,192]{1,0:T(8,128)S(1)} %bitcast.16, ...), custom_call_target="tpu_custom_call" | custom-call | flops 3221225472 | bytes 4194304 | tf_op jit(solution)/shard_map/byte_forward/pallas_call | solution.py:503
  56.4 0.9 collective-permute-start.1
  57.3 6.0 %byte_backward.1 = bf16[8,192,128]{2,1,0:T(8,128)(2,1)S(1)} custom-call(f32[1,1024]{1,0:T(1,128)S(1)} %bitcast.15, bf16[1024,4096]{1,0:T(8,128)(2,1)S(1)} %bitcast.10, bf16[4096,1024]{1,0:T(8,128)(2,1)S(1)} %get-tuple-element.44.down_ref, f32[192,4096]{1,0:T(8,128)S(1)} %get-tuple-element.45.bend_ref, f32[192,1024]{1,0:T(8,128)S(1)} %get-tuple-element.46.hidden_ref, ...), custom_call_target="tpu_custom_call" | custom-call | flops 3221225472 | bytes 4194304 | tf_op jit(solution)/shard_map/byte_backward/pallas_call | solution.py:531
  63.2 0.0 collective-permute-done.1
  63.2 12.8 %all_to_all.22 = bf16[8,192,128]{2,1,0:T(8,128)(2,1)S(1)} all-to-all(bf16[8,192,128]{2,1,0:T(8,128)(2,1)S(1)} %byte_backward.1), channel_id=1, replica_groups=mesh['seq_0'=4,'seq_1'=2,'seq_2'=2,'grp'=8] {'seq_0','seq_1'}, dimensions={0} | all-to-all | bytes 786432 | tf_op jit(solution)/shard_map/all_to_all | solution.py:390
  76.1 1.9 %collective-permute-start.2 = (f32[8,192]{1,0:T(8,128)S(1)}, f32[8,192]{1,0:T(8,128)S(1)}, u32[]{:S(2)}, u32[]{:S(2)}) collective-permute-start(f32[8,192]{1,0:T(8,128)S(1)} %add.17), channel_id=1, source_target_pairs={{0,2},{1,3},{2,0},{3,1},{4,6},{5,7},{6,4},{7,5},{8,10},{9,11},{10,... | collective-permute-start | bytes 18440 | tf_op jit(solution)/shard_map/ppermute | solution.py:394
  78.0 4.3 %backward_other.1 = (bf16[8,2,192,128]{3,2,1,0:T(8,128)(2,1)S(1)}, f32[6,128,256]{2,1,0:T(8,128)S(1)}) custom-call(bf16[8,3,192,128]{3,2,1,0:T(8,128)(2,1)S(1)} %all_to_all.20.own_ref, bf16[8,2,192,128]{3,2,1,0:T(8,128)(2,1)S(1)} %collective-permute-done.other_ref, bf16[1536,128]{1,0:T(8,128)(2,1)S(1)} %get-tuple-element.41.mixed_ref, ...), custom_call_target="tpu_custom_call" | custom-call | flops 1610612736 | bytes 4194304 | tf_op jit(solution)/shard_map/backward_other/pallas_call | solution.py:546
  82.2 0.0 collective-permute-done.2
  82.3 0.1 collective-permute-start.4
  82.4 3.9 %collective-permute-start.3 = (f32[8,192]{1,0:T(8,128)S(1)}, f32[8,192]{1,0:T(8,128)S(1)}, u32[]{:S(2)}, u32[]{:S(2)}) collective-permute-start(f32[8,192]{1,0:T(8,128)S(1)} %add.18), channel_id=1, source_target_pairs={{0,4},{1,5},{2,6},{3,7},{4,0},{5,1},{6,2},{7,3},{8,12},{9,13},{10,... | collective-permute-start | bytes 18440 | tf_op jit(solution)/shard_map/ppermute | solution.py:394
  86.2 3.5 %backward_own.1 = (bf16[1536,128]{1,0:T(8,128)(2,1)S(1)}, f32[1536,128]{1,0:T(8,128)S(1)}, f32[1536,128]{1,0:T(8,128)S(1)}) custom-call(bf16[8,3,192,128]{3,2,1,0:T(8,128)(2,1)S(1)} %all_to_all.20.own_ref, bf16[1536,128]{1,0:T(8,128)(2,1)S(1)} %get-tuple-element.41.mixed_ref, f32[1536,128]{1,0:T(8,128)S(1)} %get-tuple-element.42.inverse_ref, ...), custom_call_target="tpu_custom_call" | custom-call | flops 1409286144 | bytes 4194304 | tf_op jit(solution)/shard_map/backward_own/pallas_call | solution.py:558
  89.8 0.0 collective-permute-done.3
  89.8 0.0 collective-permute-done.4.pair_ref
  89.8 0.2 join.1
  90.0 21.5 %all_to_all.23.stack_ref = bf16[8,3,192,128]{3,2,1,0:T(8,128)(2,1)S(1)} all-to-all(bf16[8,3,192,128]{3,2,1,0:T(8,128)(2,1)S(1)} %join.1), channel_id=1, replica_groups=mesh['seq_0'=4,'seq_1'=2,'seq_2'=2,'grp'=8] {'seq_0','seq_1'}, dimensions={0} | all-to-all | bytes 2359296 | tf_op jit(solution)/shard_map/all_to_all | solution.py:390
  111.5 1.7 %unpack.1 = (bf16[192,1024]{1,0:T(8,128)(2,1)}, bf16[192,1024]{1,0:T(8,128)(2,1)}, bf16[192,1024]{1,0:T(8,128)(2,1)}, f32[8,24]{1,0:T(8,128)}) custom-call(s32[3]{0:T(128)S(1)} %pad_add_fusion.facts_ref, bf16[8,3,192,128]{3,2,1,0:T(8,128)(2,1)S(1)} %all_to_all.23.stack_ref, f32[8,192]{1,0:T(8,128)S(1)} %add.19.losses_ref), custom_call_target="tpu_custom_call" | custom-call | bytes 4194304 | tf_op jit(solution)/shard_map/unpack/pallas_call | solution.py:580
  (11 shorter events, 0.0 us)
Async XLA Ops:
  2.3 47.2 %slice-start = ((s8[8388608]{0:T(1024)(128)(4,1)}), s8[4194304]{0:T(1024)(128)(4,1)S(1)}, s32[]{:S(2)}) async-start(s8[8388608]{0:T(1024)(128)(4,1)} %bitcast.9), calls=%async_computation.4 | async-start | bytes 8388608
  28.2 21.4 %slice-start.1 = ((s8[8388608]{0:T(1024)(128)(4,1)}), s8[4194304]{0:T(1024)(128)(4,1)S(1)}, s32[]{:S(2)}) async-start(s8[8388608]{0:T(1024)(128)(4,1)} %bitcast.9), calls=%async_computation.5 | async-start | bytes 8388608
  28.2 3.7 %collective-permute-start = (bf16[8,2,192,128]{3,2,1,0:T(8,128)(2,1)S(1)}, bf16[8,2,192,128]{3,2,1,0:T(8,128)(2,1)S(1)}, u32[]{:S(2)}, u32[]{:S(2)}) collective-permute-start(bf16[8,2,192,128]{3,2,1,0:T(8,128)(2,1)S(1)} %slice.4), channel_id=1, source_target_pairs={{0,8},{8,0},{1,9},{9,1},{2,10},{10,2},{3,11},{11,3},{4,12},{12,4},... | collective-permute-start | bytes 2359304 | tf_op jit(solution)/shard_map/ppermute | solution.py:398
  31.9 17.7 %copy-start = (bf16[256,1024]{1,0:T(8,128)(2,1)S(1)}, bf16[256,1024]{1,0:T(8,128)(2,1)}, u32[]{:S(2)}) copy-start(bf16[256,1024]{1,0:T(8,128)(2,1)} %embed_ref.1) | copy-start | bytes 1572868
  31.9 17.7 %copy-start.1 = (bf16[1024,256]{1,0:T(8,128)(2,1)S(1)}, bf16[1024,256]{1,0:T(8,128)(2,1)}, u32[]{:S(2)}) copy-start(bf16[1024,256]{1,0:T(8,128)(2,1)} %vocab_ref.1) | copy-start | bytes 1572868
  31.9 17.7 %copy-start.2 = (f32[1024]{0:T(1024)S(1)}, f32[1024]{0:T(1024)}, u32[]{:S(2)}) copy-start(f32[1024]{0:T(1024)} %param.16) | copy-start | bytes 12292
  31.9 17.7 %copy-start.3 = (s32[192,8]{0,1:T(8,128)S(1)}, s32[192,8]{0,1:T(8,128)}, u32[]{:S(2)}) copy-start(s32[192,8]{0,1:T(8,128)} %param.10) | copy-start | bytes 18436
  31.9 17.7 %copy-start.4 = (s32[192]{0:T(256)S(1)}, s32[192]{0:T(256)}, u32[]{:S(2)}) copy-start(s32[192]{0:T(256)} %param.11) | copy-start | bytes 2308
  56.4 6.8 %collective-permute-start.1 = (f32[8,192]{1,0:T(8,128)S(1)}, f32[8,192]{1,0:T(8,128)S(1)}, u32[]{:S(2)}, u32[]{:S(2)}) collective-permute-start(f32[8,192]{1,0:T(8,128)S(1)} %get-tuple-element.49), channel_id=1, source_target_pairs={{0,1},{1,0},{2,3},{3,2},{4,5},{5,4},{6,7},{7,6},{8,9},{9,8},{10,11... | collective-permute-start | bytes 18440 | tf_op jit(solution)/shard_map/ppermute | solution.py:394
  76.1 6.2 %collective-permute-start.2 = (f32[8,192]{1,0:T(8,128)S(1)}, f32[8,192]{1,0:T(8,128)S(1)}, u32[]{:S(2)}, u32[]{:S(2)}) collective-permute-start(f32[8,192]{1,0:T(8,128)S(1)} %add.17), channel_id=1, source_target_pairs={{0,2},{1,3},{2,0},{3,1},{4,6},{5,7},{6,4},{7,5},{8,10},{9,11},{10,... | collective-permute-start | bytes 18440 | tf_op jit(solution)/shard_map/ppermute | solution.py:394
  82.3 7.5 %collective-permute-start.4 = (bf16[8,2,192,128]{3,2,1,0:T(8,128)(2,1)S(1)}, bf16[8,2,192,128]{3,2,1,0:T(8,128)(2,1)S(1)}, u32[]{:S(2)}, u32[]{:S(2)}) collective-permute-start(bf16[8,2,192,128]{3,2,1,0:T(8,128)(2,1)S(1)} %get-tuple-element.64), channel_id=1, source_target_pairs={{0,8},{8,0},{1,9},{9,1},{2,10},{10,2},{3,11},{11,3},{4,12},{12,4},... | collective-permute-start | bytes 2359304 | tf_op jit(solution)/shard_map/ppermute | solution.py:398
  82.4 7.4 %collective-permute-start.3 = (f32[8,192]{1,0:T(8,128)S(1)}, f32[8,192]{1,0:T(8,128)S(1)}, u32[]{:S(2)}, u32[]{:S(2)}) collective-permute-start(f32[8,192]{1,0:T(8,128)S(1)} %add.18), channel_id=1, source_target_pairs={{0,4},{1,5},{2,6},{3,7},{4,0},{5,1},{6,2},{7,3},{8,12},{9,13},{10,... | collective-permute-start | bytes 18440 | tf_op jit(solution)/shard_map/ppermute | solution.py:394

commit v4 on v2

--- a/solution.py
+++ b/solution.py
@@ -260,16 +260,22 @@
 
 
 def unpack_kernel(facts_ref, stack_ref, losses_ref, *refs):
-    arrays, loss_ref, turned_s, sems = refs[:-3], refs[-3], refs[-2], refs[-1]
+    arrays, loss_ref, row_s, turned_s, loss_s, sems = refs[:-5], refs[-5], refs[-4], refs[-3], refs[-2], refs[-1]
     copies = []
     for t, ref in enumerate(arrays):
         for h in range(stack_ref.shape[0]):
             target = ref.at[:, pl.ds(h * HEAD, HEAD)]
             copies.append(pltpu.make_async_copy(stack_ref.at[h, t], target, sems.at[len(copies)]))
-            copies[-1].start()
-    slots = loss_ref.shape[1]
-    turned_s[...] = losses_ref[...].T
-    loss_ref[...] = turned_s[pl.ds(pl.multiple_of(facts_ref[0] * slots, 8), slots)].T
+    fetch = pltpu.make_async_copy(losses_ref.at[:, pl.ds(0, 8)], row_s, sems.at[len(copies)])
+    fetch.start()
+    for copy in copies:
+        copy.start()
+    fetch.wait()
+    slots = loss_s.shape[1]
+    turned_s[...] = row_s[:, 0].T
+    loss_s[...] = turned_s[pl.ds(pl.multiple_of(facts_ref[0] * slots, 8), slots)].T
+    copies.append(pltpu.make_async_copy(loss_s, loss_ref, sems.at[len(copies) + 1]))
+    copies[-1].start()
     for copy in copies:
         copy.wait()
 
@@ -278,6 +284,8 @@
     up_out[...] = up_ref[...].T
     down_out[...] = down_ref[...].T
 
+
+LOSS_ROWS = 128
 
 GELU_A = 0.7978845608028654
 GELU_B = 0.044715
@@ -337,8 +345,8 @@
     loss = jnp.log(mass) + row_top - chosen
     row_at = lax.broadcasted_iota(jnp.int32, (count, count), 0)
     ordered = jnp.sum(jnp.where(row_at == order_ref[...] - facts_ref[1], loss, 0.0), axis=0, keepdims=True)
-    slot = lax.broadcasted_iota(jnp.int32, loss_ref.shape, 0)
-    loss_ref[...] = jnp.where(slot == place, ordered, 0.0)
+    loss_ref[...] = jnp.zeros(loss_ref.shape, F32)
+    loss_ref[0:1, 0:count] = ordered
     logit_grad = raised_mass / mass - jnp.where(is_target, 1.0, 0.0)
     final_grad = dot(logit_grad.astype(BF16), vocab_ref[...], NT).astype(BF16).astype(F32)
     mean_dot = jnp.mean(final_grad * after, axis=1, keepdims=True)
@@ -384,10 +392,6 @@
 
 def exchange(value):
     return lax.all_to_all(value, CHIPS, split_axis=0, concat_axis=0, tiled=True)
-
-
-def gather_losses(value, bit):
-    return value + lax.ppermute(value, "grp", [(i, i ^ (1 << bit)) for i in range(PATCH)])
 
 
 def swap_cores(value):
@@ -515,7 +519,7 @@
     context_grad, losses = kernel_call(
         functools.partial(byte_kernel, byte_pieces),
         "byte_layer",
-        (shape((heads, count, HEAD)), shape((PATCH, count), F32)),
+        (shape((heads, count, HEAD)), shape((LOSS_ROWS, 2 * HEAD), F32)),
         [smem()] + [vmem()] * 10,
         (vmem(), vmem()),
         [pltpu.VMEM((count, hidden), F32)],
@@ -535,8 +539,7 @@
         vocab_head,
     )
 
-    grad_rows, losses = lax.optimization_barrier((exchange(context_grad), losses))
-    grad_rows = grad_rows.reshape(rows, HEAD)
+    grad_rows = exchange(context_grad).reshape(rows, HEAD)
     side_scratch = kv_scratch + [pltpu.VMEM((rows, WIDE), BF16)]
     sums = [pltpu.VMEM((rows, HEAD), F32)] * 2
     pair_grad, turned_grad = kernel_call(
@@ -549,7 +552,6 @@
         8,
         8 * far_rows * WIDE * HEAD,
     )(own, other, attended, far_inverse, far_kept, grad_rows)
-    pair_grad, turned_grad, losses = lax.optimization_barrier((pair_grad, turned_grad, gather_losses(losses, 0)))
     pair_sent = swap_cores(pair_grad)
     query_grad, key_grad, value_grad = kernel_call(
         functools.partial(backward_own, near_plan),
@@ -561,7 +563,6 @@
         8,
         8 * near_rows * WIDE * HEAD,
     )(own, attended, near_inverse, near_kept, grad_rows, turned_grad)
-    query_grad, losses = lax.optimization_barrier((query_grad, gather_losses(losses, 1)))
     joined = kernel_call(
         join_kernel,
         "join",
@@ -572,18 +573,24 @@
         4,
         0,
     )(query_grad, key_grad, value_grad, pair_sent)
+    joined, losses = lax.optimization_barrier((joined, losses))
+    all_losses = pltpu.with_memory_space_constraint(lax.all_gather(losses, "grp"), pltpu.HBM)
     back = exchange(joined)
-    losses = gather_losses(losses, 2)
     query_out, key_out, value_out, byte_loss = kernel_call(
         unpack_kernel,
         "unpack",
         (shape((count, columns)),) * 3 + (shape((PATCH, count // PATCH), F32),),
-        [smem(), anywhere(), vmem()],
-        (anywhere(),) * 3 + (vmem(),),
-        [pltpu.VMEM((count, PATCH), F32), pltpu.SemaphoreType.DMA((3 * heads,))],
+        [smem(), anywhere(), anywhere()],
+        (anywhere(),) * 4,
+        [
+            pltpu.VMEM((PATCH, 8, 2 * HEAD), F32),
+            pltpu.VMEM((2 * HEAD, PATCH), F32),
+            pltpu.VMEM((PATCH, count // PATCH), F32),
+            pltpu.SemaphoreType.DMA((3 * heads + 2,)),
+        ],
         2,
         0,
-    )(facts, back, losses)
+    )(facts, back, all_losses)
     return byte_loss.T, query_out, key_out, value_out
 
 

time: 111 us -> 142 us (1.28)
  blocking collectives: 26.5 us -> 58.3 us
  between operations: 1.06 us -> 14.3 us
  starting transfers between devices: 17 us -> 7.45 us
  waiting for transfers between devices: 19.9 us -> 16.3 us
    all_to_all x2 -> x3, blocking collectives: 26.5 us -> 58.3 us  [exchange(): return lax.all_to_all(value, CHIPS, split_axis=0, concat_axis=0, tiled=True)]
    all_to_all x2 -> x1, waiting for transfers between devices: 18.2 us -> 4.41 us  [exchange(): return lax.all_to_all(value, CHIPS, split_axis=0, concat_axis=0, tiled=True)]
    all_gather x0 -> x1, waiting for transfers between devices: none -> 11.8 us  [shards(): lax.all_gather(losses, 'grp')]
    ppermute x3 -> x0, starting transfers between devices: 6.26 us -> none  [gather_losses(): lax.ppermute(value, 'grp', [(i, i ^ 1 << bit) for i in range(PATCH)])]
    all_to_all x2 -> x1, starting transfers between devices: 10.6 us -> 7.03 us  [exchange(): return lax.all_to_all(value, CHIPS, split_axis=0, concat_axis=0, tiled=True)]
    ppermute x3 -> x0, waiting for transfers between devices: 1.64 us -> none  [gather_losses(): lax.ppermute(value, 'grp', [(i, i ^ 1 << bit) for i in range(PATCH)])]
  transfers between devices with their start and end apart: 7 -> 4, of which waited for: 3 -> 2; matrix products, arithmetic and copies ran while one was open for 0% -> 0% of each run, Pallas kernels for 23% -> 15%
where the time goes in v4:
time: 142 us; the launch traced here: 141 us
  blocking collectives  58.3 us (41%)
  Pallas kernels  44.9 us (32%)
  waiting for transfers between devices  16.3 us (11%)
  between operations  14.3 us (10%)
  starting transfers between devices  7.45 us (5%)
    all_to_all x3, blocking collectives, exchange(): return lax.all_to_all(value, CHIPS, split_axis=0, concat_axis=0, tiled=True)  58.3 us
    pallas_call x1, Pallas kernels, shards(): pl.pallas_call(turn_kernel, out_shape=(pltpu.HBM((hidden, columns), BF16)...  14.2 us
    all_gather x1, waiting for transfers between devices, shards(): lax.all_gather(losses, 'grp')  11.8 us
    pallas_call x1, Pallas kernels, shards(): kernel_call(functools.partial(byte_kernel, byte_pieces), 'byte_layer', (s...  9.83 us
    all_to_all x1, starting transfers between devices, exchange(): return lax.all_to_all(value, CHIPS, split_axis=0, concat_axis=0, tiled=True)  7.03 us
    pallas_call x1, Pallas kernels, shards(): kernel_call(functools.partial(forward_other, far_plan), 'forward_other',...  4.73 us
    all_to_all x1, waiting for transfers between devices, exchange(): return lax.all_to_all(value, CHIPS, split_axis=0, concat_axis=0, tiled=True)  4.41 us
    pallas_call x1, Pallas kernels, shards(): kernel_call(functools.partial(backward_other, far_plan), 'backward_other'...  4.25 us
  transfers between devices with their start and end apart: 4, of which 2 were waited for; matrix products, arithmetic and copies ran while one was open for 0% of the time, Pallas kernels for 15%

profile of v4, /device:TPU:0, one launch (start us, length us, event | category | flops | bytes accessed | tf_op | source)
XLA Modules:
  0.0 141.3 jit_solution(10230548195882763837)
XLA Ops:
  7.2 0.1 pad_add_fusion.facts_ref
  7.2 2.3 %pack.1 = bf16[8,3,192,128]{3,2,1,0:T(8,128)(2,1)} custom-call(bf16[192,1024]{1,0:T(8,128)(2,1)} %refs_0_, bf16[192,1024]{1,0:T(8,128)(2,1)} %refs_1_.1, bf16[192,1024]{1,0:T(8,128)(2,1)} %refs_2_.1), custom_call_target="tpu_custom_call" | custom-call | bytes 4194304 | tf_op jit(solution)/shard_map/pack/pallas_call | solution.py:448
  9.5 7.0 %all-to-all-start = ((bf16[8,3,192,128]{3,2,1,0:T(8,128)(2,1)}), bf16[8,3,192,128]{3,2,1,0:T(8,128)(2,1)S(1)}, u32[]{:S(2)}, u32[]{:S(2)}) async-start(bf16[8,3,192,128]{3,2,1,0:T(8,128)(2,1)} %pack.1), calls=%async_computation | async-start | bytes 2359296 | tf_op jit(solution)/shard_map/all_to_all | solution.py:394
  16.6 0.0 all-gather.3.cloned.1.call-start
  16.6 14.2 %turn_weights.1 = (bf16[4096,1024]{1,0:T(8,128)(2,1)}, bf16[1024,4096]{1,0:T(8,128)(2,1)}) custom-call(bf16[1024,4096]{1,0:T(8,128)(2,1)} %load_ref.2, bf16[4096,1024]{1,0:T(8,128)(2,1)} %load_ref.3), custom_call_target="tpu_custom_call" | custom-call | bytes 33554432 | tf_op jit(solution)/shard_map/turn_weights/pallas_call | solution.py:469
  30.8 4.4 %all-to-all-done.own_ref = bf16[8,3,192,128]{3,2,1,0:T(8,128)(2,1)S(1)} async-done(((bf16[8,3,192,128]{3,2,1,0:T(8,128)(2,1)}), bf16[8,3,192,128]{3,2,1,0:T(8,128)(2,1)S(1)}, u32[]{:S(2)}, u32[]{:S(2)}) %all-to-all-start) | async-done | bytes 1179680 | tf_op jit(solution)/shard_map/all_to_all | solution.py:394
  35.2 0.1 slice.3
  35.3 0.1 collective-permute-start
  35.4 0.0 slice-start
  35.4 0.0 copy-start
  35.4 3.5 %forward_own.1 = (bf16[5376,256]{1,0:T(8,128)(2,1)S(1)}, f32[6,128,256]{2,1,0:T(8,128)S(1)}, f32[6,8,256]{2,1,0:T(8,128)S(1)}, bf16[1024,4096]{1,0:T(8,128)(2,1)S(1)}) custom-call(bf16[8,3,192,128]{3,2,1,0:T(8,128)(2,1)S(1)} %all-to-all-done.own_ref, bf16[1024,4096]{1,0:T(8,128)(2,1)} %load_ref.2), custom_call_target="tpu_custom_call" | custom-call | flops 704643072 | bytes 4194304 | tf_op jit(solution)/shard_map/forward_own/pallas_call | solution.py:483
  38.9 0.0 copy-start.1
  38.9 0.0 copy-start.2
  38.9 0.0 copy-start.3
  39.0 0.0 copy-start.4
  39.0 0.0 copy-start.5
  39.0 0.0 collective-permute-done.other_ref
  39.0 0.0 slice-start.1
  39.0 4.7 %forward_other.1 = (bf16[6144,256]{1,0:T(8,128)(2,1)S(1)}, bf16[1536,128]{1,0:T(8,128)(2,1)S(1)}, f32[1536,128]{1,0:T(8,128)S(1)}, f32[1536,128]{1,0:T(8,128)S(1)}, bf16[4096,1024]{1,0:T(8,128)(2,1)S(1)}) custom-call(s32[3]{0:T(128)S(1)} %pad_add_fusion.facts_ref, bf16[8,3,192,128]{3,2,1,0:T(8,128)(2,1)S(1)} %all-to-all-done.own_ref, ...), custom_call_target="tpu_custom_call" | custom-call | flops 805306368 | bytes 4194304 | tf_op jit(solution)/shard_map/forward_other/pallas_call | solution.py:499
  43.7 14.0 %all_to_all.20.rows_ref = bf16[8,192,128]{2,1,0:T(8,128)(2,1)S(1)} all-to-all(bf16[8,192,128]{2,1,0:T(8,128)(2,1)S(1)} %bitcast.12), channel_id=1, replica_groups=mesh['seq_0'=4,'seq_1'=2,'seq_2'=2,'grp'=8] {'seq_0','seq_1'}, dimensions={0} | all-to-all | bytes 786432 | tf_op jit(solution)/shard_map/all_to_all | solution.py:394
  57.7 0.0 slice-done
  57.8 9.8 %byte_layer.1 = (bf16[8,192,128]{2,1,0:T(8,128)(2,1)S(1)}, f32[128,256]{1,0:T(8,128)}) custom-call(s32[3]{0:T(128)S(1)} %pad_add_fusion.facts_ref, bf16[8,192,128]{2,1,0:T(8,128)(2,1)S(1)} %all_to_all.20.rows_ref, s32[8,192]{1,0:T(8,128)S(1)} %bitcast.15, s32[1,192]{1,0:T(1,128)S(1)} %bitcast.17, bf16[256,1024]{1,0:T(8,128)(2,1)S(1)} %copy-done.1, ...), custom_call_target="tpu_custom_call" | custom-call | flops 6442450944 | bytes 4194304 | tf_op jit(solution)/shard_map/byte_layer/pallas_call | solution.py:519
  67.6 12.7 %all_to_all.21 = bf16[8,192,128]{2,1,0:T(8,128)(2,1)S(1)} all-to-all(bf16[8,192,128]{2,1,0:T(8,128)(2,1)S(1)} %get-tuple-element.47), channel_id=1, replica_groups=mesh['seq_0'=4,'seq_1'=2,'seq_2'=2,'grp'=8] {'seq_0','seq_1'}, dimensions={0} | all-to-all | bytes 786432 | tf_op jit(solution)/shard_map/all_to_all | solution.py:394
  80.3 4.2 %backward_other.1 = (bf16[8,2,192,128]{3,2,1,0:T(8,128)(2,1)S(1)}, f32[6,128,256]{2,1,0:T(8,128)S(1)}) custom-call(bf16[8,3,192,128]{3,2,1,0:T(8,128)(2,1)S(1)} %all-to-all-done.own_ref, bf16[8,2,192,128]{3,2,1,0:T(8,128)(2,1)S(1)} %collective-permute-done.other_ref, bf16[1536,128]{1,0:T(8,128)(2,1)S(1)} %get-tuple-element.40.mixed_ref, ...), custom_call_target="tpu_custom_call" | custom-call | flops 1610612736 | bytes 4194304 | tf_op jit(solution)/shard_map/backward_other/pallas_call | solution.py:545
  84.6 0.3 collective-permute-start.1
  84.9 3.5 %backward_own.1 = (bf16[1536,128]{1,0:T(8,128)(2,1)S(1)}, f32[1536,128]{1,0:T(8,128)S(1)}, f32[1536,128]{1,0:T(8,128)S(1)}) custom-call(bf16[8,3,192,128]{3,2,1,0:T(8,128)(2,1)S(1)} %all-to-all-done.own_ref, bf16[1536,128]{1,0:T(8,128)(2,1)S(1)} %get-tuple-element.40.mixed_ref, f32[1536,128]{1,0:T(8,128)S(1)} %get-tuple-element.41.inverse_ref, ...), custom_call_target="tpu_custom_call" | custom-call | flops 1409286144 | bytes 4194304 | tf_op jit(solution)/shard_map/backward_own/pallas_call | solution.py:556
  88.4 0.0 collective-permute-done.1.pair_ref
  88.4 0.2 join.1
  88.6 0.0 all-gather.3.cloned.1.call-update
  88.6 31.6 %all_to_all.22.stack_ref = bf16[8,3,192,128]{3,2,1,0:T(8,128)(2,1)S(1)} all-to-all(bf16[8,3,192,128]{3,2,1,0:T(8,128)(2,1)S(1)} %join.1), channel_id=1, replica_groups=mesh['seq_0'=4,'seq_1'=2,'seq_2'=2,'grp'=8] {'seq_0','seq_1'}, dimensions={0} | all-to-all | bytes 2359296 | tf_op jit(solution)/shard_map/all_to_all | solution.py:394
  120.2 11.8 %all-gather.3.cloned.1.call-done = f32[1024,256]{1,0:T(8,128)} async-done(((f32[128,256]{1,0:T(8,128)}), f32[1024,256]{1,0:T(8,128)}) %all-gather.3.cloned.1.call-update) | async-done | bytes 1048592 | tf_op jit(solution)/shard_map/all_gather | solution.py:577
  132.0 2.4 %unpack.1 = (bf16[192,1024]{1,0:T(8,128)(2,1)}, bf16[192,1024]{1,0:T(8,128)(2,1)}, bf16[192,1024]{1,0:T(8,128)(2,1)}, f32[8,24]{1,0:T(8,128)}) custom-call(s32[3]{0:T(128)S(1)} %pad_add_fusion.facts_ref, bf16[8,3,192,128]{3,2,1,0:T(8,128)(2,1)S(1)} %all_to_all.22.stack_ref, f32[8,128,256]{2,1,0:T(8,128)} %bitcast.18), custom_call_target="tpu_custom_call" | custom-call | bytes 4194304 | tf_op jit(solution)/shard_map/unpack/pallas_call | solution.py:579
  (8 shorter events, 0.0 us)
Async XLA Ops:
  9.5 25.7 %all-to-all-start = ((bf16[8,3,192,128]{3,2,1,0:T(8,128)(2,1)}), bf16[8,3,192,128]{3,2,1,0:T(8,128)(2,1)S(1)}, u32[]{:S(2)}, u32[]{:S(2)}) async-start(bf16[8,3,192,128]{3,2,1,0:T(8,128)(2,1)} %pack.1), calls=%async_computation | async-start | bytes 2359296 | tf_op jit(solution)/shard_map/all_to_all | solution.py:394
  16.6 115.5 %all-gather.3.cloned.1.call-start = ((), (), s32[]{:S(2)}) async-start(), calls=%async_computation.4 | async-start | bytes 1179648 | tf_op jit(solution)/shard_map/all_gather | solution.py:577
  35.3 3.7 %collective-permute-start = (bf16[8,2,192,128]{3,2,1,0:T(8,128)(2,1)S(1)}, bf16[8,2,192,128]{3,2,1,0:T(8,128)(2,1)S(1)}, u32[]{:S(2)}, u32[]{:S(2)}) collective-permute-start(bf16[8,2,192,128]{3,2,1,0:T(8,128)(2,1)S(1)} %slice.3), channel_id=1, source_target_pairs={{0,8},{8,0},{1,9},{9,1},{2,10},{10,2},{3,11},{11,3},{4,12},{12,4},... | collective-permute-start | bytes 2359304 | tf_op jit(solution)/shard_map/ppermute | solution.py:398
  35.4 22.4 %slice-start = ((s8[8388608]{0:T(1024)(128)(4,1)}), s8[4194304]{0:T(1024)(128)(4,1)S(1)}, s32[]{:S(2)}) async-start(s8[8388608]{0:T(1024)(128)(4,1)} %bitcast.10), calls=%async_computation.5 | async-start | bytes 8388608
  35.4 22.4 %copy-start = (bf16[1024,4096]{1,0:T(8,128)(2,1)S(1)}, bf16[1024,4096]{1,0:T(8,128)(2,1)}, u32[]{:S(2)}) copy-start(bf16[1024,4096]{1,0:T(8,128)(2,1)} %get-tuple-element.46.down_turned_ref) | copy-start | bytes 25165828
  38.9 18.8 %copy-start.1 = (bf16[256,1024]{1,0:T(8,128)(2,1)S(1)}, bf16[256,1024]{1,0:T(8,128)(2,1)}, u32[]{:S(2)}) copy-start(bf16[256,1024]{1,0:T(8,128)(2,1)} %embed_ref.1) | copy-start | bytes 1572868
  38.9 18.8 %copy-start.2 = (bf16[1024,256]{1,0:T(8,128)(2,1)S(1)}, bf16[1024,256]{1,0:T(8,128)(2,1)}, u32[]{:S(2)}) copy-start(bf16[1024,256]{1,0:T(8,128)(2,1)} %vocab_ref.1) | copy-start | bytes 1572868
  38.9 18.8 %copy-start.3 = (s32[192,8]{0,1:T(8,128)S(1)}, s32[192,8]{0,1:T(8,128)}, u32[]{:S(2)}) copy-start(s32[192,8]{0,1:T(8,128)} %param.10) | copy-start | bytes 18436
  39.0 18.8 %copy-start.4 = (f32[1024]{0:T(1024)S(1)}, f32[1024]{0:T(1024)}, u32[]{:S(2)}) copy-start(f32[1024]{0:T(1024)} %param.16) | copy-start | bytes 12292
  39.0 18.8 %copy-start.5 = (s32[192]{0:T(256)S(1)}, s32[192]{0:T(256)}, u32[]{:S(2)}) copy-start(s32[192]{0:T(256)} %param.11) | copy-start | bytes 2308
  39.0 18.8 %slice-start.1 = ((s8[8388608]{0:T(1024)(128)(4,1)}), s8[4194304]{0:T(1024)(128)(4,1)S(1)}, s32[]{:S(2)}) async-start(s8[8388608]{0:T(1024)(128)(4,1)} %bitcast.10), calls=%async_computation.6 | async-start | bytes 8388608
  84.6 3.8 %collective-permute-start.1 = (bf16[8,2,192,128]{3,2,1,0:T(8,128)(2,1)S(1)}, bf16[8,2,192,128]{3,2,1,0:T(8,128)(2,1)S(1)}, u32[]{:S(2)}, u32[]{:S(2)}) collective-permute-start(bf16[8,2,192,128]{3,2,1,0:T(8,128)(2,1)S(1)} %get-tuple-element.54), channel_id=1, source_target_pairs={{0,8},{8,0},{1,9},{9,1},{2,10},{10,2},{3,11},{11,3},{4,12},{12,4},... | collective-permute-start | bytes 2359304 | tf_op jit(solution)/shard_map/ppermute | solution.py:398
Sparse Core Ops, SparseCore 0:
  88.8 43.2 all-gather.2

commit v5 on v2

--- a/solution.py
+++ b/solution.py
@@ -260,16 +260,18 @@
 
 
 def unpack_kernel(facts_ref, stack_ref, losses_ref, *refs):
-    arrays, loss_ref, turned_s, sems = refs[:-3], refs[-3], refs[-2], refs[-1]
+    arrays, loss_ref, turned_s, loss_s, sems = refs[:-4], refs[-4], refs[-3], refs[-2], refs[-1]
     copies = []
     for t, ref in enumerate(arrays):
         for h in range(stack_ref.shape[0]):
             target = ref.at[:, pl.ds(h * HEAD, HEAD)]
             copies.append(pltpu.make_async_copy(stack_ref.at[h, t], target, sems.at[len(copies)]))
             copies[-1].start()
-    slots = loss_ref.shape[1]
+    slots = loss_s.shape[1]
     turned_s[...] = losses_ref[...].T
-    loss_ref[...] = turned_s[pl.ds(pl.multiple_of(facts_ref[0] * slots, 8), slots)].T
+    loss_s[...] = turned_s[pl.ds(pl.multiple_of(facts_ref[0] * slots, 8), slots)].T
+    copies.append(pltpu.make_async_copy(loss_s, loss_ref, sems.at[len(copies)]))
+    copies[-1].start()
     for copy in copies:
         copy.wait()
 
@@ -386,8 +388,13 @@
     return lax.all_to_all(value, CHIPS, split_axis=0, concat_axis=0, tiled=True)
 
 
-def gather_losses(value, bit):
-    return value + lax.ppermute(value, "grp", [(i, i ^ (1 << bit)) for i in range(PATCH)])
+def gather_losses(value, steps):
+    found = [lax.ppermute(value, "grp", [(i, (i + k) % PATCH) for i in range(PATCH)]) for k in steps]
+    return functools.reduce(jnp.add, found, value)
+
+
+def pair_losses(value):
+    return value + lax.ppermute(value, "grp", [(i, i ^ 1) for i in range(PATCH)])
 
 
 def swap_cores(value):
@@ -549,7 +556,7 @@
         8,
         8 * far_rows * WIDE * HEAD,
     )(own, other, attended, far_inverse, far_kept, grad_rows)
-    pair_grad, turned_grad, losses = lax.optimization_barrier((pair_grad, turned_grad, gather_losses(losses, 0)))
+    pair_grad, turned_grad, losses = lax.optimization_barrier((pair_grad, turned_grad, gather_losses(losses, (2, 4, 6))))
     pair_sent = swap_cores(pair_grad)
     query_grad, key_grad, value_grad = kernel_call(
         functools.partial(backward_own, near_plan),
@@ -561,7 +568,7 @@
         8,
         8 * near_rows * WIDE * HEAD,
     )(own, attended, near_inverse, near_kept, grad_rows, turned_grad)
-    query_grad, losses = lax.optimization_barrier((query_grad, gather_losses(losses, 1)))
+    query_grad, losses = lax.optimization_barrier((query_grad, pair_losses(losses)))
     joined = kernel_call(
         join_kernel,
         "join",
@@ -573,14 +580,17 @@
         0,
     )(query_grad, key_grad, value_grad, pair_sent)
     back = exchange(joined)
-    losses = gather_losses(losses, 2)
     query_out, key_out, value_out, byte_loss = kernel_call(
         unpack_kernel,
         "unpack",
         (shape((count, columns)),) * 3 + (shape((PATCH, count // PATCH), F32),),
         [smem(), anywhere(), vmem()],
-        (anywhere(),) * 3 + (vmem(),),
-        [pltpu.VMEM((count, PATCH), F32), pltpu.SemaphoreType.DMA((3 * heads,))],
+        (anywhere(),) * 4,
+        [
+            pltpu.VMEM((count, PATCH), F32),
+            pltpu.VMEM((PATCH, count // PATCH), F32),
+            pltpu.SemaphoreType.DMA((3 * heads + 1,)),
+        ],
         2,
         0,
     )(facts, back, losses)

time: 111 us -> 112 us (level)
  blocking collectives: 26.5 us -> 48.6 us
  waiting for transfers between devices: 19.9 us -> 4.4 us
  starting transfers between devices: 17 us -> 13.2 us
  Pallas kernels: 46 us -> 44.3 us
    all_to_all x2 -> x3, blocking collectives: 26.5 us -> 48.6 us  [exchange(): return lax.all_to_all(value, CHIPS, split_axis=0, concat_axis=0, tiled=True)]
    all_to_all x2 -> x1, waiting for transfers between devices: 18.2 us -> 4.38 us  [exchange(): return lax.all_to_all(value, CHIPS, split_axis=0, concat_axis=0, tiled=True)]
    all_to_all x2 -> x1, starting transfers between devices: 10.6 us -> 7.03 us  [exchange(): return lax.all_to_all(value, CHIPS, split_axis=0, concat_axis=0, tiled=True)]
    ppermute x3 -> x4, waiting for transfers between devices: 1.64 us -> 0.01 us  [the longest x3 0.01 us: gather_losses(): lax.ppermute(value, 'grp', [(i, (i + k) % PATCH) for i in range(PATCH)])]
    ppermute x3 -> x4, starting transfers between devices: 6.26 us -> 5.97 us  [the longest x3 5.3 us: gather_losses(): lax.ppermute(value, 'grp', [(i, (i + k) % PATCH) for i in range(PATCH)])]
  transfers between devices with their start and end apart: 7 -> 7, of which waited for: 3 -> 1; matrix products, arithmetic and copies ran while one was open for 0% -> 0% of each run, Pallas kernels for 23% -> 23%
where the time goes in v5:
time: 112 us
  blocking collectives  48.6 us (43%)
  Pallas kernels  44.3 us (40%)
  starting transfers between devices  13.2 us (12%)
  waiting for transfers between devices  4.4 us (4%)
    all_to_all x3, blocking collectives, exchange(): return lax.all_to_all(value, CHIPS, split_axis=0, concat_axis=0, tiled=True)  48.6 us
    pallas_call x1, Pallas kernels, shards(): pl.pallas_call(turn_kernel, out_shape=(pltpu.HBM((hidden, columns), BF16)...  14.3 us
    pallas_call x1, Pallas kernels, shards(): kernel_call(functools.partial(byte_kernel, byte_pieces), 'byte_layer', (s...  9.82 us
    all_to_all x1, starting transfers between devices, exchange(): return lax.all_to_all(value, CHIPS, split_axis=0, concat_axis=0, tiled=True)  7.03 us
    ppermute x3, starting transfers between devices, gather_losses(): lax.ppermute(value, 'grp', [(i, (i + k) % PATCH) for i in range(PATCH)])  5.3 us
    pallas_call x1, Pallas kernels, shards(): kernel_call(functools.partial(forward_other, far_plan), 'forward_other',...  4.73 us
    all_to_all x1, waiting for transfers between devices, exchange(): return lax.all_to_all(value, CHIPS, split_axis=0, concat_axis=0, tiled=True)  4.38 us
    pallas_call x1, Pallas kernels, shards(): kernel_call(functools.partial(backward_other, far_plan), 'backward_other'...  4.25 us
  transfers between devices with their start and end apart: 7, of which 1 were waited for; matrix products, arithmetic and copies ran while one was open for 0% of the time, Pallas kernels for 23%

profile of v5, /device:TPU:0, one launch (start us, length us, event | category | flops | bytes accessed | tf_op | source)
XLA Modules:
  0.0 111.8 jit_solution(15264847157770034194)
XLA Ops:
  0.6 0.1 pad_add_fusion.facts_ref
  0.7 2.3 %pack.1 = bf16[8,3,192,128]{3,2,1,0:T(8,128)(2,1)} custom-call(bf16[192,1024]{1,0:T(8,128)(2,1)} %refs_0_, bf16[192,1024]{1,0:T(8,128)(2,1)} %refs_1_.1, bf16[192,1024]{1,0:T(8,128)(2,1)} %refs_2_.1), custom_call_target="tpu_custom_call" | custom-call | bytes 4194304 | tf_op jit(solution)/shard_map/pack/pallas_call | solution.py:451
  3.0 7.0 %all-to-all-start = ((bf16[8,3,192,128]{3,2,1,0:T(8,128)(2,1)}), bf16[8,3,192,128]{3,2,1,0:T(8,128)(2,1)S(1)}, u32[]{:S(2)}, u32[]{:S(2)}) async-start(bf16[8,3,192,128]{3,2,1,0:T(8,128)(2,1)} %pack.1), calls=%async_computation | async-start | bytes 2359296 | tf_op jit(solution)/shard_map/all_to_all | solution.py:388
  10.0 14.3 %turn_weights.1 = (bf16[4096,1024]{1,0:T(8,128)(2,1)}, bf16[1024,4096]{1,0:T(8,128)(2,1)}) custom-call(bf16[1024,4096]{1,0:T(8,128)(2,1)} %load_ref.2, bf16[4096,1024]{1,0:T(8,128)(2,1)} %load_ref.3), custom_call_target="tpu_custom_call" | custom-call | bytes 33554432 | tf_op jit(solution)/shard_map/turn_weights/pallas_call | solution.py:472
  24.3 4.4 %all-to-all-done.own_ref = bf16[8,3,192,128]{3,2,1,0:T(8,128)(2,1)S(1)} async-done(((bf16[8,3,192,128]{3,2,1,0:T(8,128)(2,1)}), bf16[8,3,192,128]{3,2,1,0:T(8,128)(2,1)S(1)}, u32[]{:S(2)}, u32[]{:S(2)}) %all-to-all-start) | async-done | bytes 1179680 | tf_op jit(solution)/shard_map/all_to_all | solution.py:388
  28.7 0.1 slice.3
  28.7 0.1 collective-permute-start
  28.8 0.0 slice-start
  28.8 3.5 %forward_own.1 = (bf16[5376,256]{1,0:T(8,128)(2,1)S(1)}, f32[6,128,256]{2,1,0:T(8,128)S(1)}, f32[6,8,256]{2,1,0:T(8,128)S(1)}, bf16[1024,4096]{1,0:T(8,128)(2,1)S(1)}) custom-call(bf16[8,3,192,128]{3,2,1,0:T(8,128)(2,1)S(1)} %all-to-all-done.own_ref, bf16[1024,4096]{1,0:T(8,128)(2,1)} %load_ref.2), custom_call_target="tpu_custom_call" | custom-call | flops 704643072 | bytes 4194304 | tf_op jit(solution)/shard_map/forward_own/pallas_call | solution.py:486
  32.4 0.0 copy-start.1
  32.4 0.0 copy-start.2
  32.4 0.0 copy-start.3
  32.4 0.0 copy-start.4
  32.4 0.0 copy-start.5
  32.5 0.0 collective-permute-done.other_ref
  32.5 0.0 slice-start.1
  32.5 4.7 %forward_other.1 = (bf16[6144,256]{1,0:T(8,128)(2,1)S(1)}, bf16[1536,128]{1,0:T(8,128)(2,1)S(1)}, f32[1536,128]{1,0:T(8,128)S(1)}, f32[1536,128]{1,0:T(8,128)S(1)}, bf16[4096,1024]{1,0:T(8,128)(2,1)S(1)}) custom-call(s32[3]{0:T(128)S(1)} %pad_add_fusion.facts_ref, bf16[8,3,192,128]{3,2,1,0:T(8,128)(2,1)S(1)} %all-to-all-done.own_ref, ...), custom_call_target="tpu_custom_call" | custom-call | flops 805306368 | bytes 4194304 | tf_op jit(solution)/shard_map/forward_other/pallas_call | solution.py:502
  37.2 14.0 %all_to_all.20.rows_ref = bf16[8,192,128]{2,1,0:T(8,128)(2,1)S(1)} all-to-all(bf16[8,192,128]{2,1,0:T(8,128)(2,1)S(1)} %bitcast.11), channel_id=1, replica_groups=mesh['seq_0'=4,'seq_1'=2,'seq_2'=2,'grp'=8] {'seq_0','seq_1'}, dimensions={0} | all-to-all | bytes 786432 | tf_op jit(solution)/shard_map/all_to_all | solution.py:388
  51.3 9.8 %byte_layer.1 = (bf16[8,192,128]{2,1,0:T(8,128)(2,1)S(1)}, f32[8,192]{1,0:T(8,128)S(1)}) custom-call(s32[3]{0:T(128)S(1)} %pad_add_fusion.facts_ref, bf16[8,192,128]{2,1,0:T(8,128)(2,1)S(1)} %all_to_all.20.rows_ref, s32[8,192]{1,0:T(8,128)S(1)} %bitcast.14, s32[1,192]{1,0:T(1,128)S(1)} %bitcast.16, bf16[256,1024]{1,0:T(8,128)(2,1)S(1)} %copy-done.1, ...), custom_call_target="tpu_custom_call" | custom-call | flops 6442450944 | bytes 4194304 | tf_op jit(solution)/shard_map/byte_layer/pallas_call | solution.py:522
  61.1 12.5 %all_to_all.21 = bf16[8,192,128]{2,1,0:T(8,128)(2,1)S(1)} all-to-all(bf16[8,192,128]{2,1,0:T(8,128)(2,1)S(1)} %get-tuple-element.52), channel_id=1, replica_groups=mesh['seq_0'=4,'seq_1'=2,'seq_2'=2,'grp'=8] {'seq_0','seq_1'}, dimensions={0} | all-to-all | bytes 786432 | tf_op jit(solution)/shard_map/all_to_all | solution.py:388
  73.7 4.0 %collective-permute-start.3 = (f32[8,192]{1,0:T(8,128)S(1)}, f32[8,192]{1,0:T(8,128)S(1)}, u32[]{:S(2)}, u32[]{:S(2)}) collective-permute-start(f32[8,192]{1,0:T(8,128)S(1)} %get-tuple-element.59), channel_id=1, source_target_pairs={{0,6},{1,7},{2,0},{3,1},{4,2},{5,3},{6,4},{7,5},{8,14},{9,15},{10,... | collective-permute-start | bytes 18440 | tf_op jit(solution)/shard_map/ppermute | solution.py:392
  77.7 1.3 %collective-permute-start.1 = (f32[8,192]{1,0:T(8,128)S(1)}, f32[8,192]{1,0:T(8,128)S(1)}, u32[]{:S(2)}, u32[]{:S(2)}) collective-permute-start(f32[8,192]{1,0:T(8,128)S(1)} %get-tuple-element.59), channel_id=1, source_target_pairs={{0,2},{1,3},{2,4},{3,5},{4,6},{5,7},{6,0},{7,1},{8,10},{9,11},{10,... | collective-permute-start | bytes 18440 | tf_op jit(solution)/shard_map/ppermute | solution.py:392
  79.0 4.2 %backward_other.1 = (bf16[8,2,192,128]{3,2,1,0:T(8,128)(2,1)S(1)}, f32[6,128,256]{2,1,0:T(8,128)S(1)}) custom-call(bf16[8,3,192,128]{3,2,1,0:T(8,128)(2,1)S(1)} %all-to-all-done.own_ref, bf16[8,2,192,128]{3,2,1,0:T(8,128)(2,1)S(1)} %collective-permute-done.other_ref, bf16[1536,128]{1,0:T(8,128)(2,1)S(1)} %get-tuple-element.45.mixed_ref, ...), custom_call_target="tpu_custom_call" | custom-call | flops 1610612736 | bytes 4194304 | tf_op jit(solution)/shard_map/backward_other/pallas_call | solution.py:549
  83.2 0.0 collective-permute-done.3
  83.2 0.0 collective-permute-done.1
  83.3 0.1 collective-permute-start.5
  83.4 0.7 collective-permute-start.4
  84.0 3.5 %backward_own.1 = (bf16[1536,128]{1,0:T(8,128)(2,1)S(1)}, f32[1536,128]{1,0:T(8,128)S(1)}, f32[1536,128]{1,0:T(8,128)S(1)}) custom-call(bf16[8,3,192,128]{3,2,1,0:T(8,128)(2,1)S(1)} %all-to-all-done.own_ref, bf16[1536,128]{1,0:T(8,128)(2,1)S(1)} %get-tuple-element.45.mixed_ref, f32[1536,128]{1,0:T(8,128)S(1)} %get-tuple-element.46.inverse_ref, ...), custom_call_target="tpu_custom_call" | custom-call | flops 1409286144 | bytes 4194304 | tf_op jit(solution)/shard_map/backward_own/pallas_call | solution.py:561
  87.5 0.0 collective-permute-done.4
  87.6 0.2 join.1
  87.8 22.1 %all_to_all.22.stack_ref = bf16[8,3,192,128]{3,2,1,0:T(8,128)(2,1)S(1)} all-to-all(bf16[8,3,192,128]{3,2,1,0:T(8,128)(2,1)S(1)} %join.1), channel_id=1, replica_groups=mesh['seq_0'=4,'seq_1'=2,'seq_2'=2,'grp'=8] {'seq_0','seq_1'}, dimensions={0} | all-to-all | bytes 2359296 | tf_op jit(solution)/shard_map/all_to_all | solution.py:388
  109.9 1.7 %unpack.1 = (bf16[192,1024]{1,0:T(8,128)(2,1)}, bf16[192,1024]{1,0:T(8,128)(2,1)}, bf16[192,1024]{1,0:T(8,128)(2,1)}, f32[8,24]{1,0:T(8,128)}) custom-call(s32[3]{0:T(128)S(1)} %pad_add_fusion.facts_ref, bf16[8,3,192,128]{3,2,1,0:T(8,128)(2,1)S(1)} %all_to_all.22.stack_ref, f32[8,192]{1,0:T(8,128)S(1)} %add.23.losses_ref), custom_call_target="tpu_custom_call" | custom-call | bytes 4194304 | tf_op jit(solution)/shard_map/unpack/pallas_call | solution.py:583
  (15 shorter events, 0.0 us)
Async XLA Ops:
  3.0 25.7 %all-to-all-start = ((bf16[8,3,192,128]{3,2,1,0:T(8,128)(2,1)}), bf16[8,3,192,128]{3,2,1,0:T(8,128)(2,1)S(1)}, u32[]{:S(2)}, u32[]{:S(2)}) async-start(bf16[8,3,192,128]{3,2,1,0:T(8,128)(2,1)} %pack.1), calls=%async_computation | async-start | bytes 2359296 | tf_op jit(solution)/shard_map/all_to_all | solution.py:388
  28.7 3.7 %collective-permute-start = (bf16[8,2,192,128]{3,2,1,0:T(8,128)(2,1)S(1)}, bf16[8,2,192,128]{3,2,1,0:T(8,128)(2,1)S(1)}, u32[]{:S(2)}, u32[]{:S(2)}) collective-permute-start(bf16[8,2,192,128]{3,2,1,0:T(8,128)(2,1)S(1)} %slice.3), channel_id=1, source_target_pairs={{0,8},{8,0},{1,9},{9,1},{2,10},{10,2},{3,11},{11,3},{4,12},{12,4},... | collective-permute-start | bytes 2359304 | tf_op jit(solution)/shard_map/ppermute | solution.py:401
  28.8 22.4 %slice-start = ((s8[8388608]{0:T(1024)(128)(4,1)}), s8[4194304]{0:T(1024)(128)(4,1)S(1)}, s32[]{:S(2)}) async-start(s8[8388608]{0:T(1024)(128)(4,1)} %bitcast.9), calls=%async_computation.4 | async-start | bytes 8388608
  28.8 22.4 %copy-start = (bf16[1024,4096]{1,0:T(8,128)(2,1)S(1)}, bf16[1024,4096]{1,0:T(8,128)(2,1)}, u32[]{:S(2)}) copy-start(bf16[1024,4096]{1,0:T(8,128)(2,1)} %get-tuple-element.51.down_turned_ref) | copy-start | bytes 25165828
  32.4 18.8 %copy-start.1 = (bf16[256,1024]{1,0:T(8,128)(2,1)S(1)}, bf16[256,1024]{1,0:T(8,128)(2,1)}, u32[]{:S(2)}) copy-start(bf16[256,1024]{1,0:T(8,128)(2,1)} %embed_ref.1) | copy-start | bytes 1572868
  32.4 18.8 %copy-start.2 = (bf16[1024,256]{1,0:T(8,128)(2,1)S(1)}, bf16[1024,256]{1,0:T(8,128)(2,1)}, u32[]{:S(2)}) copy-start(bf16[1024,256]{1,0:T(8,128)(2,1)} %vocab_ref.1) | copy-start | bytes 1572868
  32.4 18.8 %copy-start.3 = (s32[192,8]{0,1:T(8,128)S(1)}, s32[192,8]{0,1:T(8,128)}, u32[]{:S(2)}) copy-start(s32[192,8]{0,1:T(8,128)} %param.10) | copy-start | bytes 18436
  32.4 18.8 %copy-start.4 = (f32[1024]{0:T(1024)S(1)}, f32[1024]{0:T(1024)}, u32[]{:S(2)}) copy-start(f32[1024]{0:T(1024)} %param.16) | copy-start | bytes 12292
  32.4 18.8 %copy-start.5 = (s32[192]{0:T(256)S(1)}, s32[192]{0:T(256)}, u32[]{:S(2)}) copy-start(s32[192]{0:T(256)} %param.11) | copy-start | bytes 2308
  32.5 18.8 %slice-start.1 = ((s8[8388608]{0:T(1024)(128)(4,1)}), s8[4194304]{0:T(1024)(128)(4,1)S(1)}, s32[]{:S(2)}) async-start(s8[8388608]{0:T(1024)(128)(4,1)} %bitcast.9), calls=%async_computation.5 | async-start | bytes 8388608
  73.7 9.6 %collective-permute-start.3 = (f32[8,192]{1,0:T(8,128)S(1)}, f32[8,192]{1,0:T(8,128)S(1)}, u32[]{:S(2)}, u32[]{:S(2)}) collective-permute-start(f32[8,192]{1,0:T(8,128)S(1)} %get-tuple-element.59), channel_id=1, source_target_pairs={{0,6},{1,7},{2,0},{3,1},{4,2},{5,3},{6,4},{7,5},{8,14},{9,15},{10,... | collective-permute-start | bytes 18440 | tf_op jit(solution)/shard_map/ppermute | solution.py:392
  77.7 5.5 %collective-permute-start.2 = (f32[8,192]{1,0:T(8,128)S(1)}, f32[8,192]{1,0:T(8,128)S(1)}, u32[]{:S(2)}, u32[]{:S(2)}) collective-permute-start(f32[8,192]{1,0:T(8,128)S(1)} %get-tuple-element.59), channel_id=1, source_target_pairs={{0,4},{1,5},{2,6},{3,7},{4,0},{5,1},{6,2},{7,3},{8,12},{9,13},{10,... | collective-permute-start | bytes 18440 | tf_op jit(solution)/shard_map/ppermute | solution.py:392
  77.7 5.5 %collective-permute-start.1 = (f32[8,192]{1,0:T(8,128)S(1)}, f32[8,192]{1,0:T(8,128)S(1)}, u32[]{:S(2)}, u32[]{:S(2)}) collective-permute-start(f32[8,192]{1,0:T(8,128)S(1)} %get-tuple-element.59), channel_id=1, source_target_pairs={{0,2},{1,3},{2,4},{3,5},{4,6},{5,7},{6,0},{7,1},{8,10},{9,11},{10,... | collective-permute-start | bytes 18440 | tf_op jit(solution)/shard_map/ppermute | solution.py:392
  83.3 4.3 %collective-permute-start.5 = (bf16[8,2,192,128]{3,2,1,0:T(8,128)(2,1)S(1)}, bf16[8,2,192,128]{3,2,1,0:T(8,128)(2,1)S(1)}, u32[]{:S(2)}, u32[]{:S(2)}) collective-permute-start(bf16[8,2,192,128]{3,2,1,0:T(8,128)(2,1)S(1)} %get-tuple-element.66), channel_id=1, source_target_pairs={{0,8},{8,0},{1,9},{9,1},{2,10},{10,2},{3,11},{11,3},{4,12},{12,4},... | collective-permute-start | bytes 2359304 | tf_op jit(solution)/shard_map/ppermute | solution.py:401
  83.4 4.2 %collective-permute-start.4 = (f32[8,192]{1,0:T(8,128)S(1)}, f32[8,192]{1,0:T(8,128)S(1)}, u32[]{:S(2)}, u32[]{:S(2)}) collective-permute-start(f32[8,192]{1,0:T(8,128)S(1)} %add_add_fusion), channel_id=1, source_target_pairs={{0,1},{1,0},{2,3},{3,2},{4,5},{5,4},{6,7},{7,6},{8,9},{9,8},{10,11... | collective-permute-start | bytes 18440 | tf_op jit(solution)/shard_map/ppermute | solution.py:397

commit v6 on v5

--- a/solution.py
+++ b/solution.py
@@ -86,10 +86,11 @@
 
 def piece_scores(queries, first, pieces, key_s, score_s, core):
     top = None
+    turned = queries.T
     for at, size, kind in pieces:
         if kind == "none":
             continue
-        score = dot(key_s[pl.ds(at, size)], queries, NT)
+        score = dot(key_s[pl.ds(at, size)], turned)
         if kind == "causal":
             key_at = lax.broadcasted_iota(jnp.int32, score.shape, 0)
             query_at = lax.broadcasted_iota(jnp.int32, score.shape, 1)
@@ -117,18 +118,39 @@
     return total
 
 
+def staggered(count, start, middle, end):
+    start(0)
+    for i in range(count):
+        if i + 1 < count:
+            start(i + 1)
+        if i > 0:
+            end(i - 1)
+        middle(i)
+    end(count - 1)
+
+
 def forward_own(plan, own_ref, load_ref, kept_ref, mixed_ref, stats_ref, loaded_ref, key_s, turned_s, score_s, sem):
     load = pltpu.make_async_copy(load_ref, loaded_ref, sem)
     load.start()
     flat_rows(own_ref, 1, key_s)
     turned_rows(own_ref, 2, turned_s)
-    for i, (first, base, keys, pieces) in enumerate(plan):
-        top = piece_scores(query_chunk(own_ref, first), first, pieces, key_s, score_s, None)
-        shift = top * (SCALE * LOG2E)
-        total = piece_chances(shift, base, pieces, score_s, kept_ref)
+    tops = {}
+
+    def start(i):
+        first, _, _, pieces = plan[i]
+        tops[i] = piece_scores(query_chunk(own_ref, first), first, pieces, key_s, score_s.at[i % 2], None)
+
+    def middle(i):
+        _, base, _, pieces = plan[i]
+        shift = tops[i] * (SCALE * LOG2E)
+        stats_ref[i, 0:1] = shift
+        stats_ref[i, 1:2] = piece_chances(shift, base, pieces, score_s.at[i % 2], kept_ref)
+
+    def end(i):
+        _, base, keys, _ = plan[i]
         mixed_ref[i] = dot(turned_s[:, :keys], kept_ref[pl.ds(base, keys)])
-        stats_ref[i, 0:1] = shift
-        stats_ref[i, 1:2] = total
+
+    staggered(len(plan), start, middle, end)
     load.wait()
 
 
@@ -155,19 +177,31 @@
     flat_rows(other_ref, 0, key_s)
     turned_rows(other_ref, 1, turned_s)
     core = facts_ref[2]
-    for i, (first, base, keys, pieces) in enumerate(plan):
-        top = piece_scores(query_chunk(own_ref, first), first, pieces, key_s, score_s, core)
+    tops = {}
+    parts = {}
+
+    def start(i):
+        first, _, _, pieces = plan[i]
+        tops[i] = piece_scores(query_chunk(own_ref, first), first, pieces, key_s, score_s.at[i % 2], core)
+
+    def middle(i):
+        _, base, _, pieces = plan[i]
         own_shift = stats_ref[i, 0:1]
-        shift = jnp.maximum(top * (SCALE * LOG2E), own_shift)
-        total = piece_chances(shift, base, pieces, score_s, kept_ref)
+        shift = jnp.maximum(tops[i] * (SCALE * LOG2E), own_shift)
+        total = piece_chances(shift, base, pieces, score_s.at[i % 2], kept_ref)
         own_part = jnp.exp2(own_shift - shift)
-        total = total + own_part * stats_ref[i, 1:2]
+        parts[i] = own_part, 1.0 / (total + own_part * stats_ref[i, 1:2])
+
+    def end(i):
+        first, base, keys, _ = plan[i]
+        own_part, inverse = parts[i]
         mixed = mixed_ref[i] * own_part + dot(turned_s[:, :keys], kept_ref[pl.ds(base, keys)])
-        inverse = 1.0 / total
         rows = pl.ds(first, WIDE)
         out_ref[rows] = (mixed * inverse).T.astype(BF16)
         inverse_ref[rows] = jnp.broadcast_to(inverse, (HEAD, WIDE)).T
         own_inverse_ref[rows] = jnp.broadcast_to(own_part * inverse, (HEAD, WIDE)).T
+
+    staggered(len(plan), start, middle, end)
     load.wait()
 
 
@@ -177,32 +211,46 @@
 ):
     flat_rows(side_ref, key_at + 1, value_s)
     turned_rows(side_ref, key_at, turned_s)
-    reached = 0
+    tasks = []
     for i, (first, base, keys, pieces) in enumerate(plan):
-        queries = query_chunk(own_ref, first)
         rows = pl.ds(first, WIDE)
         grads = (grad_ref[rows].astype(F32) * inverse_ref[rows]).astype(BF16)
         product = grads.astype(F32) * mixed_ref[rows].astype(F32)
         row_dot = jnp.sum(product.T, axis=0, keepdims=True)
-        for at, size, kind in pieces:
-            spot = pl.ds(at, size)
-            if kind == "none":
-                slope_s[spot] = jnp.zeros((size, WIDE), BF16)
-                continue
-            kept = kept_ref[pl.ds(base + at, size)]
-            chance_grad = dot(value_s[spot], grads, NT)
-            slope = (kept.astype(F32) * (chance_grad - row_dot)).astype(BF16)
-            slope_s[spot] = slope
-            value_part = dot(kept, grads)
-            key_part = dot(slope, queries)
-            if at >= reached:
-                reached = at + size
-                value_sum[spot] = value_part
-                key_sum[spot] = key_part
-            else:
-                value_sum[spot] += value_part
-                key_sum[spot] += key_part
-        yield i, dot(turned_s[:, :keys], slope_s[pl.ds(0, keys)])
+        queries = query_chunk(own_ref, first)
+        live = [piece for piece in pieces if piece[2] != "none"]
+        for at, size, _ in live:
+            tasks.append((i, at, size, at == live[-1][0], queries, grads, row_dot))
+
+    def chance_grad(task):
+        _, at, size, _, _, grads, _ = task
+        return dot(value_s[pl.ds(at, size)], grads, NT)
+
+    reached = 0
+    ahead = chance_grad(tasks[0])
+    for k, (i, at, size, last, queries, grads, row_dot) in enumerate(tasks):
+        here = ahead
+        if k + 1 < len(tasks):
+            ahead = chance_grad(tasks[k + 1])
+        _, base, keys, _ = plan[i]
+        spot = pl.ds(at, size)
+        kept = kept_ref[pl.ds(base + at, size)]
+        slope = (kept.astype(F32) * (here - row_dot)).astype(BF16)
+        slope_s[i % 2, spot] = slope
+        value_part = dot(kept, grads)
+        key_part = dot(slope, queries)
+        if at >= reached:
+            reached = at + size
+            value_sum[spot] = value_part
+            key_sum[spot] = key_part
+        else:
+            value_sum[spot] += value_part
+            key_sum[spot] += key_part
+        if last:
+            for unseen, size, kind in plan[i][3]:
+                if kind == "none":
+                    slope_s[i % 2, pl.ds(unseen, size)] = jnp.zeros((size, WIDE), BF16)
+            yield i, dot(turned_s[:, :keys], slope_s[i % 2, pl.ds(0, keys)])
 
 
 def backward_other(
@@ -318,9 +366,12 @@
     gain = gain_ref[...]
     normed = (hidden_in * inverse_rms * gain).astype(BF16)
     after = hidden_in
+    ahead = dot(normed, up_ref[:, :size])
     for i in range(pieces):
         part = pl.ds(i * size, size)
-        raised = dot(normed, up_ref[:, part])
+        raised = ahead
+        if i + 1 < pieces:
+            ahead = dot(normed, up_ref[:, pl.ds((i + 1) * size, size)])
         square = raised * raised
         half = 0.5 + 0.5 * jnp.tanh(raised * (GELU_A + (GELU_A * GELU_B) * square))
         active = (raised * half).astype(BF16)
@@ -347,9 +398,12 @@
     after_grad = final_scale * final_grad - after * (final_scale * final_scale * final_scale * mean_dot)
     narrow = after_grad.astype(BF16)
     normed_grad = None
+    ahead = dot(narrow, down_turned_ref[:, :size])
     for i in range(pieces):
         part = pl.ds(i * size, size)
-        active_grad = dot(narrow, down_turned_ref[:, part]).astype(BF16).astype(F32)
+        active_grad = ahead.astype(BF16).astype(F32)
+        if i + 1 < pieces:
+            ahead = dot(narrow, down_turned_ref[:, pl.ds((i + 1) * size, size)])
         raised_grad = (active_grad * bend_s[:, part]).astype(BF16)
         term = dot(raised_grad, up_turned_ref[part])
         normed_grad = term if normed_grad is None else normed_grad + term
@@ -388,13 +442,8 @@
     return lax.all_to_all(value, CHIPS, split_axis=0, concat_axis=0, tiled=True)
 
 
-def gather_losses(value, steps):
-    found = [lax.ppermute(value, "grp", [(i, (i + k) % PATCH) for i in range(PATCH)]) for k in steps]
-    return functools.reduce(jnp.add, found, value)
-
-
-def pair_losses(value):
-    return value + lax.ppermute(value, "grp", [(i, i ^ 1) for i in range(PATCH)])
+def gather_losses(value, bit):
+    return value + lax.ppermute(value, "grp", [(i, i ^ (1 << bit)) for i in range(PATCH)])
 
 
 def swap_cores(value):
@@ -494,7 +543,7 @@
         ),
         [vmem(), far()],
         (vmem(),) * 4,
-        kv_scratch + [pltpu.VMEM((rows, WIDE), F32), pltpu.SemaphoreType.DMA],
+        kv_scratch + [pltpu.VMEM((2, rows, WIDE), F32), pltpu.SemaphoreType.DMA],
         8,
         4 * near_rows * WIDE * HEAD,
         near_rows * WIDE,
@@ -511,7 +560,7 @@
         ),
         [smem()] + [vmem()] * 4 + [far()],
         (vmem(),) * 5,
-        kv_scratch + [pltpu.VMEM((rows, WIDE), F32), pltpu.SemaphoreType.DMA],
+        kv_scratch + [pltpu.VMEM((2, rows, WIDE), F32), pltpu.SemaphoreType.DMA],
         8,
         4 * far_rows * WIDE * HEAD,
         far_rows * WIDE,
@@ -542,9 +591,8 @@
         vocab_head,
     )
 
-    grad_rows, losses = lax.optimization_barrier((exchange(context_grad), losses))
-    grad_rows = grad_rows.reshape(rows, HEAD)
-    side_scratch = kv_scratch + [pltpu.VMEM((rows, WIDE), BF16)]
+    grad_rows = exchange(context_grad).reshape(rows, HEAD)
+    side_scratch = kv_scratch + [pltpu.VMEM((2, rows, WIDE), BF16)]
     sums = [pltpu.VMEM((rows, HEAD), F32)] * 2
     pair_grad, turned_grad = kernel_call(
         functools.partial(backward_other, far_plan),
@@ -556,7 +604,6 @@
         8,
         8 * far_rows * WIDE * HEAD,
     )(own, other, attended, far_inverse, far_kept, grad_rows)
-    pair_grad, turned_grad, losses = lax.optimization_barrier((pair_grad, turned_grad, gather_losses(losses, (2, 4, 6))))
     pair_sent = swap_cores(pair_grad)
     query_grad, key_grad, value_grad = kernel_call(
         functools.partial(backward_own, near_plan),
@@ -568,7 +615,6 @@
         8,
         8 * near_rows * WIDE * HEAD,
     )(own, attended, near_inverse, near_kept, grad_rows, turned_grad)
-    query_grad, losses = lax.optimization_barrier((query_grad, pair_losses(losses)))
     joined = kernel_call(
         join_kernel,
         "join",
@@ -579,7 +625,10 @@
         4,
         0,
     )(query_grad, key_grad, value_grad, pair_sent)
+    joined, losses = lax.optimization_barrier((joined, losses))
     back = exchange(joined)
+    for bit in (1, 2, 0):
+        losses = gather_losses(losses, bit)
     query_out, key_out, value_out, byte_loss = kernel_call(
         unpack_kernel,
         "unpack",

time: 112 us -> 107 us (0.955)
  blocking collectives: 48.6 us -> 26.5 us
  waiting for transfers between devices: 4.4 us -> 17.4 us
  starting transfers between devices: 13.2 us -> 17.5 us
    all_to_all x3 -> x2, blocking collectives: 48.6 us -> 26.5 us  [exchange(): return lax.all_to_all(value, CHIPS, split_axis=0, concat_axis=0, tiled=True)]
    ppermute x4 -> x3, waiting for transfers between devices: 0.01 us -> 8.41 us  [gather_losses(): lax.ppermute(value, 'grp', [(i, i ^ 1 << bit) for i in range(PATCH)])]
    all_to_all x1 -> x2, waiting for transfers between devices: 4.38 us -> 8.98 us  [exchange(): return lax.all_to_all(value, CHIPS, split_axis=0, concat_axis=0, tiled=True)]
    all_to_all x1 -> x2, starting transfers between devices: 7.03 us -> 10.6 us  [exchange(): return lax.all_to_all(value, CHIPS, split_axis=0, concat_axis=0, tiled=True)]
    pallas_call x1, Pallas kernels: 4.25 us -> 3.13 us  [shards(): kernel_call(functools.partial(backward_other, far_plan), 'backward_other'...]
    ppermute x4 -> x3, starting transfers between devices: 5.97 us -> 6.5 us  [gather_losses(): lax.ppermute(value, 'grp', [(i, i ^ 1 << bit) for i in range(PATCH)])]
  transfers between devices with their start and end apart: 7 -> 7, of which waited for: 1 -> 5; matrix products, arithmetic and copies ran while one was open for 0% -> 0% of each run, Pallas kernels for 23% -> 19%
where the time goes in v6:
time: 107 us; the launch traced here: 106 us
  Pallas kernels  43.8 us (41%)
  blocking collectives  26.5 us (25%)
  starting transfers between devices  17.5 us (16%)
  waiting for transfers between devices  17.4 us (16%)
    all_to_all x2, blocking collectives, exchange(): return lax.all_to_all(value, CHIPS, split_axis=0, concat_axis=0, tiled=True)  26.5 us
    pallas_call x1, Pallas kernels, shards(): pl.pallas_call(turn_kernel, out_shape=(pltpu.HBM((hidden, columns), BF16)...  14.3 us
    all_to_all x2, starting transfers between devices, exchange(): return lax.all_to_all(value, CHIPS, split_axis=0, concat_axis=0, tiled=True)  10.6 us
    pallas_call x1, Pallas kernels, shards(): kernel_call(functools.partial(byte_kernel, byte_pieces), 'byte_layer', (s...  9.86 us
    all_to_all x2, waiting for transfers between devices, exchange(): return lax.all_to_all(value, CHIPS, split_axis=0, concat_axis=0, tiled=True)  8.98 us
    ppermute x3, waiting for transfers between devices, gather_losses(): lax.ppermute(value, 'grp', [(i, i ^ 1 << bit) for i in range(PATCH)])  8.41 us
    ppermute x3, starting transfers between devices, gather_losses(): lax.ppermute(value, 'grp', [(i, i ^ 1 << bit) for i in range(PATCH)])  6.5 us
    pallas_call x1, Pallas kernels, shards(): kernel_call(functools.partial(forward_other, far_plan), 'forward_other',...  4.73 us
  transfers between devices with their start and end apart: 7, of which 5 were waited for; matrix products, arithmetic and copies ran while one was open for 0% of the time, Pallas kernels for 19%

profile of v6, /device:TPU:0, one launch (start us, length us, event | category | flops | bytes accessed | tf_op | source)
XLA Modules:
  0.0 106.4 jit_solution(6542473511663169441)
XLA Ops:
  0.6 0.1 pad_add_fusion.facts_ref
  0.7 2.3 %pack.1 = bf16[8,3,192,128]{3,2,1,0:T(8,128)(2,1)} custom-call(bf16[192,1024]{1,0:T(8,128)(2,1)} %refs_0_, bf16[192,1024]{1,0:T(8,128)(2,1)} %refs_1_.1, bf16[192,1024]{1,0:T(8,128)(2,1)} %refs_2_.1), custom_call_target="tpu_custom_call" | custom-call | bytes 4194304 | tf_op jit(solution)/shard_map/pack/pallas_call | solution.py:500
  3.0 7.0 %all-to-all-start = ((bf16[8,3,192,128]{3,2,1,0:T(8,128)(2,1)}), bf16[8,3,192,128]{3,2,1,0:T(8,128)(2,1)S(1)}, u32[]{:S(2)}, u32[]{:S(2)}) async-start(bf16[8,3,192,128]{3,2,1,0:T(8,128)(2,1)} %pack.1), calls=%async_computation | async-start | bytes 2359296 | tf_op jit(solution)/shard_map/all_to_all | solution.py:442
  10.0 14.3 %turn_weights.1 = (bf16[4096,1024]{1,0:T(8,128)(2,1)}, bf16[1024,4096]{1,0:T(8,128)(2,1)}) custom-call(bf16[1024,4096]{1,0:T(8,128)(2,1)} %load_ref.2, bf16[4096,1024]{1,0:T(8,128)(2,1)} %load_ref.3), custom_call_target="tpu_custom_call" | custom-call | bytes 33554432 | tf_op jit(solution)/shard_map/turn_weights/pallas_call | solution.py:521
  24.4 4.3 %all-to-all-done.own_ref = bf16[8,3,192,128]{3,2,1,0:T(8,128)(2,1)S(1)} async-done(((bf16[8,3,192,128]{3,2,1,0:T(8,128)(2,1)}), bf16[8,3,192,128]{3,2,1,0:T(8,128)(2,1)S(1)}, u32[]{:S(2)}, u32[]{:S(2)}) %all-to-all-start) | async-done | bytes 1179680 | tf_op jit(solution)/shard_map/all_to_all | solution.py:442
  28.7 0.1 slice.3
  28.7 0.1 collective-permute-start
  28.9 3.5 %forward_own.1 = (bf16[5376,256]{1,0:T(8,128)(2,1)S(1)}, f32[6,128,256]{2,1,0:T(8,128)S(1)}, f32[6,8,256]{2,1,0:T(8,128)S(1)}, bf16[1024,4096]{1,0:T(8,128)(2,1)S(1)}) custom-call(bf16[8,3,192,128]{3,2,1,0:T(8,128)(2,1)S(1)} %all-to-all-done.own_ref, bf16[1024,4096]{1,0:T(8,128)(2,1)} %load_ref.2), custom_call_target="tpu_custom_call" | custom-call | flops 704643072 | bytes 4194304 | tf_op jit(solution)/shard_map/forward_own/pallas_call | solution.py:535
  32.4 0.0 copy-start.1
  32.4 0.0 copy-start.2
  32.4 0.0 copy-start.3
  32.4 0.0 copy-start.4
  32.5 0.0 copy-start.5
  32.5 0.0 collective-permute-done.other_ref
  32.5 4.7 %forward_other.1 = (bf16[6144,256]{1,0:T(8,128)(2,1)S(1)}, bf16[1536,128]{1,0:T(8,128)(2,1)S(1)}, f32[1536,128]{1,0:T(8,128)S(1)}, f32[1536,128]{1,0:T(8,128)S(1)}, bf16[4096,1024]{1,0:T(8,128)(2,1)S(1)}) custom-call(s32[3]{0:T(128)S(1)} %pad_add_fusion.facts_ref, bf16[8,3,192,128]{3,2,1,0:T(8,128)(2,1)S(1)} %all-to-all-done.own_ref, ...), custom_call_target="tpu_custom_call" | custom-call | flops 805306368 | bytes 4194304 | tf_op jit(solution)/shard_map/forward_other/pallas_call | solution.py:551
  37.2 14.0 %all_to_all.20.rows_ref = bf16[8,192,128]{2,1,0:T(8,128)(2,1)S(1)} all-to-all(bf16[8,192,128]{2,1,0:T(8,128)(2,1)S(1)} %bitcast.11), channel_id=1, replica_groups=mesh['seq_0'=4,'seq_1'=2,'seq_2'=2,'grp'=8] {'seq_0','seq_1'}, dimensions={0} | all-to-all | bytes 786432 | tf_op jit(solution)/shard_map/all_to_all | solution.py:442
  51.3 9.9 %byte_layer.1 = (bf16[8,192,128]{2,1,0:T(8,128)(2,1)S(1)}, f32[8,192]{1,0:T(8,128)S(1)}) custom-call(s32[3]{0:T(128)S(1)} %pad_add_fusion.facts_ref, bf16[8,192,128]{2,1,0:T(8,128)(2,1)S(1)} %all_to_all.20.rows_ref, s32[8,192]{1,0:T(8,128)S(1)} %bitcast.14, s32[1,192]{1,0:T(1,128)S(1)} %bitcast.16, bf16[256,1024]{1,0:T(8,128)(2,1)S(1)} %copy-done.1, ...), custom_call_target="tpu_custom_call" | custom-call | flops 6442450944 | bytes 4194304 | tf_op jit(solution)/shard_map/byte_layer/pallas_call | solution.py:571
  61.2 12.5 %all_to_all.21 = bf16[8,192,128]{2,1,0:T(8,128)(2,1)S(1)} all-to-all(bf16[8,192,128]{2,1,0:T(8,128)(2,1)S(1)} %get-tuple-element.47), channel_id=1, replica_groups=mesh['seq_0'=4,'seq_1'=2,'seq_2'=2,'grp'=8] {'seq_0','seq_1'}, dimensions={0} | all-to-all | bytes 786432 | tf_op jit(solution)/shard_map/all_to_all | solution.py:442
  73.7 3.1 %backward_other.1 = (bf16[8,2,192,128]{3,2,1,0:T(8,128)(2,1)S(1)}, f32[6,128,256]{2,1,0:T(8,128)S(1)}) custom-call(bf16[8,3,192,128]{3,2,1,0:T(8,128)(2,1)S(1)} %all-to-all-done.own_ref, bf16[8,2,192,128]{3,2,1,0:T(8,128)(2,1)S(1)} %collective-permute-done.other_ref, bf16[1536,128]{1,0:T(8,128)(2,1)S(1)} %get-tuple-element.40.mixed_ref, ...), custom_call_target="tpu_custom_call" | custom-call | flops 1610612736 | bytes 4194304 | tf_op jit(solution)/shard_map/backward_other/pallas_call | solution.py:597
  76.8 0.3 collective-permute-start.1
  77.1 2.9 %backward_own.1 = (bf16[1536,128]{1,0:T(8,128)(2,1)S(1)}, f32[1536,128]{1,0:T(8,128)S(1)}, f32[1536,128]{1,0:T(8,128)S(1)}) custom-call(bf16[8,3,192,128]{3,2,1,0:T(8,128)(2,1)S(1)} %all-to-all-done.own_ref, bf16[1536,128]{1,0:T(8,128)(2,1)S(1)} %get-tuple-element.40.mixed_ref, f32[1536,128]{1,0:T(8,128)S(1)} %get-tuple-element.41.inverse_ref, ...), custom_call_target="tpu_custom_call" | custom-call | flops 1409286144 | bytes 4194304 | tf_op jit(solution)/shard_map/backward_own/pallas_call | solution.py:608
  80.0 0.0 collective-permute-done.1.pair_ref
  80.0 1.3 %join.1 = bf16[8,3,192,128]{3,2,1,0:T(8,128)(2,1)} custom-call(bf16[1536,128]{1,0:T(8,128)(2,1)S(1)} %get-tuple-element.51.query_ref, f32[1536,128]{1,0:T(8,128)S(1)} %get-tuple-element.52.key_ref, f32[1536,128]{1,0:T(8,128)S(1)} %get-tuple-element.53.value_ref, bf16[8,2,192,128]{3,2,1,0:T(8,128)(2,1)S(1)} %collective-permute-done.1.pair_ref), custom_call_target="tpu_custom_call" | custom-call | bytes 4194304 | tf_op jit(solution)/shard_map/join/pallas_call | solution.py:618
  81.3 3.6 %all-to-all-start.3 = ((bf16[8,3,192,128]{3,2,1,0:T(8,128)(2,1)}), bf16[8,3,192,128]{3,2,1,0:T(8,128)(2,1)S(1)}, u32[]{:S(2)}, u32[]{:S(2)}) async-start(bf16[8,3,192,128]{3,2,1,0:T(8,128)(2,1)} %join.1), calls=%async_computation.3 | async-start | bytes 2359296 | tf_op jit(solution)/shard_map/all_to_all | solution.py:442
  84.9 2.0 %collective-permute-start.2 = (f32[8,192]{1,0:T(8,128)S(1)}, f32[8,192]{1,0:T(8,128)S(1)}, u32[]{:S(2)}, u32[]{:S(2)}) collective-permute-start(f32[8,192]{1,0:T(8,128)S(1)} %get-tuple-element.57), channel_id=1, source_target_pairs={{0,2},{1,3},{2,0},{3,1},{4,6},{5,7},{6,4},{7,5},{8,10},{9,11},{10,... | collective-permute-start | bytes 18440 | tf_op jit(solution)/shard_map/ppermute | solution.py:446
  86.9 1.7 %collective-permute-done.2 = f32[8,192]{1,0:T(8,128)S(1)} collective-permute-done((f32[8,192]{1,0:T(8,128)S(1)}, f32[8,192]{1,0:T(8,128)S(1)}, u32[]{:S(2)}, u32[]{:S(2)}) %collective-permute-start.2) | collective-permute-done | bytes 6176 | tf_op jit(solution)/shard_map/ppermute | solution.py:446
  88.6 3.9 %collective-permute-start.3 = (f32[8,192]{1,0:T(8,128)S(1)}, f32[8,192]{1,0:T(8,128)S(1)}, u32[]{:S(2)}, u32[]{:S(2)}) collective-permute-start(f32[8,192]{1,0:T(8,128)S(1)} %add.17), channel_id=1, source_target_pairs={{0,4},{1,5},{2,6},{3,7},{4,0},{5,1},{6,2},{7,3},{8,12},{9,13},{10,... | collective-permute-start | bytes 18440 | tf_op jit(solution)/shard_map/ppermute | solution.py:446
  92.5 1.6 %collective-permute-done.3 = f32[8,192]{1,0:T(8,128)S(1)} collective-permute-done((f32[8,192]{1,0:T(8,128)S(1)}, f32[8,192]{1,0:T(8,128)S(1)}, u32[]{:S(2)}, u32[]{:S(2)}) %collective-permute-start.3) | collective-permute-done | bytes 6176 | tf_op jit(solution)/shard_map/ppermute | solution.py:446
  94.1 0.6 collective-permute-start.4
  94.7 5.1 %collective-permute-done.4 = f32[8,192]{1,0:T(8,128)S(1)} collective-permute-done((f32[8,192]{1,0:T(8,128)S(1)}, f32[8,192]{1,0:T(8,128)S(1)}, u32[]{:S(2)}, u32[]{:S(2)}) %collective-permute-start.4) | collective-permute-done | bytes 6176 | tf_op jit(solution)/shard_map/ppermute | solution.py:446
  99.8 4.6 %all-to-all-done.3.stack_ref = bf16[8,3,192,128]{3,2,1,0:T(8,128)(2,1)S(1)} async-done(((bf16[8,3,192,128]{3,2,1,0:T(8,128)(2,1)}), bf16[8,3,192,128]{3,2,1,0:T(8,128)(2,1)S(1)}, u32[]{:S(2)}, u32[]{:S(2)}) %all-to-all-start.3) | async-done | bytes 1179680 | tf_op jit(solution)/shard_map/all_to_all | solution.py:442
  104.4 1.7 %unpack.1 = (bf16[192,1024]{1,0:T(8,128)(2,1)}, bf16[192,1024]{1,0:T(8,128)(2,1)}, bf16[192,1024]{1,0:T(8,128)(2,1)}, f32[8,24]{1,0:T(8,128)}) custom-call(s32[3]{0:T(128)S(1)} %pad_add_fusion.facts_ref, bf16[8,3,192,128]{3,2,1,0:T(8,128)(2,1)S(1)} %all-to-all-done.3.stack_ref, f32[8,192]{1,0:T(8,128)S(1)} %add.19.losses_ref), custom_call_target="tpu_custom_call" | custom-call | bytes 4194304 | tf_op jit(solution)/shard_map/unpack/pallas_call | solution.py:632
  (15 shorter events, 0.0 us)
Async XLA Ops:
  3.0 25.7 %all-to-all-start = ((bf16[8,3,192,128]{3,2,1,0:T(8,128)(2,1)}), bf16[8,3,192,128]{3,2,1,0:T(8,128)(2,1)S(1)}, u32[]{:S(2)}, u32[]{:S(2)}) async-start(bf16[8,3,192,128]{3,2,1,0:T(8,128)(2,1)} %pack.1), calls=%async_computation | async-start | bytes 2359296 | tf_op jit(solution)/shard_map/all_to_all | solution.py:442
  28.7 3.7 %collective-permute-start = (bf16[8,2,192,128]{3,2,1,0:T(8,128)(2,1)S(1)}, bf16[8,2,192,128]{3,2,1,0:T(8,128)(2,1)S(1)}, u32[]{:S(2)}, u32[]{:S(2)}) collective-permute-start(bf16[8,2,192,128]{3,2,1,0:T(8,128)(2,1)S(1)} %slice.3), channel_id=1, source_target_pairs={{0,8},{8,0},{1,9},{9,1},{2,10},{10,2},{3,11},{11,3},{4,12},{12,4},... | collective-permute-start | bytes 2359304 | tf_op jit(solution)/shard_map/ppermute | solution.py:450
  28.8 22.4 %slice-start = ((s8[8388608]{0:T(1024)(128)(4,1)}), s8[4194304]{0:T(1024)(128)(4,1)S(1)}, s32[]{:S(2)}) async-start(s8[8388608]{0:T(1024)(128)(4,1)} %bitcast.9), calls=%async_computation.4 | async-start | bytes 8388608
  28.8 22.4 %copy-start = (bf16[1024,4096]{1,0:T(8,128)(2,1)S(1)}, bf16[1024,4096]{1,0:T(8,128)(2,1)}, u32[]{:S(2)}) copy-start(bf16[1024,4096]{1,0:T(8,128)(2,1)} %get-tuple-element.46.down_turned_ref) | copy-start | bytes 25165828
  32.4 18.8 %copy-start.1 = (bf16[256,1024]{1,0:T(8,128)(2,1)S(1)}, bf16[256,1024]{1,0:T(8,128)(2,1)}, u32[]{:S(2)}) copy-start(bf16[256,1024]{1,0:T(8,128)(2,1)} %embed_ref.1) | copy-start | bytes 1572868
  32.4 18.8 %copy-start.2 = (bf16[1024,256]{1,0:T(8,128)(2,1)S(1)}, bf16[1024,256]{1,0:T(8,128)(2,1)}, u32[]{:S(2)}) copy-start(bf16[1024,256]{1,0:T(8,128)(2,1)} %vocab_ref.1) | copy-start | bytes 1572868
  32.4 18.8 %copy-start.3 = (s32[192,8]{0,1:T(8,128)S(1)}, s32[192,8]{0,1:T(8,128)}, u32[]{:S(2)}) copy-start(s32[192,8]{0,1:T(8,128)} %param.10) | copy-start | bytes 18436
  32.4 18.8 %copy-start.4 = (f32[1024]{0:T(1024)S(1)}, f32[1024]{0:T(1024)}, u32[]{:S(2)}) copy-start(f32[1024]{0:T(1024)} %param.16) | copy-start | bytes 12292
  32.5 18.8 %copy-start.5 = (s32[192]{0:T(256)S(1)}, s32[192]{0:T(256)}, u32[]{:S(2)}) copy-start(s32[192]{0:T(256)} %param.11) | copy-start | bytes 2308
  32.5 18.8 %slice-start.1 = ((s8[8388608]{0:T(1024)(128)(4,1)}), s8[4194304]{0:T(1024)(128)(4,1)S(1)}, s32[]{:S(2)}) async-start(s8[8388608]{0:T(1024)(128)(4,1)} %bitcast.9), calls=%async_computation.5 | async-start | bytes 8388608
  76.8 3.2 %collective-permute-start.1 = (bf16[8,2,192,128]{3,2,1,0:T(8,128)(2,1)S(1)}, bf16[8,2,192,128]{3,2,1,0:T(8,128)(2,1)S(1)}, u32[]{:S(2)}, u32[]{:S(2)}) collective-permute-start(bf16[8,2,192,128]{3,2,1,0:T(8,128)(2,1)S(1)} %get-tuple-element.54), channel_id=1, source_target_pairs={{0,8},{8,0},{1,9},{9,1},{2,10},{10,2},{3,11},{11,3},{4,12},{12,4},... | collective-permute-start | bytes 2359304 | tf_op jit(solution)/shard_map/ppermute | solution.py:450
  81.3 23.1 %all-to-all-start.3 = ((bf16[8,3,192,128]{3,2,1,0:T(8,128)(2,1)}), bf16[8,3,192,128]{3,2,1,0:T(8,128)(2,1)S(1)}, u32[]{:S(2)}, u32[]{:S(2)}) async-start(bf16[8,3,192,128]{3,2,1,0:T(8,128)(2,1)} %join.1), calls=%async_computation.3 | async-start | bytes 2359296 | tf_op jit(solution)/shard_map/all_to_all | solution.py:442
  84.9 3.7 %collective-permute-start.2 = (f32[8,192]{1,0:T(8,128)S(1)}, f32[8,192]{1,0:T(8,128)S(1)}, u32[]{:S(2)}, u32[]{:S(2)}) collective-permute-start(f32[8,192]{1,0:T(8,128)S(1)} %get-tuple-element.57), channel_id=1, source_target_pairs={{0,2},{1,3},{2,0},{3,1},{4,6},{5,7},{6,4},{7,5},{8,10},{9,11},{10,... | collective-permute-start | bytes 18440 | tf_op jit(solution)/shard_map/ppermute | solution.py:446
  88.6 5.5 %collective-permute-start.3 = (f32[8,192]{1,0:T(8,128)S(1)}, f32[8,192]{1,0:T(8,128)S(1)}, u32[]{:S(2)}, u32[]{:S(2)}) collective-permute-start(f32[8,192]{1,0:T(8,128)S(1)} %add.17), channel_id=1, source_target_pairs={{0,4},{1,5},{2,6},{3,7},{4,0},{5,1},{6,2},{7,3},{8,12},{9,13},{10,... | collective-permute-start | bytes 18440 | tf_op jit(solution)/shard_map/ppermute | solution.py:446
  94.1 5.7 %collective-permute-start.4 = (f32[8,192]{1,0:T(8,128)S(1)}, f32[8,192]{1,0:T(8,128)S(1)}, u32[]{:S(2)}, u32[]{:S(2)}) collective-permute-start(f32[8,192]{1,0:T(8,128)S(1)} %add.18), channel_id=1, source_target_pairs={{0,1},{1,0},{2,3},{3,2},{4,5},{5,4},{6,7},{7,6},{8,9},{9,8},{10,11... | collective-permute-start | bytes 18440 | tf_op jit(solution)/shard_map/ppermute | solution.py:446

commit v7 on v6

--- a/solution.py
+++ b/solution.py
@@ -32,6 +32,7 @@
 
 
 WIDE = 256
+COVER = 32
 
 
 def own_plan(rows):
@@ -129,9 +130,7 @@
     end(count - 1)
 
 
-def forward_own(plan, own_ref, load_ref, kept_ref, mixed_ref, stats_ref, loaded_ref, key_s, turned_s, score_s, sem):
-    load = pltpu.make_async_copy(load_ref, loaded_ref, sem)
-    load.start()
+def forward_own(plan, own_ref, kept_ref, mixed_ref, stats_ref, key_s, turned_s, score_s):
     flat_rows(own_ref, 1, key_s)
     turned_rows(own_ref, 2, turned_s)
     tops = {}
@@ -151,7 +150,6 @@
         mixed_ref[i] = dot(turned_s[:, :keys], kept_ref[pl.ds(base, keys)])
 
     staggered(len(plan), start, middle, end)
-    load.wait()
 
 
 def forward_other(
@@ -161,19 +159,14 @@
     other_ref,
     mixed_ref,
     stats_ref,
-    load_ref,
     kept_ref,
     out_ref,
     own_inverse_ref,
     inverse_ref,
-    loaded_ref,
     key_s,
     turned_s,
     score_s,
-    sem,
 ):
-    load = pltpu.make_async_copy(load_ref, loaded_ref, sem)
-    load.start()
     flat_rows(other_ref, 0, key_s)
     turned_rows(other_ref, 1, turned_s)
     core = facts_ref[2]
@@ -202,7 +195,6 @@
         own_inverse_ref[rows] = jnp.broadcast_to(own_part * inverse, (HEAD, WIDE)).T
 
     staggered(len(plan), start, middle, end)
-    load.wait()
 
 
 def backward_side(
@@ -281,13 +273,22 @@
         query_ref[pl.ds(first, WIDE)] = ((turned + turned_ref[i]) * SCALE).T.astype(BF16)
 
 
-def join_kernel(query_ref, key_ref, value_ref, pair_ref, out_ref):
+def join_kernel(query_ref, key_ref, value_ref, pair_ref, out_ref, pair_s, sems):
     parts, _, block, _ = out_ref.shape
+    copies = []
+    for j in range(parts):
+        source = query_ref.at[pl.ds(j * block, block)]
+        copies.append(pltpu.make_async_copy(source, out_ref.at[j, 0], sems.at[len(copies)]))
+        copies[-1].start()
     for j in range(parts):
         rows = pl.ds(j * block, block)
-        out_ref[j, 0] = query_ref[rows]
-        out_ref[j, 1] = (key_ref[rows] * SCALE + pair_ref[j, 0].astype(F32)).astype(BF16)
-        out_ref[j, 2] = (value_ref[rows] + pair_ref[j, 1].astype(F32)).astype(BF16)
+        pair_s[j, 0] = (key_ref[rows] * SCALE + pair_ref[j, 0].astype(F32)).astype(BF16)
+        pair_s[j, 1] = (value_ref[rows] + pair_ref[j, 1].astype(F32)).astype(BF16)
+        target = out_ref.at[j, pl.ds(1, 2)]
+        copies.append(pltpu.make_async_copy(pair_s.at[j], target, sems.at[len(copies)]))
+        copies[-1].start()
+    for copy in copies:
+        copy.wait()
 
 
 def pack_kernel(*refs):
@@ -309,17 +310,16 @@
 
 def unpack_kernel(facts_ref, stack_ref, losses_ref, *refs):
     arrays, loss_ref, turned_s, loss_s, sems = refs[:-4], refs[-4], refs[-3], refs[-2], refs[-1]
-    copies = []
+    slots = loss_s.shape[1]
+    turned_s[...] = losses_ref[...].T
+    loss_s[...] = turned_s[pl.ds(pl.multiple_of(facts_ref[0] * slots, 8), slots)].T
+    copies = [pltpu.make_async_copy(loss_s, loss_ref, sems.at[0])]
     for t, ref in enumerate(arrays):
         for h in range(stack_ref.shape[0]):
             target = ref.at[:, pl.ds(h * HEAD, HEAD)]
             copies.append(pltpu.make_async_copy(stack_ref.at[h, t], target, sems.at[len(copies)]))
-            copies[-1].start()
-    slots = loss_s.shape[1]
-    turned_s[...] = losses_ref[...].T
-    loss_s[...] = turned_s[pl.ds(pl.multiple_of(facts_ref[0] * slots, 8), slots)].T
-    copies.append(pltpu.make_async_copy(loss_s, loss_ref, sems.at[len(copies)]))
-    copies[-1].start()
+    for copy in copies:
+        copy.start()
     for copy in copies:
         copy.wait()
 
@@ -514,6 +514,7 @@
     own = exchange(stacked)
 
     size = 512
+    w_up_free, w_down_free = w_up, w_down
     w_up = pltpu.with_memory_space_constraint(w_up, pltpu.HBM)
     w_down = pltpu.with_memory_space_constraint(w_down, pltpu.HBM)
     wide_block = pl.BlockSpec((columns, size), lambda i: (0, i))
@@ -532,23 +533,22 @@
     other = swap_cores(own[:, 1:])
 
     kv_scratch = [pltpu.VMEM((rows, HEAD), BF16), pltpu.VMEM((HEAD, rows), BF16)]
-    near_kept, near_mixed, stats, up_held = kernel_call(
+    near_kept, near_mixed, stats = kernel_call(
         functools.partial(forward_own, near_plan),
         "forward_own",
         (
             held((near_rows, WIDE)),
             held((chunks, HEAD, WIDE), F32),
             held((chunks, 8, WIDE), F32),
-            held(w_up.shape),
         ),
-        [vmem(), far()],
-        (vmem(),) * 4,
-        kv_scratch + [pltpu.VMEM((2, rows, WIDE), F32), pltpu.SemaphoreType.DMA],
+        [vmem()],
+        (vmem(),) * 3,
+        kv_scratch + [pltpu.VMEM((2, rows, WIDE), F32)],
         8,
-        4 * near_rows * WIDE * HEAD,
+        COVER * 4 * near_rows * WIDE * HEAD,
         near_rows * WIDE,
-    )(own, w_up)
-    far_kept, attended, near_inverse, far_inverse, down_held = kernel_call(
+    )(own)
+    far_kept, attended, near_inverse, far_inverse = kernel_call(
         functools.partial(forward_other, far_plan),
         "forward_other",
         (
@@ -556,17 +556,16 @@
             held((rows, HEAD)),
             held((rows, HEAD), F32),
             held((rows, HEAD), F32),
-            held(w_down.shape),
         ),
-        [smem()] + [vmem()] * 4 + [far()],
-        (vmem(),) * 5,
-        kv_scratch + [pltpu.VMEM((2, rows, WIDE), F32), pltpu.SemaphoreType.DMA],
+        [smem()] + [vmem()] * 4,
+        (vmem(),) * 4,
+        kv_scratch + [pltpu.VMEM((2, rows, WIDE), F32)],
         8,
-        4 * far_rows * WIDE * HEAD,
+        COVER * 4 * far_rows * WIDE * HEAD,
         far_rows * WIDE,
-    )(facts, own, other, near_mixed, stats, w_down)
-
-    byte_pieces = 4
+    )(facts, own, other, near_mixed, stats)
+
+    byte_pieces = 2
     owned_rows = exchange(attended.reshape(heads, count, HEAD))
     context_grad, losses = kernel_call(
         functools.partial(byte_kernel, byte_pieces),
@@ -585,8 +584,8 @@
         patch_order[None],
         byte_embed,
         norm_gain[None],
-        up_held,
-        down_held,
+        w_up_free,
+        w_down_free,
         *turned,
         vocab_head,
     )
@@ -620,8 +619,8 @@
         "join",
         shape((heads, 3, count, HEAD)),
         [vmem()] * 4,
-        vmem(),
-        [],
+        anywhere(),
+        [pltpu.VMEM((heads, 2, count, HEAD), BF16), pltpu.SemaphoreType.DMA((2 * heads,))],
         4,
         0,
     )(query_grad, key_grad, value_grad, pair_sent)

time: 107 us -> 105 us (0.981)
  Pallas kernels: 43.8 us -> 41.1 us
    pallas_call x1, Pallas kernels: 4.73 us -> 3.24 us  [shards(): kernel_call(functools.partial(forward_other, far_plan), 'forward_other',...]
    pallas_call x1, Pallas kernels: 3.54 us -> 2.27 us  [shards(): kernel_call(functools.partial(forward_own, near_plan), 'forward_own', (he...]
where the time goes in v7:
time: 105 us; the launch traced here: 104 us
  Pallas kernels  41.1 us (39%)
  blocking collectives  27 us (26%)
  starting transfers between devices  17.5 us (17%)
  waiting for transfers between devices  17.5 us (17%)
  between operations  1.13 us (1%)
    all_to_all x2, blocking collectives, exchange(): return lax.all_to_all(value, CHIPS, split_axis=0, concat_axis=0, tiled=True)  27 us
    pallas_call x1, Pallas kernels, shards(): pl.pallas_call(turn_kernel, out_shape=(pltpu.HBM((hidden, columns), BF16)...  14.2 us
    all_to_all x2, starting transfers between devices, exchange(): return lax.all_to_all(value, CHIPS, split_axis=0, concat_axis=0, tiled=True)  10.6 us
    pallas_call x1, Pallas kernels, shards(): kernel_call(functools.partial(byte_kernel, byte_pieces), 'byte_layer', (s...  9.83 us
    all_to_all x2, waiting for transfers between devices, exchange(): return lax.all_to_all(value, CHIPS, split_axis=0, concat_axis=0, tiled=True)  9.06 us
    ppermute x3, waiting for transfers between devices, gather_losses(): lax.ppermute(value, 'grp', [(i, i ^ 1 << bit) for i in range(PATCH)])  8.44 us
    ppermute x3, starting transfers between devices, gather_losses(): lax.ppermute(value, 'grp', [(i, i ^ 1 << bit) for i in range(PATCH)])  6.46 us
    pallas_call x1, Pallas kernels, shards(): kernel_call(functools.partial(forward_other, far_plan), 'forward_other',...  3.24 us
  transfers between devices with their start and end apart: 7, of which 5 were waited for; matrix products, arithmetic and copies ran while one was open for 0% of the time, Pallas kernels for 19%

profile of v7, /device:TPU:0, one launch (start us, length us, event | category | flops | bytes accessed | tf_op | source)
XLA Modules:
  0.0 104.4 jit_solution(12923951368540056175)
XLA Ops:
  0.6 0.1 pad_add_fusion.facts_ref
  0.7 2.3 %pack.1 = bf16[8,3,192,128]{3,2,1,0:T(8,128)(2,1)} custom-call(bf16[192,1024]{1,0:T(8,128)(2,1)} %refs_0_, bf16[192,1024]{1,0:T(8,128)(2,1)} %refs_1_.1, bf16[192,1024]{1,0:T(8,128)(2,1)} %refs_2_.1), custom_call_target="tpu_custom_call" | custom-call | bytes 4194304 | tf_op jit(solution)/shard_map/pack/pallas_call | solution.py:500
  3.0 7.0 %all-to-all-start = ((bf16[8,3,192,128]{3,2,1,0:T(8,128)(2,1)}), bf16[8,3,192,128]{3,2,1,0:T(8,128)(2,1)S(1)}, u32[]{:S(2)}, u32[]{:S(2)}) async-start(bf16[8,3,192,128]{3,2,1,0:T(8,128)(2,1)} %pack.1), calls=%async_computation | async-start | bytes 2359296 | tf_op jit(solution)/shard_map/all_to_all | solution.py:442
  10.0 14.2 %turn_weights.1 = (bf16[4096,1024]{1,0:T(8,128)(2,1)}, bf16[1024,4096]{1,0:T(8,128)(2,1)}) custom-call(bf16[1024,4096]{1,0:T(8,128)(2,1)} %up_ref.3, bf16[4096,1024]{1,0:T(8,128)(2,1)} %down_ref.3), custom_call_target="tpu_custom_call" | custom-call | bytes 33554432 | tf_op jit(solution)/shard_map/turn_weights/pallas_call | solution.py:522
  24.3 4.4 %all-to-all-done.own_ref = bf16[8,3,192,128]{3,2,1,0:T(8,128)(2,1)S(1)} async-done(((bf16[8,3,192,128]{3,2,1,0:T(8,128)(2,1)}), bf16[8,3,192,128]{3,2,1,0:T(8,128)(2,1)S(1)}, u32[]{:S(2)}, u32[]{:S(2)}) %all-to-all-start) | async-done | bytes 1179680 | tf_op jit(solution)/shard_map/all_to_all | solution.py:442
  28.7 0.1 slice.3
  28.7 0.1 collective-permute-start
  28.8 2.3 %forward_own.1 = (bf16[5376,256]{1,0:T(8,128)(2,1)S(1)}, f32[6,128,256]{2,1,0:T(8,128)S(1)}, f32[6,8,256]{2,1,0:T(8,128)S(1)}) custom-call(bf16[8,3,192,128]{3,2,1,0:T(8,128)(2,1)S(1)} %all-to-all-done.own_ref), custom_call_target="tpu_custom_call" | custom-call | flops 22548578304 | bytes 4194304 | tf_op jit(solution)/shard_map/forward_own/pallas_call | solution.py:536
  31.1 0.0 slice-start
  31.1 0.0 slice-start.2
  31.2 0.0 copy-start
  31.2 0.0 copy-start.1
  31.2 0.0 copy-start.2
  31.2 0.0 copy-start.3
  31.3 0.0 copy-start.4
  31.3 3.2 %forward_other.1 = (bf16[6144,256]{1,0:T(8,128)(2,1)S(1)}, bf16[1536,128]{1,0:T(8,128)(2,1)S(1)}, f32[1536,128]{1,0:T(8,128)S(1)}, f32[1536,128]{1,0:T(8,128)S(1)}) custom-call(s32[3]{0:T(128)S(1)} %pad_add_fusion.facts_ref, bf16[8,3,192,128]{3,2,1,0:T(8,128)(2,1)S(1)} %all-to-all-done.own_ref, bf16[8,2,192,128]{3,2,1,0:T(8,128)(2,1)S(1)} %collective-permute-done.other_ref, ...), custom_call_target="tpu_custom_call" | custom-call | flops 25769803776 | bytes 4194304 | tf_op jit(solution)/shard_map/forward_other/pallas_call | solution.py:551
  34.5 14.1 %all_to_all.20.rows_ref = bf16[8,192,128]{2,1,0:T(8,128)(2,1)S(1)} all-to-all(bf16[8,192,128]{2,1,0:T(8,128)(2,1)S(1)} %bitcast.17), channel_id=1, replica_groups=mesh['seq_0'=4,'seq_1'=2,'seq_2'=2,'grp'=8] {'seq_0','seq_1'}, dimensions={0} | all-to-all | bytes 786432 | tf_op jit(solution)/shard_map/all_to_all | solution.py:442
  48.8 9.8 %byte_layer.1 = (bf16[8,192,128]{2,1,0:T(8,128)(2,1)S(1)}, f32[8,192]{1,0:T(8,128)S(1)}) custom-call(s32[3]{0:T(128)S(1)} %pad_add_fusion.facts_ref, bf16[8,192,128]{2,1,0:T(8,128)(2,1)S(1)} %all_to_all.20.rows_ref, s32[8,192]{1,0:T(8,128)S(1)} %bitcast.20, s32[1,192]{1,0:T(1,128)S(1)} %bitcast.22, bf16[256,1024]{1,0:T(8,128)(2,1)S(1)} %copy-done, ...), custom_call_target="tpu_custom_call" | custom-call | flops 6442450944 | bytes 4194304 | tf_op jit(solution)/shard_map/byte_layer/pallas_call | solution.py:570
  58.6 12.9 %all_to_all.21 = bf16[8,192,128]{2,1,0:T(8,128)(2,1)S(1)} all-to-all(bf16[8,192,128]{2,1,0:T(8,128)(2,1)S(1)} %get-tuple-element.43), channel_id=1, replica_groups=mesh['seq_0'=4,'seq_1'=2,'seq_2'=2,'grp'=8] {'seq_0','seq_1'}, dimensions={0} | all-to-all | bytes 786432 | tf_op jit(solution)/shard_map/all_to_all | solution.py:442
  71.5 3.2 %backward_other.1 = (bf16[8,2,192,128]{3,2,1,0:T(8,128)(2,1)S(1)}, f32[6,128,256]{2,1,0:T(8,128)S(1)}) custom-call(bf16[8,3,192,128]{3,2,1,0:T(8,128)(2,1)S(1)} %all-to-all-done.own_ref, bf16[8,2,192,128]{3,2,1,0:T(8,128)(2,1)S(1)} %collective-permute-done.other_ref, bf16[1536,128]{1,0:T(8,128)(2,1)S(1)} %get-tuple-element.38.mixed_ref, ...), custom_call_target="tpu_custom_call" | custom-call | flops 1610612736 | bytes 4194304 | tf_op jit(solution)/shard_map/backward_other/pallas_call | solution.py:596
  74.7 0.3 collective-permute-start.1
  75.0 3.0 %backward_own.1 = (bf16[1536,128]{1,0:T(8,128)(2,1)S(1)}, f32[1536,128]{1,0:T(8,128)S(1)}, f32[1536,128]{1,0:T(8,128)S(1)}) custom-call(bf16[8,3,192,128]{3,2,1,0:T(8,128)(2,1)S(1)} %all-to-all-done.own_ref, bf16[1536,128]{1,0:T(8,128)(2,1)S(1)} %get-tuple-element.38.mixed_ref, f32[1536,128]{1,0:T(8,128)S(1)} %get-tuple-element.39.inverse_ref, ...), custom_call_target="tpu_custom_call" | custom-call | flops 1409286144 | bytes 4194304 | tf_op jit(solution)/shard_map/backward_own/pallas_call | solution.py:607
  78.0 1.2 %join.1 = bf16[8,3,192,128]{3,2,1,0:T(8,128)(2,1)} custom-call(bf16[1536,128]{1,0:T(8,128)(2,1)S(1)} %get-tuple-element.47.query_ref, f32[1536,128]{1,0:T(8,128)S(1)} %get-tuple-element.48.key_ref, f32[1536,128]{1,0:T(8,128)S(1)} %get-tuple-element.49.value_ref, bf16[8,2,192,128]{3,2,1,0:T(8,128)(2,1)S(1)} %collective-permute-done.1.pair_ref), custom_call_target="tpu_custom_call" | custom-call | bytes 4194304 | tf_op jit(solution)/shard_map/join/pallas_call | solution.py:617
  79.2 3.6 %all-to-all-start.3 = ((bf16[8,3,192,128]{3,2,1,0:T(8,128)(2,1)}), bf16[8,3,192,128]{3,2,1,0:T(8,128)(2,1)S(1)}, u32[]{:S(2)}, u32[]{:S(2)}) async-start(bf16[8,3,192,128]{3,2,1,0:T(8,128)(2,1)} %join.1), calls=%async_computation.3 | async-start | bytes 2359296 | tf_op jit(solution)/shard_map/all_to_all | solution.py:442
  82.8 2.0 %collective-permute-start.2 = (f32[8,192]{1,0:T(8,128)S(1)}, f32[8,192]{1,0:T(8,128)S(1)}, u32[]{:S(2)}, u32[]{:S(2)}) collective-permute-start(f32[8,192]{1,0:T(8,128)S(1)} %get-tuple-element.53), channel_id=1, source_target_pairs={{0,2},{1,3},{2,0},{3,1},{4,6},{5,7},{6,4},{7,5},{8,10},{9,11},{10,... | collective-permute-start | bytes 18440 | tf_op jit(solution)/shard_map/ppermute | solution.py:446
  84.8 1.7 %collective-permute-done.2 = f32[8,192]{1,0:T(8,128)S(1)} collective-permute-done((f32[8,192]{1,0:T(8,128)S(1)}, f32[8,192]{1,0:T(8,128)S(1)}, u32[]{:S(2)}, u32[]{:S(2)}) %collective-permute-start.2) | collective-permute-done | bytes 6176 | tf_op jit(solution)/shard_map/ppermute | solution.py:446
  86.5 3.9 %collective-permute-start.3 = (f32[8,192]{1,0:T(8,128)S(1)}, f32[8,192]{1,0:T(8,128)S(1)}, u32[]{:S(2)}, u32[]{:S(2)}) collective-permute-start(f32[8,192]{1,0:T(8,128)S(1)} %add.17), channel_id=1, source_target_pairs={{0,4},{1,5},{2,6},{3,7},{4,0},{5,1},{6,2},{7,3},{8,12},{9,13},{10,... | collective-permute-start | bytes 18440 | tf_op jit(solution)/shard_map/ppermute | solution.py:446
  90.4 1.6 %collective-permute-done.3 = f32[8,192]{1,0:T(8,128)S(1)} collective-permute-done((f32[8,192]{1,0:T(8,128)S(1)}, f32[8,192]{1,0:T(8,128)S(1)}, u32[]{:S(2)}, u32[]{:S(2)}) %collective-permute-start.3) | collective-permute-done | bytes 6176 | tf_op jit(solution)/shard_map/ppermute | solution.py:446
  92.0 0.6 collective-permute-start.4
  92.6 5.1 %collective-permute-done.4 = f32[8,192]{1,0:T(8,128)S(1)} collective-permute-done((f32[8,192]{1,0:T(8,128)S(1)}, f32[8,192]{1,0:T(8,128)S(1)}, u32[]{:S(2)}, u32[]{:S(2)}) %collective-permute-start.4) | collective-permute-done | bytes 6176 | tf_op jit(solution)/shard_map/ppermute | solution.py:446
  97.7 4.7 %all-to-all-done.3.stack_ref = bf16[8,3,192,128]{3,2,1,0:T(8,128)(2,1)S(1)} async-done(((bf16[8,3,192,128]{3,2,1,0:T(8,128)(2,1)}), bf16[8,3,192,128]{3,2,1,0:T(8,128)(2,1)S(1)}, u32[]{:S(2)}, u32[]{:S(2)}) %all-to-all-start.3) | async-done | bytes 1179680 | tf_op jit(solution)/shard_map/all_to_all | solution.py:442
  102.3 1.9 %unpack.1 = (bf16[192,1024]{1,0:T(8,128)(2,1)}, bf16[192,1024]{1,0:T(8,128)(2,1)}, bf16[192,1024]{1,0:T(8,128)(2,1)}, f32[8,24]{1,0:T(8,128)}) custom-call(s32[3]{0:T(128)S(1)} %pad_add_fusion.facts_ref, bf16[8,3,192,128]{3,2,1,0:T(8,128)(2,1)S(1)} %all-to-all-done.3.stack_ref, f32[8,192]{1,0:T(8,128)S(1)} %add.19.losses_ref), custom_call_target="tpu_custom_call" | custom-call | bytes 4194304 | tf_op jit(solution)/shard_map/unpack/pallas_call | solution.py:631
  (28 shorter events, 0.1 us)
Async XLA Ops:
  3.0 25.7 %all-to-all-start = ((bf16[8,3,192,128]{3,2,1,0:T(8,128)(2,1)}), bf16[8,3,192,128]{3,2,1,0:T(8,128)(2,1)S(1)}, u32[]{:S(2)}, u32[]{:S(2)}) async-start(bf16[8,3,192,128]{3,2,1,0:T(8,128)(2,1)} %pack.1), calls=%async_computation | async-start | bytes 2359296 | tf_op jit(solution)/shard_map/all_to_all | solution.py:442
  28.7 2.4 %collective-permute-start = (bf16[8,2,192,128]{3,2,1,0:T(8,128)(2,1)S(1)}, bf16[8,2,192,128]{3,2,1,0:T(8,128)(2,1)S(1)}, u32[]{:S(2)}, u32[]{:S(2)}) collective-permute-start(bf16[8,2,192,128]{3,2,1,0:T(8,128)(2,1)S(1)} %slice.3), channel_id=1, source_target_pairs={{0,8},{8,0},{1,9},{9,1},{2,10},{10,2},{3,11},{11,3},{4,12},{12,4},... | collective-permute-start | bytes 2359304 | tf_op jit(solution)/shard_map/ppermute | solution.py:450
  31.1 17.5 %slice-start = ((s8[8388608]{0:T(1024)(128)(4,1)}), s8[4194304]{0:T(1024)(128)(4,1)S(1)}, s32[]{:S(2)}) async-start(s8[8388608]{0:T(1024)(128)(4,1)} %bitcast.9), calls=%async_computation.4 | async-start | bytes 8388608
  31.1 17.5 %slice-start.2 = ((s8[8388608]{0:T(1024)(128)(4,1)}), s8[4194304]{0:T(1024)(128)(4,1)S(1)}, s32[]{:S(2)}) async-start(s8[8388608]{0:T(1024)(128)(4,1)} %bitcast.11), calls=%async_computation.6 | async-start | bytes 8388608
  31.1 17.5 %slice-start.4 = ((s8[8388608]{0:T(1024)(128)(4,1)}), s8[4194304]{0:T(1024)(128)(4,1)S(1)}, s32[]{:S(2)}) async-start(s8[8388608]{0:T(1024)(128)(4,1)} %bitcast.13), calls=%async_computation.8 | async-start | bytes 8388608
  31.2 17.5 %slice-start.6 = ((s8[8388608]{0:T(1024)(128)(4,1)}), s8[4194304]{0:T(1024)(128)(4,1)S(1)}, s32[]{:S(2)}) async-start(s8[8388608]{0:T(1024)(128)(4,1)} %bitcast.15), calls=%async_computation.10 | async-start | bytes 8388608
  31.2 17.5 %slice-start.1 = ((s8[8388608]{0:T(1024)(128)(4,1)}), s8[4194304]{0:T(1024)(128)(4,1)S(1)}, s32[]{:S(2)}) async-start(s8[8388608]{0:T(1024)(128)(4,1)} %bitcast.9), calls=%async_computation.5 | async-start | bytes 8388608
  31.2 17.5 %slice-start.3 = ((s8[8388608]{0:T(1024)(128)(4,1)}), s8[4194304]{0:T(1024)(128)(4,1)S(1)}, s32[]{:S(2)}) async-start(s8[8388608]{0:T(1024)(128)(4,1)} %bitcast.11), calls=%async_computation.7 | async-start | bytes 8388608
  31.2 17.5 %slice-start.5 = ((s8[8388608]{0:T(1024)(128)(4,1)}), s8[4194304]{0:T(1024)(128)(4,1)S(1)}, s32[]{:S(2)}) async-start(s8[8388608]{0:T(1024)(128)(4,1)} %bitcast.13), calls=%async_computation.9 | async-start | bytes 8388608
  31.2 17.5 %slice-start.7 = ((s8[8388608]{0:T(1024)(128)(4,1)}), s8[4194304]{0:T(1024)(128)(4,1)S(1)}, s32[]{:S(2)}) async-start(s8[8388608]{0:T(1024)(128)(4,1)} %bitcast.15), calls=%async_computation.11 | async-start | bytes 8388608
  31.2 17.5 %copy-start = (bf16[256,1024]{1,0:T(8,128)(2,1)S(1)}, bf16[256,1024]{1,0:T(8,128)(2,1)}, u32[]{:S(2)}) copy-start(bf16[256,1024]{1,0:T(8,128)(2,1)} %embed_ref.1) | copy-start | bytes 1572868
  31.2 17.5 %copy-start.1 = (bf16[1024,256]{1,0:T(8,128)(2,1)S(1)}, bf16[1024,256]{1,0:T(8,128)(2,1)}, u32[]{:S(2)}) copy-start(bf16[1024,256]{1,0:T(8,128)(2,1)} %vocab_ref.1) | copy-start | bytes 1572868
  31.2 17.5 %copy-start.2 = (s32[192,8]{0,1:T(8,128)S(1)}, s32[192,8]{0,1:T(8,128)}, u32[]{:S(2)}) copy-start(s32[192,8]{0,1:T(8,128)} %param.10) | copy-start | bytes 18436
  31.2 17.5 %copy-start.3 = (f32[1024]{0:T(1024)S(1)}, f32[1024]{0:T(1024)}, u32[]{:S(2)}) copy-start(f32[1024]{0:T(1024)} %param.16) | copy-start | bytes 12292
  31.3 17.5 %copy-start.4 = (s32[192]{0:T(256)S(1)}, s32[192]{0:T(256)}, u32[]{:S(2)}) copy-start(s32[192]{0:T(256)} %param.11) | copy-start | bytes 2308
  74.7 3.3 %collective-permute-start.1 = (bf16[8,2,192,128]{3,2,1,0:T(8,128)(2,1)S(1)}, bf16[8,2,192,128]{3,2,1,0:T(8,128)(2,1)S(1)}, u32[]{:S(2)}, u32[]{:S(2)}) collective-permute-start(bf16[8,2,192,128]{3,2,1,0:T(8,128)(2,1)S(1)} %get-tuple-element.50), channel_id=1, source_target_pairs={{0,8},{8,0},{1,9},{9,1},{2,10},{10,2},{3,11},{11,3},{4,12},{12,4},... | collective-permute-start | bytes 2359304 | tf_op jit(solution)/shard_map/ppermute | solution.py:450
  79.2 23.2 %all-to-all-start.3 = ((bf16[8,3,192,128]{3,2,1,0:T(8,128)(2,1)}), bf16[8,3,192,128]{3,2,1,0:T(8,128)(2,1)S(1)}, u32[]{:S(2)}, u32[]{:S(2)}) async-start(bf16[8,3,192,128]{3,2,1,0:T(8,128)(2,1)} %join.1), calls=%async_computation.3 | async-start | bytes 2359296 | tf_op jit(solution)/shard_map/all_to_all | solution.py:442
  82.8 3.7 %collective-permute-start.2 = (f32[8,192]{1,0:T(8,128)S(1)}, f32[8,192]{1,0:T(8,128)S(1)}, u32[]{:S(2)}, u32[]{:S(2)}) collective-permute-start(f32[8,192]{1,0:T(8,128)S(1)} %get-tuple-element.53), channel_id=1, source_target_pairs={{0,2},{1,3},{2,0},{3,1},{4,6},{5,7},{6,4},{7,5},{8,10},{9,11},{10,... | collective-permute-start | bytes 18440 | tf_op jit(solution)/shard_map/ppermute | solution.py:446
  86.5 5.5 %collective-permute-start.3 = (f32[8,192]{1,0:T(8,128)S(1)}, f32[8,192]{1,0:T(8,128)S(1)}, u32[]{:S(2)}, u32[]{:S(2)}) collective-permute-start(f32[8,192]{1,0:T(8,128)S(1)} %add.17), channel_id=1, source_target_pairs={{0,4},{1,5},{2,6},{3,7},{4,0},{5,1},{6,2},{7,3},{8,12},{9,13},{10,... | collective-permute-start | bytes 18440 | tf_op jit(solution)/shard_map/ppermute | solution.py:446
  92.0 5.7 %collective-permute-start.4 = (f32[8,192]{1,0:T(8,128)S(1)}, f32[8,192]{1,0:T(8,128)S(1)}, u32[]{:S(2)}, u32[]{:S(2)}) collective-permute-start(f32[8,192]{1,0:T(8,128)S(1)} %add.18), channel_id=1, source_target_pairs={{0,1},{1,0},{2,3},{3,2},{4,5},{5,4},{6,7},{7,6},{8,9},{9,8},{10,11... | collective-permute-start | bytes 18440 | tf_op jit(solution)/shard_map/ppermute | solution.py:446

commit v8 on v7

--- a/solution.py
+++ b/solution.py
@@ -55,7 +55,10 @@
         for at in range(0, keys, block):
             part = at // block
             kind = "all" if part < lowest else "block" if part <= highest else "none"
-            pieces.append((at, block, kind))
+            if kind == "all" and part % 2 and pieces[-1][2] == "all":
+                pieces[-1] = (at - block, 2 * block, kind)
+            else:
+                pieces.append((at, block, kind))
         plan.append((first, base, keys, pieces))
         base += keys
     return plan, base
@@ -273,22 +276,13 @@
         query_ref[pl.ds(first, WIDE)] = ((turned + turned_ref[i]) * SCALE).T.astype(BF16)
 
 
-def join_kernel(query_ref, key_ref, value_ref, pair_ref, out_ref, pair_s, sems):
+def join_kernel(query_ref, key_ref, value_ref, pair_ref, out_ref):
     parts, _, block, _ = out_ref.shape
-    copies = []
-    for j in range(parts):
-        source = query_ref.at[pl.ds(j * block, block)]
-        copies.append(pltpu.make_async_copy(source, out_ref.at[j, 0], sems.at[len(copies)]))
-        copies[-1].start()
     for j in range(parts):
         rows = pl.ds(j * block, block)
-        pair_s[j, 0] = (key_ref[rows] * SCALE + pair_ref[j, 0].astype(F32)).astype(BF16)
-        pair_s[j, 1] = (value_ref[rows] + pair_ref[j, 1].astype(F32)).astype(BF16)
-        target = out_ref.at[j, pl.ds(1, 2)]
-        copies.append(pltpu.make_async_copy(pair_s.at[j], target, sems.at[len(copies)]))
-        copies[-1].start()
-    for copy in copies:
-        copy.wait()
+        out_ref[j, 0] = query_ref[rows]
+        out_ref[j, 1] = (key_ref[rows] * SCALE + pair_ref[j, 0].astype(F32)).astype(BF16)
+        out_ref[j, 2] = (value_ref[rows] + pair_ref[j, 1].astype(F32)).astype(BF16)
 
 
 def pack_kernel(*refs):
@@ -310,16 +304,17 @@
 
 def unpack_kernel(facts_ref, stack_ref, losses_ref, *refs):
     arrays, loss_ref, turned_s, loss_s, sems = refs[:-4], refs[-4], refs[-3], refs[-2], refs[-1]
-    slots = loss_s.shape[1]
-    turned_s[...] = losses_ref[...].T
-    loss_s[...] = turned_s[pl.ds(pl.multiple_of(facts_ref[0] * slots, 8), slots)].T
-    copies = [pltpu.make_async_copy(loss_s, loss_ref, sems.at[0])]
+    copies = []
     for t, ref in enumerate(arrays):
         for h in range(stack_ref.shape[0]):
             target = ref.at[:, pl.ds(h * HEAD, HEAD)]
             copies.append(pltpu.make_async_copy(stack_ref.at[h, t], target, sems.at[len(copies)]))
-    for copy in copies:
-        copy.start()
+            copies[-1].start()
+    slots = loss_s.shape[1]
+    turned_s[...] = losses_ref[...].T
+    loss_s[...] = turned_s[pl.ds(pl.multiple_of(facts_ref[0] * slots, 8), slots)].T
+    copies.append(pltpu.make_async_copy(loss_s, loss_ref, sems.at[len(copies)]))
+    copies[-1].start()
     for copy in copies:
         copy.wait()
 
@@ -565,7 +560,7 @@
         far_rows * WIDE,
     )(facts, own, other, near_mixed, stats)
 
-    byte_pieces = 2
+    byte_pieces = 4
     owned_rows = exchange(attended.reshape(heads, count, HEAD))
     context_grad, losses = kernel_call(
         functools.partial(byte_kernel, byte_pieces),
@@ -619,8 +614,8 @@
         "join",
         shape((heads, 3, count, HEAD)),
         [vmem()] * 4,
-        anywhere(),
-        [pltpu.VMEM((heads, 2, count, HEAD), BF16), pltpu.SemaphoreType.DMA((2 * heads,))],
+        vmem(),
+        [],
         4,
         0,
     )(query_grad, key_grad, value_grad, pair_sent)

time: 105 us -> 105 us (level)
  no operation moved by 1% of the time
where the time goes in v8:
time: 105 us; the launch traced here: 104 us
  Pallas kernels  41 us (39%)
  blocking collectives  27 us (26%)
  starting transfers between devices  17.5 us (17%)
  waiting for transfers between devices  17.5 us (17%)
  between operations  1.12 us (1%)
    all_to_all x2, blocking collectives, exchange(): return lax.all_to_all(value, CHIPS, split_axis=0, concat_axis=0, tiled=True)  27 us
    pallas_call x1, Pallas kernels, shards(): pl.pallas_call(turn_kernel, out_shape=(pltpu.HBM((hidden, columns), BF16)...  14.2 us
    all_to_all x2, starting transfers between devices, exchange(): return lax.all_to_all(value, CHIPS, split_axis=0, concat_axis=0, tiled=True)  10.6 us
    pallas_call x1, Pallas kernels, shards(): kernel_call(functools.partial(byte_kernel, byte_pieces), 'byte_layer', (s...  9.87 us
    all_to_all x2, waiting for transfers between devices, exchange(): return lax.all_to_all(value, CHIPS, split_axis=0, concat_axis=0, tiled=True)  9.04 us
    ppermute x3, waiting for transfers between devices, gather_losses(): lax.ppermute(value, 'grp', [(i, i ^ 1 << bit) for i in range(PATCH)])  8.43 us
    ppermute x3, starting transfers between devices, gather_losses(): lax.ppermute(value, 'grp', [(i, i ^ 1 << bit) for i in range(PATCH)])  6.49 us
    pallas_call x1, Pallas kernels, shards(): kernel_call(functools.partial(forward_other, far_plan), 'forward_other',...  3.21 us
  transfers between devices with their start and end apart: 7, of which 5 were waited for; matrix products, arithmetic and copies ran while one was open for 0% of the time, Pallas kernels for 19%

profile of v8, /device:TPU:0, one launch (start us, length us, event | category | flops | bytes accessed | tf_op | source)
XLA Modules:
  0.0 104.3 jit_solution(6373709555255872078)
XLA Ops:
  0.6 0.1 pad_add_fusion.facts_ref
  0.7 2.3 %pack.1 = bf16[8,3,192,128]{3,2,1,0:T(8,128)(2,1)} custom-call(bf16[192,1024]{1,0:T(8,128)(2,1)} %refs_0_, bf16[192,1024]{1,0:T(8,128)(2,1)} %refs_1_.1, bf16[192,1024]{1,0:T(8,128)(2,1)} %refs_2_.1), custom_call_target="tpu_custom_call" | custom-call | bytes 4194304 | tf_op jit(solution)/shard_map/pack/pallas_call | solution.py:495
  3.0 7.0 %all-to-all-start = ((bf16[8,3,192,128]{3,2,1,0:T(8,128)(2,1)}), bf16[8,3,192,128]{3,2,1,0:T(8,128)(2,1)S(1)}, u32[]{:S(2)}, u32[]{:S(2)}) async-start(bf16[8,3,192,128]{3,2,1,0:T(8,128)(2,1)} %pack.1), calls=%async_computation | async-start | bytes 2359296 | tf_op jit(solution)/shard_map/all_to_all | solution.py:437
  10.0 14.2 %turn_weights.1 = (bf16[4096,1024]{1,0:T(8,128)(2,1)}, bf16[1024,4096]{1,0:T(8,128)(2,1)}) custom-call(bf16[1024,4096]{1,0:T(8,128)(2,1)} %up_ref.3, bf16[4096,1024]{1,0:T(8,128)(2,1)} %down_ref.3), custom_call_target="tpu_custom_call" | custom-call | bytes 33554432 | tf_op jit(solution)/shard_map/turn_weights/pallas_call | solution.py:517
  24.3 4.4 %all-to-all-done.own_ref = bf16[8,3,192,128]{3,2,1,0:T(8,128)(2,1)S(1)} async-done(((bf16[8,3,192,128]{3,2,1,0:T(8,128)(2,1)}), bf16[8,3,192,128]{3,2,1,0:T(8,128)(2,1)S(1)}, u32[]{:S(2)}, u32[]{:S(2)}) %all-to-all-start) | async-done | bytes 1179680 | tf_op jit(solution)/shard_map/all_to_all | solution.py:437
  28.7 0.1 slice.3
  28.7 0.1 collective-permute-start
  28.8 2.3 %forward_own.1 = (bf16[5376,256]{1,0:T(8,128)(2,1)S(1)}, f32[6,128,256]{2,1,0:T(8,128)S(1)}, f32[6,8,256]{2,1,0:T(8,128)S(1)}) custom-call(bf16[8,3,192,128]{3,2,1,0:T(8,128)(2,1)S(1)} %all-to-all-done.own_ref), custom_call_target="tpu_custom_call" | custom-call | flops 22548578304 | bytes 4194304 | tf_op jit(solution)/shard_map/forward_own/pallas_call | solution.py:531
  31.1 0.0 slice-start
  31.1 0.0 slice-start.2
  31.2 0.0 copy-start
  31.2 0.0 copy-start.1
  31.2 0.0 copy-start.2
  31.2 0.0 copy-start.3
  31.3 0.0 copy-start.4
  31.3 3.2 %forward_other.1 = (bf16[6144,256]{1,0:T(8,128)(2,1)S(1)}, bf16[1536,128]{1,0:T(8,128)(2,1)S(1)}, f32[1536,128]{1,0:T(8,128)S(1)}, f32[1536,128]{1,0:T(8,128)S(1)}) custom-call(s32[3]{0:T(128)S(1)} %pad_add_fusion.facts_ref, bf16[8,3,192,128]{3,2,1,0:T(8,128)(2,1)S(1)} %all-to-all-done.own_ref, bf16[8,2,192,128]{3,2,1,0:T(8,128)(2,1)S(1)} %collective-permute-done.other_ref, ...), custom_call_target="tpu_custom_call" | custom-call | flops 25769803776 | bytes 4194304 | tf_op jit(solution)/shard_map/forward_other/pallas_call | solution.py:546
  34.5 14.1 %all_to_all.20.rows_ref = bf16[8,192,128]{2,1,0:T(8,128)(2,1)S(1)} all-to-all(bf16[8,192,128]{2,1,0:T(8,128)(2,1)S(1)} %bitcast.17), channel_id=1, replica_groups=mesh['seq_0'=4,'seq_1'=2,'seq_2'=2,'grp'=8] {'seq_0','seq_1'}, dimensions={0} | all-to-all | bytes 786432 | tf_op jit(solution)/shard_map/all_to_all | solution.py:437
  48.7 9.9 %byte_layer.1 = (bf16[8,192,128]{2,1,0:T(8,128)(2,1)S(1)}, f32[8,192]{1,0:T(8,128)S(1)}) custom-call(s32[3]{0:T(128)S(1)} %pad_add_fusion.facts_ref, bf16[8,192,128]{2,1,0:T(8,128)(2,1)S(1)} %all_to_all.20.rows_ref, s32[8,192]{1,0:T(8,128)S(1)} %bitcast.20, s32[1,192]{1,0:T(1,128)S(1)} %bitcast.22, bf16[256,1024]{1,0:T(8,128)(2,1)S(1)} %copy-done, ...), custom_call_target="tpu_custom_call" | custom-call | flops 6442450944 | bytes 4194304 | tf_op jit(solution)/shard_map/byte_layer/pallas_call | solution.py:565
  58.6 12.9 %all_to_all.21 = bf16[8,192,128]{2,1,0:T(8,128)(2,1)S(1)} all-to-all(bf16[8,192,128]{2,1,0:T(8,128)(2,1)S(1)} %get-tuple-element.43), channel_id=1, replica_groups=mesh['seq_0'=4,'seq_1'=2,'seq_2'=2,'grp'=8] {'seq_0','seq_1'}, dimensions={0} | all-to-all | bytes 786432 | tf_op jit(solution)/shard_map/all_to_all | solution.py:437
  71.5 3.2 %backward_other.1 = (bf16[8,2,192,128]{3,2,1,0:T(8,128)(2,1)S(1)}, f32[6,128,256]{2,1,0:T(8,128)S(1)}) custom-call(bf16[8,3,192,128]{3,2,1,0:T(8,128)(2,1)S(1)} %all-to-all-done.own_ref, bf16[8,2,192,128]{3,2,1,0:T(8,128)(2,1)S(1)} %collective-permute-done.other_ref, bf16[1536,128]{1,0:T(8,128)(2,1)S(1)} %get-tuple-element.38.mixed_ref, ...), custom_call_target="tpu_custom_call" | custom-call | flops 1610612736 | bytes 4194304 | tf_op jit(solution)/shard_map/backward_other/pallas_call | solution.py:591
  74.7 0.3 collective-permute-start.1
  75.0 3.0 %backward_own.1 = (bf16[1536,128]{1,0:T(8,128)(2,1)S(1)}, f32[1536,128]{1,0:T(8,128)S(1)}, f32[1536,128]{1,0:T(8,128)S(1)}) custom-call(bf16[8,3,192,128]{3,2,1,0:T(8,128)(2,1)S(1)} %all-to-all-done.own_ref, bf16[1536,128]{1,0:T(8,128)(2,1)S(1)} %get-tuple-element.38.mixed_ref, f32[1536,128]{1,0:T(8,128)S(1)} %get-tuple-element.39.inverse_ref, ...), custom_call_target="tpu_custom_call" | custom-call | flops 1409286144 | bytes 4194304 | tf_op jit(solution)/shard_map/backward_own/pallas_call | solution.py:602
  78.0 1.2 %join.1 = bf16[8,3,192,128]{3,2,1,0:T(8,128)(2,1)} custom-call(bf16[1536,128]{1,0:T(8,128)(2,1)S(1)} %get-tuple-element.47.query_ref, f32[1536,128]{1,0:T(8,128)S(1)} %get-tuple-element.48.key_ref, f32[1536,128]{1,0:T(8,128)S(1)} %get-tuple-element.49.value_ref, bf16[8,2,192,128]{3,2,1,0:T(8,128)(2,1)S(1)} %collective-permute-done.1.pair_ref), custom_call_target="tpu_custom_call" | custom-call | bytes 4194304 | tf_op jit(solution)/shard_map/join/pallas_call | solution.py:612
  79.2 3.6 %all-to-all-start.3 = ((bf16[8,3,192,128]{3,2,1,0:T(8,128)(2,1)}), bf16[8,3,192,128]{3,2,1,0:T(8,128)(2,1)S(1)}, u32[]{:S(2)}, u32[]{:S(2)}) async-start(bf16[8,3,192,128]{3,2,1,0:T(8,128)(2,1)} %join.1), calls=%async_computation.3 | async-start | bytes 2359296 | tf_op jit(solution)/shard_map/all_to_all | solution.py:437
  82.8 2.0 %collective-permute-start.2 = (f32[8,192]{1,0:T(8,128)S(1)}, f32[8,192]{1,0:T(8,128)S(1)}, u32[]{:S(2)}, u32[]{:S(2)}) collective-permute-start(f32[8,192]{1,0:T(8,128)S(1)} %get-tuple-element.53), channel_id=1, source_target_pairs={{0,2},{1,3},{2,0},{3,1},{4,6},{5,7},{6,4},{7,5},{8,10},{9,11},{10,... | collective-permute-start | bytes 18440 | tf_op jit(solution)/shard_map/ppermute | solution.py:441
  84.8 1.7 %collective-permute-done.2 = f32[8,192]{1,0:T(8,128)S(1)} collective-permute-done((f32[8,192]{1,0:T(8,128)S(1)}, f32[8,192]{1,0:T(8,128)S(1)}, u32[]{:S(2)}, u32[]{:S(2)}) %collective-permute-start.2) | collective-permute-done | bytes 6176 | tf_op jit(solution)/shard_map/ppermute | solution.py:441
  86.5 3.9 %collective-permute-start.3 = (f32[8,192]{1,0:T(8,128)S(1)}, f32[8,192]{1,0:T(8,128)S(1)}, u32[]{:S(2)}, u32[]{:S(2)}) collective-permute-start(f32[8,192]{1,0:T(8,128)S(1)} %add.17), channel_id=1, source_target_pairs={{0,4},{1,5},{2,6},{3,7},{4,0},{5,1},{6,2},{7,3},{8,12},{9,13},{10,... | collective-permute-start | bytes 18440 | tf_op jit(solution)/shard_map/ppermute | solution.py:441
  90.4 1.6 %collective-permute-done.3 = f32[8,192]{1,0:T(8,128)S(1)} collective-permute-done((f32[8,192]{1,0:T(8,128)S(1)}, f32[8,192]{1,0:T(8,128)S(1)}, u32[]{:S(2)}, u32[]{:S(2)}) %collective-permute-start.3) | collective-permute-done | bytes 6176 | tf_op jit(solution)/shard_map/ppermute | solution.py:441
  92.0 0.6 collective-permute-start.4
  92.6 5.1 %collective-permute-done.4 = f32[8,192]{1,0:T(8,128)S(1)} collective-permute-done((f32[8,192]{1,0:T(8,128)S(1)}, f32[8,192]{1,0:T(8,128)S(1)}, u32[]{:S(2)}, u32[]{:S(2)}) %collective-permute-start.4) | collective-permute-done | bytes 6176 | tf_op jit(solution)/shard_map/ppermute | solution.py:441
  97.7 4.6 %all-to-all-done.3.stack_ref = bf16[8,3,192,128]{3,2,1,0:T(8,128)(2,1)S(1)} async-done(((bf16[8,3,192,128]{3,2,1,0:T(8,128)(2,1)}), bf16[8,3,192,128]{3,2,1,0:T(8,128)(2,1)S(1)}, u32[]{:S(2)}, u32[]{:S(2)}) %all-to-all-start.3) | async-done | bytes 1179680 | tf_op jit(solution)/shard_map/all_to_all | solution.py:437
  102.3 1.7 %unpack.1 = (bf16[192,1024]{1,0:T(8,128)(2,1)}, bf16[192,1024]{1,0:T(8,128)(2,1)}, bf16[192,1024]{1,0:T(8,128)(2,1)}, f32[8,24]{1,0:T(8,128)}) custom-call(s32[3]{0:T(128)S(1)} %pad_add_fusion.facts_ref, bf16[8,3,192,128]{3,2,1,0:T(8,128)(2,1)S(1)} %all-to-all-done.3.stack_ref, f32[8,192]{1,0:T(8,128)S(1)} %add.19.losses_ref), custom_call_target="tpu_custom_call" | custom-call | bytes 4194304 | tf_op jit(solution)/shard_map/unpack/pallas_call | solution.py:626
  (28 shorter events, 0.1 us)
Async XLA Ops:
  3.0 25.7 %all-to-all-start = ((bf16[8,3,192,128]{3,2,1,0:T(8,128)(2,1)}), bf16[8,3,192,128]{3,2,1,0:T(8,128)(2,1)S(1)}, u32[]{:S(2)}, u32[]{:S(2)}) async-start(bf16[8,3,192,128]{3,2,1,0:T(8,128)(2,1)} %pack.1), calls=%async_computation | async-start | bytes 2359296 | tf_op jit(solution)/shard_map/all_to_all | solution.py:437
  28.7 2.4 %collective-permute-start = (bf16[8,2,192,128]{3,2,1,0:T(8,128)(2,1)S(1)}, bf16[8,2,192,128]{3,2,1,0:T(8,128)(2,1)S(1)}, u32[]{:S(2)}, u32[]{:S(2)}) collective-permute-start(bf16[8,2,192,128]{3,2,1,0:T(8,128)(2,1)S(1)} %slice.3), channel_id=1, source_target_pairs={{0,8},{8,0},{1,9},{9,1},{2,10},{10,2},{3,11},{11,3},{4,12},{12,4},... | collective-permute-start | bytes 2359304 | tf_op jit(solution)/shard_map/ppermute | solution.py:445
  31.1 17.5 %slice-start = ((s8[8388608]{0:T(1024)(128)(4,1)}), s8[4194304]{0:T(1024)(128)(4,1)S(1)}, s32[]{:S(2)}) async-start(s8[8388608]{0:T(1024)(128)(4,1)} %bitcast.9), calls=%async_computation.4 | async-start | bytes 8388608
  31.1 17.5 %slice-start.2 = ((s8[8388608]{0:T(1024)(128)(4,1)}), s8[4194304]{0:T(1024)(128)(4,1)S(1)}, s32[]{:S(2)}) async-start(s8[8388608]{0:T(1024)(128)(4,1)} %bitcast.11), calls=%async_computation.6 | async-start | bytes 8388608
  31.1 17.5 %slice-start.4 = ((s8[8388608]{0:T(1024)(128)(4,1)}), s8[4194304]{0:T(1024)(128)(4,1)S(1)}, s32[]{:S(2)}) async-start(s8[8388608]{0:T(1024)(128)(4,1)} %bitcast.13), calls=%async_computation.8 | async-start | bytes 8388608
  31.2 17.5 %slice-start.6 = ((s8[8388608]{0:T(1024)(128)(4,1)}), s8[4194304]{0:T(1024)(128)(4,1)S(1)}, s32[]{:S(2)}) async-start(s8[8388608]{0:T(1024)(128)(4,1)} %bitcast.15), calls=%async_computation.10 | async-start | bytes 8388608
  31.2 17.5 %slice-start.1 = ((s8[8388608]{0:T(1024)(128)(4,1)}), s8[4194304]{0:T(1024)(128)(4,1)S(1)}, s32[]{:S(2)}) async-start(s8[8388608]{0:T(1024)(128)(4,1)} %bitcast.9), calls=%async_computation.5 | async-start | bytes 8388608
  31.2 17.5 %slice-start.3 = ((s8[8388608]{0:T(1024)(128)(4,1)}), s8[4194304]{0:T(1024)(128)(4,1)S(1)}, s32[]{:S(2)}) async-start(s8[8388608]{0:T(1024)(128)(4,1)} %bitcast.11), calls=%async_computation.7 | async-start | bytes 8388608
  31.2 17.5 %slice-start.5 = ((s8[8388608]{0:T(1024)(128)(4,1)}), s8[4194304]{0:T(1024)(128)(4,1)S(1)}, s32[]{:S(2)}) async-start(s8[8388608]{0:T(1024)(128)(4,1)} %bitcast.13), calls=%async_computation.9 | async-start | bytes 8388608
  31.2 17.5 %slice-start.7 = ((s8[8388608]{0:T(1024)(128)(4,1)}), s8[4194304]{0:T(1024)(128)(4,1)S(1)}, s32[]{:S(2)}) async-start(s8[8388608]{0:T(1024)(128)(4,1)} %bitcast.15), calls=%async_computation.11 | async-start | bytes 8388608
  31.2 17.5 %copy-start = (bf16[256,1024]{1,0:T(8,128)(2,1)S(1)}, bf16[256,1024]{1,0:T(8,128)(2,1)}, u32[]{:S(2)}) copy-start(bf16[256,1024]{1,0:T(8,128)(2,1)} %embed_ref.1) | copy-start | bytes 1572868
  31.2 17.5 %copy-start.1 = (bf16[1024,256]{1,0:T(8,128)(2,1)S(1)}, bf16[1024,256]{1,0:T(8,128)(2,1)}, u32[]{:S(2)}) copy-start(bf16[1024,256]{1,0:T(8,128)(2,1)} %vocab_ref.1) | copy-start | bytes 1572868
  31.2 17.5 %copy-start.2 = (s32[192,8]{0,1:T(8,128)S(1)}, s32[192,8]{0,1:T(8,128)}, u32[]{:S(2)}) copy-start(s32[192,8]{0,1:T(8,128)} %param.10) | copy-start | bytes 18436
  31.2 17.5 %copy-start.3 = (f32[1024]{0:T(1024)S(1)}, f32[1024]{0:T(1024)}, u32[]{:S(2)}) copy-start(f32[1024]{0:T(1024)} %param.16) | copy-start | bytes 12292
  31.3 17.4 %copy-start.4 = (s32[192]{0:T(256)S(1)}, s32[192]{0:T(256)}, u32[]{:S(2)}) copy-start(s32[192]{0:T(256)} %param.11) | copy-start | bytes 2308
  74.7 3.3 %collective-permute-start.1 = (bf16[8,2,192,128]{3,2,1,0:T(8,128)(2,1)S(1)}, bf16[8,2,192,128]{3,2,1,0:T(8,128)(2,1)S(1)}, u32[]{:S(2)}, u32[]{:S(2)}) collective-permute-start(bf16[8,2,192,128]{3,2,1,0:T(8,128)(2,1)S(1)} %get-tuple-element.50), channel_id=1, source_target_pairs={{0,8},{8,0},{1,9},{9,1},{2,10},{10,2},{3,11},{11,3},{4,12},{12,4},... | collective-permute-start | bytes 2359304 | tf_op jit(solution)/shard_map/ppermute | solution.py:445
  79.2 23.1 %all-to-all-start.3 = ((bf16[8,3,192,128]{3,2,1,0:T(8,128)(2,1)}), bf16[8,3,192,128]{3,2,1,0:T(8,128)(2,1)S(1)}, u32[]{:S(2)}, u32[]{:S(2)}) async-start(bf16[8,3,192,128]{3,2,1,0:T(8,128)(2,1)} %join.1), calls=%async_computation.3 | async-start | bytes 2359296 | tf_op jit(solution)/shard_map/all_to_all | solution.py:437
  82.8 3.7 %collective-permute-start.2 = (f32[8,192]{1,0:T(8,128)S(1)}, f32[8,192]{1,0:T(8,128)S(1)}, u32[]{:S(2)}, u32[]{:S(2)}) collective-permute-start(f32[8,192]{1,0:T(8,128)S(1)} %get-tuple-element.53), channel_id=1, source_target_pairs={{0,2},{1,3},{2,0},{3,1},{4,6},{5,7},{6,4},{7,5},{8,10},{9,11},{10,... | collective-permute-start | bytes 18440 | tf_op jit(solution)/shard_map/ppermute | solution.py:441
  86.5 5.5 %collective-permute-start.3 = (f32[8,192]{1,0:T(8,128)S(1)}, f32[8,192]{1,0:T(8,128)S(1)}, u32[]{:S(2)}, u32[]{:S(2)}) collective-permute-start(f32[8,192]{1,0:T(8,128)S(1)} %add.17), channel_id=1, source_target_pairs={{0,4},{1,5},{2,6},{3,7},{4,0},{5,1},{6,2},{7,3},{8,12},{9,13},{10,... | collective-permute-start | bytes 18440 | tf_op jit(solution)/shard_map/ppermute | solution.py:441
  92.0 5.7 %collective-permute-start.4 = (f32[8,192]{1,0:T(8,128)S(1)}, f32[8,192]{1,0:T(8,128)S(1)}, u32[]{:S(2)}, u32[]{:S(2)}) collective-permute-start(f32[8,192]{1,0:T(8,128)S(1)} %add.18), channel_id=1, source_target_pairs={{0,1},{1,0},{2,3},{3,2},{4,5},{5,4},{6,7},{7,6},{8,9},{9,8},{10,11... | collective-permute-start | bytes 18440 | tf_op jit(solution)/shard_map/ppermute | solution.py:441
